TPU v7x, 256 devices: a whole 4x4x8 slice. The times are simulated.
256 devices in a mesh: group: 8 (over z_lo, y), ctx: 32 (over x, z_hi, core).
Axes of the slice: x: 4, y: 4, z: 8 (z_hi: 4, z_lo: 2; z = z_hi * 2 + z_lo), core: 2. Of those that a mesh axis runs over, the one named last changes fastest.
Arguments:
- hidden_x: bfloat16 [8, 8192, 8192], P('group', 'ctx'), may hold values from -6 to 6
- gate_z: bfloat16 [8, 8192, 8192], P('group', 'ctx'), may hold values from -6 to 6
- lengths: int32 [8, 32], P('group', 'ctx'), may hold values from 128 to 256, as said below
- conv_weight: float32 [4, 8192], P(None, ('group', 'ctx')), may hold values from -3 to 3
- conv_bias: float32 [8192], P(('group', 'ctx')), may hold values from -3 to 3
- xproj_weight: bfloat16 [8192, 288], P(('group', 'ctx')), may hold values from -0.0625 to 0.0625
- dtproj_weight: bfloat16 [256, 8192], P(None, ('group', 'ctx')), may hold values from -0.375 to 0.375
- dt_bias: float32 [8192], P(('group', 'ctx')), may hold values from -4.6 to -2.25
- a_log: float32 [16, 8192], P(None, ('group', 'ctx')), may hold values from -8.5 to -0.7
- skip_gain: float32 [8192], P(('group', 'ctx')), may hold values from 0.5 to 2
Outputs:
- gated: bfloat16 [8, 8192, 8192], P('group', 'ctx')
Inputs may be any that keep to these rules, and one draw needn't show every extreme that they name: Block c of record r holds lengths[r, c] valid positions at its start and padding after them.
All inputs are finite; a program needn't handle non-finite values.
Results may differ from a plain program's by a relative error of at most 0.0015.
The roundings to bfloat16 on the way count: a program that leaves them out, or rounds other values in their place, can miss the bound.
Values may be sent and summed in bfloat16 or wider, within the bound.
No kernel may reach another device: no remote copies, remote signals or barrier semaphores. Data moves between devices by JAX's collectives and lax.ppermute only.
A program may use at most 192 MiB of HBM per device.

v0:
```python
import jax
import jax.numpy as jnp
from jax import lax
from jax.sharding import PartitionSpec as P


def shifted(block, axis, distance):
    devices = range(lax.axis_size(axis))
    route = [(i - distance, i) for i in devices if i - distance in devices]
    return lax.ppermute(block, axis, route)


def run_scan(state, x_act, step_size, b_rows, c_rows, a_matrix):
    tok_rows, width = x_act.shape
    blocks = tok_rows // 16

    def advance(state, block):
        x_block, d_block, b_block, c_block = block
        outputs = []
        for offset in range(16):
            state = (
                jnp.exp(a_matrix * d_block[offset][None, :]) * state
                + (d_block[offset] * x_block[offset])[None, :] * b_block[offset][:, None]
            )
            outputs.append(jnp.sum(c_block[offset][:, None] * state, axis=0))
        return (state, jnp.stack(outputs))

    ending, y_blocks = lax.scan(
        advance,
        state,
        (
            x_act.reshape(blocks, 16, width),
            step_size.reshape(blocks, 16, width),
            b_rows.reshape(blocks, 16, -1),
            c_rows.reshape(blocks, 16, -1),
        ),
    )
    return (y_blocks.reshape(tok_rows, width), ending)


def shards(
    hidden_x,
    gate_z,
    lengths,
    conv_weight,
    conv_bias,
    xproj_weight,
    dtproj_weight,
    dt_bias,
    a_log,
    skip_gain,
):
    tok_rows = hidden_x.shape[1]
    taps = conv_weight.shape[0]
    valid_row = (lax.iota(jnp.int32, tok_rows) < lengths[0, 0]).astype(jnp.float32)
    valid = valid_row[:, None]
    conv_full, bias_full, dtb_full, alog_full, skip_full = (
        lax.all_gather(conv_weight, ("group", "ctx"), axis=1, tiled=True),
        lax.all_gather(conv_bias, ("group", "ctx"), axis=0, tiled=True),
        lax.all_gather(dt_bias, ("group", "ctx"), axis=0, tiled=True),
        lax.all_gather(a_log, ("group", "ctx"), axis=1, tiled=True),
        lax.all_gather(skip_gain, ("group", "ctx"), axis=0, tiled=True),
    )
    masked_half = hidden_x[0] * valid_row.astype(jnp.bfloat16)[:, None]
    rim_rows = shifted(masked_half[tok_rows - (taps - 1) :], "ctx", 1)
    padded = jnp.concatenate(
        [rim_rows.astype(jnp.float32), masked_half.astype(jnp.float32)], axis=0
    )
    total = bias_full[None, :] + conv_full[0][None, :] * padded[0:tok_rows]
    for offset in range(1, taps):
        total = total + conv_full[offset][None, :] * padded[offset : offset + tok_rows]
    conv_act = jax.nn.silu(total).astype(jnp.bfloat16)
    rank = dtproj_weight.shape[0]
    states = alog_full.shape[0]
    proj = jnp.dot(
        conv_act,
        lax.all_gather(xproj_weight, ("group", "ctx"), axis=0, tiled=True),
        preferred_element_type=jnp.float32,
    )
    dt_low = proj[:, :rank].astype(jnp.bfloat16)
    b_rows = proj[:, rank : rank + states]
    c_rows = proj[:, rank + states :]
    step_size = (
        jax.nn.softplus(
            jnp.dot(
                dt_low,
                lax.all_gather(dtproj_weight, ("group", "ctx"), axis=1, tiled=True),
                preferred_element_type=jnp.float32,
            )
            + dtb_full[None, :]
        )
        * valid
    )
    a_matrix = -jnp.exp(alog_full)
    x_act = conv_act.astype(jnp.float32)
    zero_state = jnp.zeros(a_matrix.shape, jnp.float32)
    y_local, local_end = run_scan(zero_state, x_act, step_size, b_rows, c_rows, a_matrix)
    total_decay = jnp.exp(a_matrix * jnp.sum(step_size, axis=0)[None, :])

    def relay(turn, incoming):
        return shifted(total_decay * incoming + local_end, "ctx", 1)

    incoming = lax.fori_loop(0, lax.axis_size("ctx") - 1, relay, zero_state)
    y_all, ending = run_scan(incoming, x_act, step_size, b_rows, c_rows, a_matrix)
    mixed = (
        (y_all + skip_full[None, :] * x_act) * jax.nn.silu(gate_z[0].astype(jnp.float32)) * valid
    )
    return mixed.astype(jnp.bfloat16)[None]


def solution(mesh):
    in_specs = (
        P("group", "ctx", None),
        P("group", "ctx", None),
        P("group", "ctx"),
        P(None, ("group", "ctx")),
        P(("group", "ctx")),
        P(("group", "ctx"), None),
        P(None, ("group", "ctx")),
        P(("group", "ctx")),
        P(None, ("group", "ctx")),
        P(("group", "ctx")),
    )
    out_specs = P("group", "ctx", None)
    return jax.shard_map(shards, mesh=mesh, in_specs=in_specs, out_specs=out_specs, check_vma=False)
```

profile of v0, /device:TPU:18, one launch (start us, length us, event | category | flops | bytes accessed | tf_op | source)
XLA Modules:
  0.0 1949.0 jit_solution(5807592894544555180)
XLA Ops:
  11.9 6.3 fusion.89
  20.2 331.3 %all-gather.1 = f32[256,32,4]{1,2,0:T(4,128)S(1)} all-gather(f32[1,32,4]{1,2,0:T(4,128)S(1)} %bitcast.520), channel_id=1, replica_groups=mesh['group'=8,'ctx'=32] {'group','ctx'}, dimensions={0}, use_global_device_ids=true | all-gather | bytes 131584 | tf_op jit(solution)/shard_map/all_gather | solution.py:58
  351.8 403.9 %all-gather = f32[256,32,16]{1,2,0:T(8,128)S(1)} all-gather(f32[1,32,16]{1,2,0:T(8,128)S(1)} %bitcast.519), channel_id=1, replica_groups=mesh['group'=8,'ctx'=32] {'group','ctx'}, dimensions={0}, use_global_device_ids=true | all-gather | bytes 526336 | tf_op jit(solution)/shard_map/all_gather | solution.py:61
  761.7 13.6 multiply_convert_fusion
  781.6 6.3 fusion.93
  788.2 299.0 %all-gather.7.cloned.1.call-done = bf16[256,8192]{0,1:T(8,128)(2,1)} async-done(((bf16[256,32]{0,1:T(8,128)(2,1)}), bf16[256,8192]{0,1:T(8,128)(2,1)}) %all-gather.7.cloned.1.call-update) | async-done | bytes 4194320 | tf_op jit(solution)/shard_map/all_gather | solution.py:87
  1087.2 10.6 fusion.92
  1097.8 118.0 %while.35 = (s32[]{:T(128)}, f32[16,8192]{1,0:T(8,128)S(1)}, f32[16,16,8192]{2,1,0:T(8,128)}, f32[16,8192]{1,0:T(8,128)S(1)}, f32[16,16,8192]{2,1,0:T(8,128)}, /...) while((s32[]{:T(128)}, f32[16,8192]{1,0:T(8,128)S(1)}, ...), condition=%wide.region_2.3_spmd.clone, body=%wide.region_1.2_spmd.clone.sunk | while | flops 8650770 | bytes 6295059 | solution.py:28
  1193.3 5.4 constant_dynamic-slice_fusion.115
  1215.9 514.3 %while.33 = (s32[]{:T(128)}, f32[16,8192]{1,0:T(8,128)S(1)}, f32[16,8192]{1,0:T(8,128)S(1)}, f32[16,8192]{1,0:T(8,128)S(1)}, s32[]{:T(128)}) while((s32[]{:T(128)}, f32[16,8192]{1,0:T(8,128)S(1)}, f32[16,8192]{1,0:T(8,128)S(1)}, f32[16,8192]{1,0:T(8,128)S(1)}, s32[]{:T(128)}) %tuple.251), condition=%wide.region_4.5_spmd, body=%wide.region_3.4_spmd.sunk | while | flops 262146 | bytes 4194405 | solution.py:103
  1217.9 16.6 collective-permute-done
  1236.6 13.6 collective-permute-done
  1252.2 14.8 collective-permute-done
  1268.9 15.6 collective-permute-done
  1286.6 12.7 collective-permute-done
  1301.3 14.5 collective-permute-done
  1317.8 14.5 collective-permute-done
  1334.4 14.7 collective-permute-done
  1351.0 14.5 collective-permute-done
  1367.6 14.5 collective-permute-done
  1384.1 14.7 collective-permute-done
  1400.8 14.5 collective-permute-done
  1417.3 14.5 collective-permute-done
  1433.8 14.7 collective-permute-done
  1450.5 14.5 collective-permute-done
  1467.1 14.5 collective-permute-done
  1483.6 14.7 collective-permute-done
  1500.3 14.5 collective-permute-done
  1516.8 14.5 collective-permute-done
  1533.3 14.7 collective-permute-done
  1550.0 14.5 collective-permute-done
  1566.6 14.5 collective-permute-done
  1583.1 14.7 collective-permute-done
  1599.8 14.5 collective-permute-done
  1616.3 14.5 collective-permute-done
  1632.8 14.7 collective-permute-done
  1649.5 14.5 collective-permute-done
  1666.0 14.5 collective-permute-done
  1682.6 14.7 collective-permute-done
  1699.3 14.5 collective-permute-done
  1715.8 14.4 collective-permute-done
  1730.2 203.4 %while.34 = (s32[]{:T(128)}, f32[16,8192]{1,0:T(8,128)S(1)}, f32[16,16,8192]{2,1,0:T(8,128)}, f32[16,16,8192]{2,1,0:T(8,128)}, f32[16,8192]{1,0:T(8,128)S(1)}, /...) while((s32[]{:T(128)}, f32[16,8192]{1,0:T(8,128)S(1)}, ...), condition=%wide.region_22.23_spmd, body=%wide.region_5.22_spmd.sunk | while | flops 18874384 | bytes 15473949 | solution.py:28
  1856.7 5.4 constant_dynamic-slice_fusion.114
  1869.6 5.4 constant_dynamic-slice_fusion.114
  1895.0 5.5 constant_dynamic-slice_fusion.114
  1908.0 5.4 constant_dynamic-slice_fusion.114
  1920.8 5.4 constant_dynamic-slice_fusion.114
  1933.6 8.8 fusion.87
  (811 shorter events, 364.9 us)
Async XLA Ops:
  6.5 755.2 %all-reduce.6.cloned.1.call-start = ((), (), s32[]{:S(2)}) async-start(), calls=%async_computation.2 | async-start | bytes 196608
  7.4 1.7 copy-start.2
  8.2 0.9 copy-start.3
  9.1 0.6 copy-start.1
  9.7 771.9 %all-gather.5.cloned.1.call-start = ((), (), s32[]{:S(2)}) async-start(), calls=%async_computation | async-start | bytes 6316032 | tf_op jit(solution)/shard_map/all_gather | solution.py:77
  10.5 1076.7 %all-gather.7.cloned.1.call-start = ((), (), s32[]{:S(2)}) async-start(), calls=%async_computation.1 | async-start | bytes 4210688 | tf_op jit(solution)/shard_map/all_gather | solution.py:87
  11.9 8.3 copy-start.6
  11.9 339.9 %copy-start.5 = (f32[16,32]{1,0:T(8,128)S(1)}, f32[16,32]{1,0:T(8,128)}, u32[]{:S(2)}) copy-start(f32[16,32]{1,0:T(8,128)} %param.24) | copy-start | bytes 6148
  18.2 743.4 %collective-permute-start.1 = (bf16[3,8192]{1,0:T(4,128)(2,1)S(1)}, bf16[3,8192]{1,0:T(4,128)(2,1)S(1)}, u32[]{:S(2)}, u32[]{:S(2)}) collective-permute-start(bf16[3,8192]{1,0:T(4,128)(2,1)S(1)} %slice.574), channel_id=1, source_target_pairs={{0,1},{1,2},{2,3},{3,4},{4,5},{5,6},{6,7},{7,8},{8,9},{9,10},{10,1... | collective-permute-start | bytes 147464 | tf_op jit(solution)/shard_map/ppermute | solution.py:10
  775.4 2.0 copy-start
  781.6 305.6 %copy-start.7 = (f32[8192]{0:T(1024)S(1)}, f32[8192]{0:T(1024)}, u32[]{:S(2)}) copy-start(f32[8192]{0:T(1024)} %get-tuple-element.232) | copy-start | bytes 98308
  1216.0 18.6 collective-permute-start
  1234.6 15.5 collective-permute-start
  1250.2 16.7 collective-permute-start
  1267.0 17.6 collective-permute-start
  1284.6 14.6 collective-permute-start
  1299.3 16.5 collective-permute-start
  1315.9 16.5 collective-permute-start
  1332.4 16.6 collective-permute-start
  1349.1 16.5 collective-permute-start
  1365.6 16.5 collective-permute-start
  1382.2 16.6 collective-permute-start
  1398.8 16.5 collective-permute-start
  1415.4 16.5 collective-permute-start
  1431.9 16.6 collective-permute-start
  1448.6 16.5 collective-permute-start
  1465.1 16.5 collective-permute-start
  1481.7 16.6 collective-permute-start
  1498.3 16.5 collective-permute-start
  1514.9 16.5 collective-permute-start
  1531.4 16.6 collective-permute-start
  1548.1 16.5 collective-permute-start
  1564.6 16.5 collective-permute-start
  1581.2 16.6 collective-permute-start
  1597.8 16.5 collective-permute-start
  1614.4 16.5 collective-permute-start
  1630.9 16.6 collective-permute-start
  1647.6 16.5 collective-permute-start
  1664.1 16.5 collective-permute-start
  1680.7 16.6 collective-permute-start
  1697.3 16.5 collective-permute-start
  1713.9 16.4 collective-permute-start
  1730.2 203.4 %copy-start.4 = (f32[8192]{0:T(1024)S(1)}, f32[8192]{0:T(1024)}, u32[]{:S(2)}) copy-start(f32[8192]{0:T(1024)} %get-tuple-element.234) | copy-start | bytes 98308
Sparse Core Ops, SparseCore 0:
  13.4 244.1 all-reduce.5
  259.4 414.3 all-gather.4
  675.7 411.3 all-gather.6
where the time goes:
time: 1950 us
  waiting for transfers between devices  752 us (39%)
  blocking collectives  735 us (38%)
  local copies, waits for them, and re-layouts  206 us (11%)
  other arithmetic  157 us (8%)
  starting transfers between devices  61.5 us (3%)
    ppermute x32, waiting for transfers between devices, shifted(): return lax.ppermute(block, axis, route)  452 us
    all_gather x1, blocking collectives, shards(): lax.all_gather(a_log, ('group', 'ctx'), axis=1, tiled=True)  404 us
    all_gather x1, blocking collectives, shards(): lax.all_gather(conv_weight, ('group', 'ctx'), axis=1, tiled=True)  331 us
    all_gather x1, waiting for transfers between devices, shards(): lax.all_gather(dtproj_weight, ('group', 'ctx'), axis=1, tiled=True)  299 us
    slice x32, local copies, waits for them, and re-layouts, advance(): x_block[offset]  167 us
    reduce_sum x80, other arithmetic, advance(): outputs.append(jnp.sum(c_block[offset][:, None] * state, axis=0))  88.3 us
    ppermute x32, starting transfers between devices, shifted(): return lax.ppermute(block, axis, route)  61.5 us
  transfers between devices with their start and end apart: 35, of which 32 were waited for; matrix products, arithmetic and copies ran while one was open for 2% of the time, Pallas kernels for 0%

commit v1 on v0

v1 whole, which is shorter than its diff:
```python
import jax
import jax.numpy as jnp
from jax import lax
from jax.experimental import pallas as pl
from jax.experimental.pallas import tpu as pltpu
from jax.sharding import PartitionSpec as P

LOG2E = 1.4426950408889634
LANES = 128
ROWS = 8
WIDE = ROWS * LANES


def sigmoid(v):
    return 1.0 / (1.0 + jnp.exp(-v))


def settings():
    return pltpu.CompilerParams(dimension_semantics=("arbitrary",), vmem_limit_bytes=56 << 20)


def whole(shape):
    return pl.BlockSpec(shape, lambda i, *_: (0,) * len(shape))


def per_step(count):
    return pl.BlockSpec((count, ROWS, LANES), lambda i, *_: (0, i, 0))


def conv_kernel(len_ref, x_ref, rim_ref, par_ref, xw_ref, act_ref, proj_ref, pad_ref):
    tok, width = x_ref.shape
    keep = lax.broadcasted_iota(jnp.int32, (tok, LANES), 0) < len_ref[0]
    for g in range(width // LANES):
        cols = slice(g * LANES, (g + 1) * LANES)
        pad_ref[0:8, :] = rim_ref[:, cols].astype(jnp.float32)
        pad_ref[8 : 8 + tok, :] = jnp.where(keep, x_ref[:, cols].astype(jnp.float32), 0.0)
        total = par_ref[4, g : g + 1, :] + par_ref[0, g : g + 1, :] * pad_ref[5 : 5 + tok, :]
        for k in range(1, 4):
            total = total + par_ref[k, g : g + 1, :] * pad_ref[5 + k : 5 + k + tok, :]
        act_ref[:, cols] = (total * sigmoid(total)).astype(jnp.bfloat16)
    weight = xw_ref[...].reshape(width, xw_ref.shape[-1])
    part = jnp.dot(act_ref[...], weight, preferred_element_type=jnp.float32)

    @pl.when(pl.program_id(0) == 0)
    def _():
        proj_ref[...] = part

    @pl.when(pl.program_id(0) > 0)
    def _():
        proj_ref[...] += part


def conv_proj(length, x, rim, pars, xw):
    tok, chans = x.shape
    pieces, _, rows, cols = xw.shape
    return pl.pallas_call(
        conv_kernel,
        grid_spec=pltpu.PrefetchScalarGridSpec(
            num_scalar_prefetch=1,
            grid=(chans // WIDE,),
            in_specs=[
                pl.BlockSpec((tok, WIDE), lambda i, *_: (0, i)),
                pl.BlockSpec((8, WIDE), lambda i, *_: (0, i)),
                per_step(pars.shape[0]),
                pl.BlockSpec((pieces, 1, rows, cols), lambda i, *_: (0, i, 0, 0)),
            ],
            out_specs=[pl.BlockSpec((tok, WIDE), lambda i, *_: (0, i)), whole((tok, cols))],
            scratch_shapes=[pltpu.VMEM((tok + 8, LANES), jnp.float32)],
        ),
        out_shape=[
            jax.ShapeDtypeStruct((tok, chans), jnp.bfloat16),
            jax.ShapeDtypeStruct((tok, cols), jnp.float32),
        ],
        compiler_params=settings(),
        name="conv_proj",
    )(length, x, rim, pars, xw)


def scan_kernel(
    len_ref, low_ref, dw_ref, par_ref, alog_ref, act_ref, b_ref, c_ref,
    y_ref, cum_ref, end_ref, d_scr, x_scr, a_scr,
):
    tok, rank = low_ref.shape
    states = alog_ref.shape[0]
    keep = lax.broadcasted_iota(jnp.int32, (tok, LANES), 0) < len_ref[0]
    raw = lax.dot_general(
        low_ref[...],
        dw_ref[...].reshape(WIDE, rank),
        (((1,), (1,)), ((), ())),
        preferred_element_type=jnp.float32,
    )
    for g in range(ROWS):
        cols = slice(g * LANES, (g + 1) * LANES)
        v = raw[:, cols] + par_ref[5, g : g + 1, :]
        soft = jnp.maximum(v, 0.0) + jnp.log1p(jnp.exp(-jnp.abs(v)))
        d = jnp.where(keep, soft, 0.0)
        place = slice(g * 8, (g + 1) * 8)
        d_scr[:, place, :] = d.reshape(tok // 8, 8, LANES)
        x_scr[:, place, :] = (d * act_ref[:, cols].astype(jnp.float32)).reshape(tok // 8, 8, LANES)
    a_scr[...] = jnp.exp(alog_ref[...]) * (-LOG2E)

    def block(i, carry):
        hs, cum = carry
        hs = list(hs)
        for o in range(16):
            t = i * 16 + o
            tile = i * 2 + o // 8
            d = d_scr[tile, pl.ds(o % 8, ROWS, stride=8), :]
            dx = x_scr[tile, pl.ds(o % 8, ROWS, stride=8), :]
            cum = cum + d
            acc = [None] * 4
            for n in range(states):
                b = b_ref[pl.ds(t * states + n, ROWS, stride=0), :]
                c = c_ref[pl.ds(t * states + n, ROWS, stride=0), :]
                hs[n] = jnp.exp2(a_scr[n] * d) * hs[n] + dx * b
                term = c * hs[n]
                acc[n % 4] = term if acc[n % 4] is None else acc[n % 4] + term
            y_ref[t] = (acc[0] + acc[1]) + (acc[2] + acc[3])
            cum_ref[t] = cum
        return tuple(hs), cum

    zero = jnp.zeros((ROWS, LANES), jnp.float32)
    hs, cum = lax.fori_loop(0, tok // 16, block, ((zero,) * states, zero))
    for q in range(ROWS // 2):
        pair = slice(2 * q, 2 * q + 2)
        for n in range(states):
            end_ref[q, 2 * n : 2 * n + 2, :] = hs[n][pair]
        for k in range(4):
            at = 2 * states + 2 * k
            end_ref[q, at : at + 2, :] = cum[pair]


def scan_pass(length, low, dw, pars, alog, act, b_wide, c_wide):
    tok, chans = act.shape
    pieces, _, rows, rank = dw.shape
    states = alog.shape[0]
    groups = chans // LANES
    sent = 2 * states + 8
    return pl.pallas_call(
        scan_kernel,
        grid_spec=pltpu.PrefetchScalarGridSpec(
            num_scalar_prefetch=1,
            grid=(chans // WIDE,),
            in_specs=[
                whole((tok, rank)),
                pl.BlockSpec((pieces, 1, rows, rank), lambda i, *_: (0, i, 0, 0)),
                per_step(pars.shape[0]),
                per_step(states),
                pl.BlockSpec((tok, WIDE), lambda i, *_: (0, i)),
                whole((tok * states, LANES)),
                whole((tok * states, LANES)),
            ],
            out_specs=[
                per_step(tok),
                per_step(tok),
                pl.BlockSpec((ROWS // 2, sent, LANES), lambda i, *_: (i, 0, 0)),
            ],
            scratch_shapes=[
                pltpu.VMEM((tok // 8, 8 * ROWS, LANES), jnp.float32),
                pltpu.VMEM((tok // 8, 8 * ROWS, LANES), jnp.float32),
                pltpu.VMEM((states, ROWS, LANES), jnp.float32),
            ],
        ),
        out_shape=[
            jax.ShapeDtypeStruct((tok, groups, LANES), jnp.float32),
            jax.ShapeDtypeStruct((tok, groups, LANES), jnp.float32),
            jax.ShapeDtypeStruct((groups // 2, sent, LANES), jnp.float32),
        ],
        compiler_params=settings(),
        name="scan_pass",
    )(length, low, dw, pars, alog, act, b_wide, c_wide)


def prefix_kernel(end_ref, alog_ref, in_ref):
    blocks = end_ref.shape[0]
    rows = alog_ref.shape[0]
    a = [jnp.exp(alog_ref[r : r + 8, :]) * (-LOG2E) for r in range(0, rows, 8)]
    hs = [jnp.zeros((8, LANES), jnp.float32) for _ in a]
    for k in range(blocks):
        spent = end_ref[k, rows : rows + 8, :]
        for j in range(len(a)):
            in_ref[k, 8 * j : 8 * j + 8, :] = hs[j]
            hs[j] = jnp.exp2(a[j] * spent) * hs[j] + end_ref[k, 8 * j : 8 * j + 8, :]


def prefix(ends, alog):
    return pl.pallas_call(
        prefix_kernel,
        out_shape=jax.ShapeDtypeStruct((ends.shape[0], *alog.shape), jnp.float32),
        name="prefix",
    )(ends, alog)


def gate_kernel(
    len_ref, y_ref, cum_ref, hin_ref, par_ref, alog_ref, act_ref, z_ref, c_ref,
    out_ref, y_scr, a_scr, h_scr,
):
    tok = act_ref.shape[0]
    states = alog_ref.shape[0]
    a_scr[...] = jnp.exp(alog_ref[...]) * (-LOG2E)
    for q in range(ROWS // 2):
        for n in range(states):
            h_scr[n, 2 * q : 2 * q + 2, :] = hin_ref[q, 2 * n : 2 * n + 2, :]

    def block(i, carry):
        for o in range(8):
            t = i * 8 + o
            cum = cum_ref[t]
            acc = [y_ref[t]] + [None] * 3
            for n in range(states):
                c = c_ref[pl.ds(t * states + n, ROWS, stride=0), :]
                term = (c * h_scr[n]) * jnp.exp2(a_scr[n] * cum)
                acc[n % 4] = term if acc[n % 4] is None else acc[n % 4] + term
            y_scr[i, pl.ds(o, ROWS, stride=8), :] = (acc[0] + acc[1]) + (acc[2] + acc[3])
        return carry

    lax.fori_loop(0, tok // 8, block, 0)
    keep = lax.broadcasted_iota(jnp.int32, (tok, LANES), 0) < len_ref[0]
    for g in range(ROWS):
        cols = slice(g * LANES, (g + 1) * LANES)
        y = y_scr[:, g * 8 : (g + 1) * 8, :].reshape(tok, LANES)
        z = z_ref[:, cols].astype(jnp.float32)
        out = (y + par_ref[6, g : g + 1, :] * act_ref[:, cols].astype(jnp.float32)) * (z * sigmoid(z))
        out_ref[:, cols] = jnp.where(keep, out, 0.0).astype(jnp.bfloat16)


def gate_pass(length, y, cum, hin, pars, alog, act, z, c_wide):
    tok, chans = act.shape
    states = alog.shape[0]
    return pl.pallas_call(
        gate_kernel,
        grid_spec=pltpu.PrefetchScalarGridSpec(
            num_scalar_prefetch=1,
            grid=(chans // WIDE,),
            in_specs=[
                per_step(tok),
                per_step(tok),
                pl.BlockSpec((ROWS // 2, 2 * states, LANES), lambda i, *_: (i, 0, 0)),
                per_step(pars.shape[0]),
                per_step(states),
                pl.BlockSpec((tok, WIDE), lambda i, *_: (0, i)),
                pl.BlockSpec((tok, WIDE), lambda i, *_: (0, i)),
                whole((tok * states, LANES)),
            ],
            out_specs=pl.BlockSpec((tok, WIDE), lambda i, *_: (0, i)),
            scratch_shapes=[
                pltpu.VMEM((tok // 8, 8 * ROWS, LANES), jnp.float32),
                pltpu.VMEM((states, ROWS, LANES), jnp.float32),
                pltpu.VMEM((states, ROWS, LANES), jnp.float32),
            ],
        ),
        out_shape=jax.ShapeDtypeStruct((tok, chans), jnp.bfloat16),
        compiler_params=settings(),
        name="gate_pass",
    )(length, y, cum, hin, pars, alog, act, z, c_wide)


def everywhere(shard):
    return lax.all_gather(lax.all_gather(shard, "group"), "ctx")


def shards(
    hidden_x, gate_z, lengths, conv_weight, conv_bias, xproj_weight, dtproj_weight, dt_bias, a_log, skip_gain
):
    x, z = hidden_x[0], gate_z[0]
    tok, chans = x.shape
    taps = conv_weight.shape[0]
    rank = dtproj_weight.shape[0]
    states = a_log.shape[0]
    blocks = lax.axis_size("ctx")
    length = lengths[0]

    small = jnp.concatenate(
        [conv_weight, conv_bias[None], dt_bias[None], skip_gain[None], a_log], axis=0
    )
    small = everywhere(small)
    small = small.reshape(8, 4, *small.shape[1:]).transpose(3, 2, 0, 1, 4)
    small = small.reshape(small.shape[0], chans // LANES, LANES)
    pars, alog = small[: taps + 3], small[taps + 3 :]
    xw = everywhere(xproj_weight)
    dw = everywhere(dtproj_weight.T)

    edge = jnp.arange(tok - (taps - 1), tok, dtype=jnp.int32)[:, None] < length
    edge = jnp.where(edge, x[tok - (taps - 1) :], jnp.bfloat16(0))
    rim = lax.ppermute(edge, "ctx", [(i, i + 1) for i in range(blocks - 1)])
    rim = jnp.concatenate([jnp.zeros((8 - (taps - 1), chans), x.dtype), rim], axis=0)

    act, proj = conv_proj(length, x, rim, pars, xw)
    low = proj[:, :rank].astype(jnp.bfloat16)
    b_wide = jnp.broadcast_to(proj[:, rank : rank + states].reshape(-1, 1), (tok * states, LANES))
    c_wide = jnp.broadcast_to(proj[:, rank + states :].reshape(-1, 1), (tok * states, LANES))
    y, cum, ends = scan_pass(length, low, dw, pars, alog, act, b_wide, c_wide)

    own = 2 * lax.axis_index("ctx")
    mine = lax.dynamic_slice_in_dim(alog, own, 2, axis=1).reshape(2 * states, LANES)
    ends = lax.all_to_all(ends, "ctx", split_axis=0, concat_axis=0, tiled=True)
    hin = prefix(ends, mine)
    hin = lax.all_to_all(hin, "ctx", split_axis=0, concat_axis=0, tiled=True)
    out = gate_pass(length, y, cum, hin, pars, alog, act, z, c_wide)
    return out[None]


def solution(mesh):
    spread = ("group", "ctx")
    in_specs = (
        P("group", "ctx", None),
        P("group", "ctx", None),
        P("group", "ctx"),
        P(None, spread),
        P(spread),
        P(spread, None),
        P(None, spread),
        P(spread),
        P(None, spread),
        P(spread),
    )
    return jax.shard_map(
        shards, mesh=mesh, in_specs=in_specs, out_specs=P("group", "ctx", None), check_vma=False
    )
```

time: 1950 us -> 344 us (0.18)
  the two profiles are of different devices: /device:TPU:18 before, /device:TPU:1 now
where the time goes in v1:
time: 344 us; the launch traced here: 343 us
  blocking collectives  178 us (52%)
  Pallas kernels  93.7 us (27%)
  starting transfers between devices  24.7 us (7%)
  waiting for transfers between devices  16.2 us (5%)
  local copies, waits for them, and re-layouts  15.3 us (4%)
  between operations  14.1 us (4%)
    all_gather x4, blocking collectives, everywhere(): return lax.all_gather(lax.all_gather(shard, 'group'), 'ctx')  156 us
    pallas_call x1, Pallas kernels, scan_pass(): pl.pallas_call(scan_kernel, grid_spec=pltpu.PrefetchScalarGridSpec(num_sc...  44.9 us
    pallas_call x1, Pallas kernels, gate_pass(): pl.pallas_call(gate_kernel, grid_spec=pltpu.PrefetchScalarGridSpec(num_sc...  34.5 us
    all_to_all x1, blocking collectives, shards(): hin = lax.all_to_all(hin, 'ctx', split_axis=0, concat_axis=0, tiled=True)  22.7 us
    ppermute x1, starting transfers between devices, shards(): rim = lax.ppermute(edge, 'ctx', [(i, i + 1) for i in range(blocks - 1)])  18.7 us
    all_to_all x1, waiting for transfers between devices, shards(): ends = lax.all_to_all(ends, 'ctx', split_axis=0, concat_axis=0, tiled=True)  16.1 us
    pallas_call x1, Pallas kernels, conv_proj(): pl.pallas_call(conv_kernel, grid_spec=pltpu.PrefetchScalarGridSpec(num_sc...  12.3 us
  transfers between devices with their start and end apart: 4, of which 1 were waited for; matrix products, arithmetic and copies ran while one was open for 3% of the time, Pallas kernels for 4%

profile of v1, /device:TPU:1, one launch (start us, length us, event | category | flops | bytes accessed | tf_op | source)
XLA Modules:
  0.0 343.3 jit_solution(18323347181461822154)
XLA Ops:
  6.5 0.0 all-gather.10.cloned.1.call-start
  6.5 25.9 %all-gather.2 = bf16[256,288]{1,0:T(8,128)(2,1)} all-gather(bf16[32,288]{1,0:T(8,128)(2,1)} %param.15), channel_id=4, replica_groups=mesh['group'=8,'ctx'=32] {'group'}, dimensions={0}, use_global_device_ids=true | all-gather | bytes 165888 | tf_op jit(solution)/shard_map/all_gather | solution.py:259
  32.5 0.0 all-gather.10.cloned.1.call-update
  32.5 0.0 all-gather.12.cloned.1.call-start
  32.5 24.0 %all-gather.4 = bf16[256,256]{1,0:T(8,128)(2,1)} all-gather(bf16[32,256]{1,0:T(8,128)(2,1)} %bitcast.36), channel_id=6, replica_groups=mesh['group'=8,'ctx'=32] {'group'}, dimensions={0}, use_global_device_ids=true | all-gather | bytes 147456 | tf_op jit(solution)/shard_map/all_gather | solution.py:259
  56.5 0.0 all-gather.12.cloned.1.call-update
  57.2 1.0 bitcast_select_fusion
  58.2 18.7 %collective-permute-start = (bf16[3,8192]{1,0:T(4,128)(2,1)S(1)}, bf16[3,8192]{1,0:T(4,128)(2,1)S(1)}, u32[]{:S(2)}, u32[]{:S(2)}) collective-permute-start(bf16[3,8192]{1,0:T(4,128)(2,1)S(1)} %bitcast_select_fusion), channel_id=1, source_target_pairs={{0,1},{1,2},{2,3},{3,4},{4,5},{5,6},{6,7},{7,8},{8,9},{9,10},{10,1... | collective-permute-start | bytes 147464 | tf_op jit(solution)/shard_map/ppermute | solution.py:285
  76.9 1.5 concatenate.7
  78.4 27.4 %all-gather.6 = f32[8,23,32]{2,1,0:T(8,128)S(1)} all-gather(f32[1,23,32]{2,1,0:T(8,128)S(1)} %bitcast.35), channel_id=2, replica_groups=mesh['group'=8,'ctx'=32] {'group'}, dimensions={0}, use_global_device_ids=true | all-gather | bytes 26496 | tf_op jit(solution)/shard_map/all_gather | solution.py:259
  105.9 78.2 %all-gather.1 = f32[256,23,32]{2,0,1:T(8,128)S(1)} all-gather(f32[8,23,32]{2,0,1:T(8,128)S(1)} %copy.13), channel_id=3, replica_groups=mesh['group'=8,'ctx'=32] {'ctx'}, dimensions={0}, use_global_device_ids=true | all-gather | bytes 777216 | tf_op jit(solution)/shard_map/all_gather | solution.py:259
  184.1 0.9 copy.16
  185.0 0.1 slice.37
  185.1 0.3 slice.39
  185.4 1.1 slice.31.par_ref
  186.5 1.7 slice.34.alog_ref
  188.1 0.0 collective-permute-done
  188.1 0.7 concatenate.6.rim_ref
  188.8 0.0 all-gather.10.cloned.1.call-done
  188.8 12.3 %conv_proj.1 = (bf16[256,8192]{1,0:T(8,128)(2,1)}, f32[256,288]{1,0:T(8,128)}) custom-call(s32[1]{0:T(128)} %bitcast.21.len_ref, bf16[256,8192]{1,0:T(8,128)(2,1)} %bitcast.29, bf16[8,8192]{1,0:T(8,128)(2,1)} %concatenate.6.rim_ref, f32[7,64,128]{2,1,0:T(8,128)} %slice.31.par_ref, bf16[32,8,32,288]{3,2,1,0:T(8,128)(2,1)} %bitcast.28), custom_call_target="tpu_custom_call" | custom-call | tf_op jit(solution)/shard_map/conv_proj/pallas_call | solution.py:56
  201.1 1.6 slice.42.low_ref
  202.8 1.1 fusion
  203.8 0.1 broadcast_in_dim.47
  203.9 0.1 broadcast_in_dim.45
  204.0 0.0 all-gather.12.cloned.1.call-done
  204.1 2.0 broadcast_in_dim.48.c_ref
  206.1 1.9 broadcast_in_dim.46.b_ref
  208.0 44.9 %scan_pass.1 = (f32[256,64,128]{2,1,0:T(8,128)}, f32[256,64,128]{2,1,0:T(8,128)}, f32[32,40,128]{2,1,0:T(8,128)}) custom-call(s32[1]{0:T(128)} %bitcast.22.len_ref, bf16[256,256]{1,0:T(8,128)(2,1)} %slice.42.low_ref, bf16[32,8,32,256]{3,2,1,0:T(8,128)(2,1)} %bitcast.31, f32[7,64,128]{2,1,0:T(8,128)} %slice.31.par_ref, f32[16,64,128]{2,1,0:T(8,128)} %slice.34.alog_ref, ...), custom_call_target="tpu_custom_call" | custom-call | tf_op jit(solution)/shard_map/scan_pass/pallas_call | solution.py:139
  252.9 6.0 %all-to-all-start = ((f32[32,40,128]{2,1,0:T(8,128)}), f32[32,40,128]{2,1,0:T(8,128)S(1)}, u32[]{:S(2)}, u32[]{:S(2)}) async-start(f32[32,40,128]{2,1,0:T(8,128)} %get-tuple-element.14), calls=%async_computation | async-start | bytes 1310720 | tf_op jit(solution)/shard_map/all_to_all | solution.py:296
  258.8 1.5 constant_dynamic-slice_fusion
  260.3 16.1 %all-to-all-done.end_ref = f32[32,40,128]{2,1,0:T(8,128)S(1)} async-done(((f32[32,40,128]{2,1,0:T(8,128)}), f32[32,40,128]{2,1,0:T(8,128)S(1)}, u32[]{:S(2)}, u32[]{:S(2)}) %all-to-all-start) | async-done | bytes 655392 | tf_op jit(solution)/shard_map/all_to_all | solution.py:296
  276.4 0.0 copy-start
  276.4 0.8 copy-done
  277.2 2.0 prefix.1
  279.2 22.7 %all_to_all.10.hin_ref = f32[32,32,128]{2,1,0:T(8,128)} all-to-all(f32[32,32,128]{2,1,0:T(8,128)} %prefix.1), channel_id=1, replica_groups=mesh['group'=8,'ctx'=32] {'ctx'}, dimensions={0} | all-to-all | bytes 1048576 | tf_op jit(solution)/shard_map/all_to_all | solution.py:298
  301.9 34.5 %gate_pass.1 = bf16[256,8192]{1,0:T(8,128)(2,1)} custom-call(s32[1]{0:T(128)} %bitcast.23.len_ref, f32[256,64,128]{2,1,0:T(8,128)} %get-tuple-element.12.y_ref, f32[256,64,128]{2,1,0:T(8,128)} %get-tuple-element.13.cum_ref, f32[32,32,128]{2,1,0:T(8,128)} %all_to_all.10.hin_ref, f32[7,64,128]{2,1,0:T(8,128)} %slice.31.par_ref, ...), custom_call_target="tpu_custom_call" | custom-call | tf_op jit(solution)/shard_map/gate_pass/pallas_call | solution.py:230
  (2 shorter events, 0.0 us)
Async XLA Ops:
  6.5 182.3 %all-gather.10.cloned.1.call-start = ((), (), s32[]{:S(2)}) async-start(), calls=%async_computation.2 | async-start | bytes 6488064 | tf_op jit(solution)/shard_map/all_gather | solution.py:259
  32.5 171.6 %all-gather.12.cloned.1.call-start = ((), (), s32[]{:S(2)}) async-start(), calls=%async_computation.3 | async-start | bytes 4325376 | tf_op jit(solution)/shard_map/all_gather | solution.py:259
  58.2 129.9 %collective-permute-start = (bf16[3,8192]{1,0:T(4,128)(2,1)S(1)}, bf16[3,8192]{1,0:T(4,128)(2,1)S(1)}, u32[]{:S(2)}, u32[]{:S(2)}) collective-permute-start(bf16[3,8192]{1,0:T(4,128)(2,1)S(1)} %bitcast_select_fusion), channel_id=1, source_target_pairs={{0,1},{1,2},{2,3},{3,4},{4,5},{5,6},{6,7},{7,8},{8,9},{9,10},{10,1... | collective-permute-start | bytes 147464 | tf_op jit(solution)/shard_map/ppermute | solution.py:285
  252.9 23.5 %all-to-all-start = ((f32[32,40,128]{2,1,0:T(8,128)}), f32[32,40,128]{2,1,0:T(8,128)S(1)}, u32[]{:S(2)}, u32[]{:S(2)}) async-start(f32[32,40,128]{2,1,0:T(8,128)} %get-tuple-element.14), calls=%async_computation | async-start | bytes 1310720 | tf_op jit(solution)/shard_map/all_to_all | solution.py:296
  276.4 0.8 copy-start
Sparse Core Ops, SparseCore 0:
  32.6 78.6 all-gather.9
  113.8 71.4 all-gather.11

commit v2 on v1

v2 whole, which is shorter than its diff:
```python
import jax
import jax.numpy as jnp
from jax import lax
from jax.experimental import pallas as pl
from jax.experimental.pallas import tpu as pltpu
from jax.sharding import PartitionSpec as P

LOG2E = 1.4426950408889634
LANES = 128
ROWS = 8
VECTORS = 7
WIDE = ROWS * LANES


def sigmoid(v):
    return 1.0 / (1.0 + jnp.exp(-v))


def settings():
    return pltpu.CompilerParams(dimension_semantics=("arbitrary",), vmem_limit_bytes=56 << 20)


def whole(shape):
    return pl.BlockSpec(shape, lambda i, *_: (0,) * len(shape))


def per_step(count):
    return pl.BlockSpec((count, ROWS, LANES), lambda i, *_: (0, i, 0))


def conv_kernel(len_ref, x_ref, rim_ref, raw_ref, act_ref, par_ref, pad_ref):
    tok, width = x_ref.shape
    quarter = LANES // 4
    spot = lax.broadcasted_iota(jnp.int32, (ROWS, LANES), 1) // quarter
    for r in range(par_ref.shape[0] // 4):
        rows = [raw_ref[pl.ds(q * 64 + r, ROWS, stride=8), :] for q in range(4)]
        for j in range(4):
            turned = [rows[q] if q == j else pltpu.roll(rows[q], ((q - j) % 4) * quarter, 1) for q in range(4)]
            low = jnp.where(spot == 0, turned[0], turned[1])
            high = jnp.where(spot == 2, turned[2], turned[3])
            par_ref[4 * r + j] = jnp.where(spot < 2, low, high)
    keep = lax.broadcasted_iota(jnp.int32, (tok, LANES), 0) < len_ref[0]
    for g in range(width // LANES):
        cols = slice(g * LANES, (g + 1) * LANES)
        pad_ref[0:8, :] = rim_ref[:, cols].astype(jnp.float32)
        pad_ref[8 : 8 + tok, :] = jnp.where(keep, x_ref[:, cols].astype(jnp.float32), 0.0)
        total = par_ref[4, g : g + 1, :] + par_ref[0, g : g + 1, :] * pad_ref[5 : 5 + tok, :]
        for k in range(1, 4):
            total = total + par_ref[k, g : g + 1, :] * pad_ref[5 + k : 5 + k + tok, :]
        act_ref[:, cols] = (total * sigmoid(total)).astype(jnp.bfloat16)


def convolve(length, x, rim, raw, count):
    tok, chans = x.shape
    return pl.pallas_call(
        conv_kernel,
        grid_spec=pltpu.PrefetchScalarGridSpec(
            num_scalar_prefetch=1,
            grid=(chans // WIDE,),
            in_specs=[
                pl.BlockSpec((tok, WIDE), lambda i, *_: (0, i)),
                pl.BlockSpec((8, WIDE), lambda i, *_: (0, i)),
                pl.BlockSpec((256, LANES), lambda i, *_: (i, 0)),
            ],
            out_specs=[pl.BlockSpec((tok, WIDE), lambda i, *_: (0, i)), per_step(count)],
            scratch_shapes=[pltpu.VMEM((tok + 8, LANES), jnp.float32)],
        ),
        out_shape=[
            jax.ShapeDtypeStruct((tok, chans), jnp.bfloat16),
            jax.ShapeDtypeStruct((count, chans // LANES, LANES), jnp.float32),
        ],
        compiler_params=settings(),
        name="convolve",
    )(length, x, rim, raw)


def piece_specs(pieces):
    specs = []
    for k, p in enumerate(pieces):
        rest = (p.shape[1], p.shape[2], 1, *p.shape[4:])
        if k < len(pieces) // 2:
            specs.append(
                pl.BlockSpec((1, *rest), lambda i, s: ((jnp.minimum(i, 7) - s[2]) & 3, 0, 0, jnp.minimum(i, 7) // 4, 0, 0))
            )
        else:
            specs.append(pl.BlockSpec((4, *rest), lambda i, s: (0, 0, 0, jnp.minimum(i, 7) // 4, 0, 0)))
    return specs


def assemble(step, info_ref, piece_refs, w_ref):
    own_x, own_y, own_core = info_ref[1], info_ref[2], info_ref[3]
    half = piece_refs[0].shape[4]
    many = len(piece_refs) // 2
    ahead = 1 + 2 * own_core
    away = (0, ahead, 4 - ahead, 2, 2)
    first = (0, 0, 0, own_core, 1 - own_core)
    for j, ref in enumerate(piece_refs[:many]):
        at = (own_x + away[j]) & 3
        for core in range(ref.shape[1]):
            for h in range(ref.shape[2]):
                w_ref[at, h, first[j] + core, 0:half, :] = ref[0, core, h, 0]
    wanted = (step - own_y) & 3
    for j, ref in enumerate(piece_refs[many:]):

        @pl.when(wanted == away[j])
        def _(ref=ref, first=first[j]):
            for q in range(4):
                for core in range(ref.shape[1]):
                    for h in range(ref.shape[2]):
                        w_ref[(own_x + q) & 3, h, first + core, half : 2 * half, :] = ref[q, core, h, 0]


def scan_kernel(info_ref, par_ref, act_ref, *refs):
    *piece_refs, y_ref, cum_ref, end_ref, c_ref, sum_scr, low_scr, b_scr, act_scr, d_scr, x_scr, a_scr, w_scr = refs
    step = pl.program_id(0)
    many = act_scr.shape[0]
    tok, rank = low_scr.shape
    states = a_scr.shape[0]

    @pl.when(step < many)
    def _():
        assemble(step, info_ref, piece_refs, w_scr.at[step])
        weight = w_scr[step].reshape(WIDE, w_scr.shape[-1])[:, : sum_scr.shape[1]]
        act_scr[step] = act_ref[...]
        part = jnp.dot(act_ref[...], weight, preferred_element_type=jnp.float32)

        @pl.when(step == 0)
        def _():
            sum_scr[...] = part

        @pl.when(step > 0)
        def _():
            sum_scr[...] += part

        @pl.when(step == many - 1)
        def _():
            low_scr[...] = sum_scr[:, :rank].astype(jnp.bfloat16)
            for n in range(states):
                for ref, col in ((b_scr, rank + n), (c_ref, rank + states + n)):
                    ref[n * tok : (n + 1) * tok, :] = jnp.broadcast_to(sum_scr[:, col : col + 1], (tok, LANES))

    @pl.when(step >= many)
    def _():
        at = step - many
        keep = lax.broadcasted_iota(jnp.int32, (tok, LANES), 0) < info_ref[0]
        raw = lax.dot_general(
            low_scr[...],
            w_scr[at].reshape(WIDE, w_scr.shape[-1])[:, w_scr.shape[-1] - rank :],
            (((1,), (1,)), ((), ())),
            preferred_element_type=jnp.float32,
        )
        for g in range(ROWS):
            cols = slice(g * LANES, (g + 1) * LANES)
            v = raw[:, cols] + par_ref[5, g : g + 1, :]
            soft = jnp.maximum(v, 0.0) + jnp.log1p(jnp.exp(-jnp.abs(v)))
            d = jnp.where(keep, soft, 0.0)
            place = slice(g * 8, (g + 1) * 8)
            d_scr[:, place, :] = d.reshape(tok // 8, 8, LANES)
            dx = d * act_scr[at, :, cols].astype(jnp.float32)
            x_scr[:, place, :] = dx.reshape(tok // 8, 8, LANES)
        a_scr[...] = jnp.exp(par_ref[VECTORS : VECTORS + states]) * (-LOG2E)

        def block(i, carry):
            hs, cum = carry
            hs = list(hs)
            for o in range(16):
                t = i * 16 + o
                tile = i * 2 + o // 8
                d = d_scr[tile, pl.ds(o % 8, ROWS, stride=8), :]
                dx = x_scr[tile, pl.ds(o % 8, ROWS, stride=8), :]
                cum = cum + d
                acc = [None] * 4
                for n in range(states):
                    b = b_scr[pl.ds(n * tok + t, ROWS, stride=0), :]
                    c = c_ref[pl.ds(n * tok + t, ROWS, stride=0), :]
                    hs[n] = jnp.exp2(a_scr[n] * d) * hs[n] + dx * b
                    term = c * hs[n]
                    acc[n % 4] = term if acc[n % 4] is None else acc[n % 4] + term
                y_ref[t] = (acc[0] + acc[1]) + (acc[2] + acc[3])
                cum_ref[t] = cum
            return tuple(hs), cum

        zero = jnp.zeros((ROWS, LANES), jnp.float32)
        hs, cum = lax.fori_loop(0, tok // 16, block, ((zero,) * states, zero))
        for q in range(ROWS // 2):
            pair = slice(2 * q, 2 * q + 2)
            for n in range(states):
                end_ref[q, 2 * n : 2 * n + 2, :] = hs[n][pair]
            for k in range(4):
                row = 2 * states + 2 * k
                end_ref[q, row : row + 2, :] = cum[pair]


def scan_pass(info, pars, act, pieces, rank, states):
    tok, chans = act.shape
    rows, cols = pieces[0].shape[4:]
    many = chans // WIDE
    groups = chans // LANES
    sent = 2 * states + 8

    def turn(shape, where):
        def index(i, s):
            later = jnp.maximum(i - many, 0)
            return (0,) * where + (later,) + (0,) * (len(shape) - 1 - where)

        return pl.BlockSpec(shape, index)

    return pl.pallas_call(
        scan_kernel,
        grid_spec=pltpu.PrefetchScalarGridSpec(
            num_scalar_prefetch=1,
            grid=(2 * many,),
            in_specs=[
                turn((pars.shape[0], ROWS, LANES), 1),
                pl.BlockSpec((tok, WIDE), lambda i, s: (0, jnp.minimum(i, many - 1))),
                *piece_specs(pieces),
            ],
            out_specs=[
                turn((tok, ROWS, LANES), 1),
                turn((tok, ROWS, LANES), 1),
                turn((ROWS // 2, sent, LANES), 0),
                whole((tok * states, LANES)),
            ],
            scratch_shapes=[
                pltpu.VMEM((tok, cols - rank), jnp.float32),
                pltpu.VMEM((tok, rank), jnp.bfloat16),
                pltpu.VMEM((tok * states, LANES), jnp.float32),
                pltpu.VMEM((many, tok, WIDE), jnp.bfloat16),
                pltpu.VMEM((tok // 8, 8 * ROWS, LANES), jnp.float32),
                pltpu.VMEM((tok // 8, 8 * ROWS, LANES), jnp.float32),
                pltpu.VMEM((states, ROWS, LANES), jnp.float32),
                pltpu.VMEM((many, 4, 4, 2, 2 * rows, cols), jnp.bfloat16),
            ],
        ),
        out_shape=[
            jax.ShapeDtypeStruct((tok, groups, LANES), jnp.float32),
            jax.ShapeDtypeStruct((tok, groups, LANES), jnp.float32),
            jax.ShapeDtypeStruct((groups // 2, sent, LANES), jnp.float32),
            jax.ShapeDtypeStruct((tok * states, LANES), jnp.float32),
        ],
        compiler_params=settings(),
        name="scan_pass",
    )(info, pars, act, *pieces)


def prefix_kernel(end_ref, alog_ref, in_ref):
    blocks = end_ref.shape[0]
    rows = alog_ref.shape[0]
    a = [jnp.exp(alog_ref[r : r + 8, :]) * (-LOG2E) for r in range(0, rows, 8)]
    hs = [jnp.zeros((8, LANES), jnp.float32) for _ in a]
    for k in range(blocks):
        spent = end_ref[k, rows : rows + 8, :]
        for j in range(len(a)):
            in_ref[k, 8 * j : 8 * j + 8, :] = hs[j]
            hs[j] = jnp.exp2(a[j] * spent) * hs[j] + end_ref[k, 8 * j : 8 * j + 8, :]


def prefix(ends, alog):
    return pl.pallas_call(
        prefix_kernel,
        out_shape=jax.ShapeDtypeStruct((ends.shape[0], *alog.shape), jnp.float32),
        name="prefix",
    )(ends, alog)


def gate_kernel(len_ref, y_ref, cum_ref, hin_ref, par_ref, act_ref, z_ref, c_ref, out_ref, y_scr, a_scr, h_scr):
    tok = act_ref.shape[0]
    states = a_scr.shape[0]
    a_scr[...] = jnp.exp(par_ref[VECTORS : VECTORS + states]) * (-LOG2E)
    for q in range(ROWS // 2):
        for n in range(states):
            h_scr[n, 2 * q : 2 * q + 2, :] = hin_ref[q, 2 * n : 2 * n + 2, :]

    def block(i, carry):
        for o in range(8):
            t = i * 8 + o
            cum = cum_ref[t]
            acc = [y_ref[t]] + [None] * 3
            for n in range(states):
                c = c_ref[pl.ds(n * tok + t, ROWS, stride=0), :]
                term = (c * h_scr[n]) * jnp.exp2(a_scr[n] * cum)
                acc[n % 4] = term if acc[n % 4] is None else acc[n % 4] + term
            y_scr[i, pl.ds(o, ROWS, stride=8), :] = (acc[0] + acc[1]) + (acc[2] + acc[3])
        return carry

    lax.fori_loop(0, tok // 8, block, 0)
    keep = lax.broadcasted_iota(jnp.int32, (tok, LANES), 0) < len_ref[0]
    for g in range(ROWS):
        cols = slice(g * LANES, (g + 1) * LANES)
        y = y_scr[:, g * 8 : (g + 1) * 8, :].reshape(tok, LANES)
        z = z_ref[:, cols].astype(jnp.float32)
        out = (y + par_ref[6, g : g + 1, :] * act_ref[:, cols].astype(jnp.float32)) * (z * sigmoid(z))
        out_ref[:, cols] = jnp.where(keep, out, 0.0).astype(jnp.bfloat16)


def gate_pass(info, y, cum, hin, pars, act, z, c_wide):
    tok, chans = act.shape
    states = c_wide.shape[0] // tok
    columns = pl.BlockSpec((tok, WIDE), lambda i, *_: (0, i))
    return pl.pallas_call(
        gate_kernel,
        grid_spec=pltpu.PrefetchScalarGridSpec(
            num_scalar_prefetch=1,
            grid=(chans // WIDE,),
            in_specs=[
                per_step(tok),
                per_step(tok),
                pl.BlockSpec((ROWS // 2, 2 * states, LANES), lambda i, *_: (i, 0, 0)),
                per_step(pars.shape[0]),
                columns,
                columns,
                whole((tok * states, LANES)),
            ],
            out_specs=columns,
            scratch_shapes=[
                pltpu.VMEM((tok // 8, 8 * ROWS, LANES), jnp.float32),
                pltpu.VMEM((states, ROWS, LANES), jnp.float32),
                pltpu.VMEM((states, ROWS, LANES), jnp.float32),
            ],
        ),
        out_shape=jax.ShapeDtypeStruct((tok, chans), jnp.bfloat16),
        compiler_params=settings(),
        name="gate_pass",
    )(info, y, cum, hin, pars, act, z, c_wide)


def device(x, y, z, core):
    return ((z & 1) * 4 + y) * 32 + x * 8 + (z >> 1) * 2 + core


def fetch(value, move):
    route = []
    for x in range(4):
        for y in range(4):
            for z in range(8):
                for core in range(2):
                    route.append((device(*move(x, y, z, core)), device(x, y, z, core)))
    return lax.ppermute(value, ("group", "ctx"), route)


def onward(axis):
    def move(x, y, z, core):
        step = 1 - 2 * core
        return ((x + step) % 4, y, z, core) if axis == "x" else (x, (y + step) % 4, z, core)

    return move


def flip(axis, bit):
    def move(x, y, z, core):
        return x ^ (bit if axis == "x" else 0), y ^ (bit if axis == "y" else 0), z ^ (bit if axis == "z" else 0), core ^ (
            bit if axis == "core" else 0
        )

    return move


def double(value, axis, bit, own):
    other = fetch(value, flip(axis, bit))
    low = (own & bit) == 0
    return jnp.concatenate([jnp.where(low, value, other), jnp.where(low, other, value)], axis=0)


def farther(near, axis, own_core):
    return fetch(jnp.where(own_core == 0, near[:, :1], near[:, 1:]), onward(axis))


def swap(value):
    return fetch(value, flip("core", 1))


def row_of_four(value, axis, own_core):
    near = fetch(value, onward(axis))
    far = farther(near, axis, own_core)
    near_too, far_too = swap(near), swap(far)
    zero = own_core == 0
    far = jnp.concatenate([jnp.where(zero, far, far_too), jnp.where(zero, far_too, far)], axis=1)
    return jnp.concatenate([value, jnp.where(zero, near, near_too), far, jnp.where(zero, near_too, near)], axis=0)


def shards(
    hidden_x, gate_z, lengths, conv_weight, conv_bias, xproj_weight, dtproj_weight, dt_bias, a_log, skip_gain
):
    x, z = hidden_x[0], gate_z[0]
    tok, chans = x.shape
    taps = conv_weight.shape[0]
    rank = dtproj_weight.shape[0]
    states = a_log.shape[0]
    blocks = lax.axis_size("ctx")
    length = lengths[0]
    group, ctx = lax.axis_index("group"), lax.axis_index("ctx")
    own_x, own_y, own_core = ctx >> 3, group & 3, ctx & 1
    own_z = ((ctx >> 1) & 3) * 2 + (group >> 2)
    own = {"x": own_x, "y": own_y, "z": own_z, "core": own_core}
    info = jnp.stack([lengths[0, 0], own_x, own_y, own_core]).astype(jnp.int32)

    edge = jnp.arange(tok - (taps - 1), tok, dtype=jnp.int32)[:, None] < length
    edge = jnp.where(edge, x[tok - (taps - 1) :], jnp.bfloat16(0))
    rim = lax.ppermute(edge, "ctx", [(i, i + 1) for i in range(blocks - 1)])
    rim = jnp.concatenate([jnp.zeros((8 - (taps - 1), chans), x.dtype), rim], axis=0)

    small = jnp.concatenate(
        [conv_weight, conv_bias[None], dt_bias[None], skip_gain[None], a_log, a_log[:1]], axis=0
    )
    width = small.shape[1]
    count = small.shape[0]
    small = small.reshape(1, count // 4, 4 * width)
    small = jnp.pad(small, ((0, 0), (0, 8 - count // 4), (0, 0)))
    for axis, bit in (("z", 4), ("x", 1), ("x", 2), ("core", 1), ("z", 2), ("y", 1), ("y", 2), ("z", 1)):
        small = double(small, axis, bit, own[axis])
    small = small.reshape(-1, LANES)

    fill = -(xproj_weight.shape[1] + rank) % LANES
    mats = jnp.concatenate(
        [xproj_weight, jnp.zeros((width, fill), xproj_weight.dtype), dtproj_weight.T], axis=1
    )[None]
    for axis, bit in (("z", 1), ("z", 2), ("z", 4), ("core", 1)):
        mats = double(mats, axis, bit, own[axis])
    mats = mats.reshape(1, 2, 4, 2, *mats.shape[1:])
    upper = row_of_four(mats[..., : width // 2, :], "y", own_core)
    lower = row_of_four(mats[..., width // 2 :, :], "x", own_core)
    near_x, near_y = fetch(upper, onward("x")), fetch(lower, onward("y"))
    act, pars = convolve(length, x, rim, small, count)
    near_x, near_y, act = lax.optimization_barrier((near_x, near_y, act))
    pieces = []
    for value, near, axis in ((upper, near_x, "x"), (lower, near_y, "y")):
        far = farther(near, axis, own_core)
        pieces += [value, near, swap(near), far, swap(far)]

    y, cum, ends, c_wide = scan_pass(info, pars, act, pieces, rank, states)
    mine = lax.dynamic_slice_in_dim(pars[VECTORS : VECTORS + states], 2 * ctx, 2, axis=1).reshape(2 * states, LANES)
    ends = lax.all_to_all(ends, "ctx", split_axis=0, concat_axis=0, tiled=True)
    hin = prefix(ends, mine)
    hin = lax.all_to_all(hin, "ctx", split_axis=0, concat_axis=0, tiled=True)
    out = gate_pass(info, y, cum, hin, pars, act, z, c_wide)
    return out[None]


def solution(mesh):
    spread = ("group", "ctx")
    in_specs = (
        P("group", "ctx", None),
        P("group", "ctx", None),
        P("group", "ctx"),
        P(None, spread),
        P(spread),
        P(spread, None),
        P(None, spread),
        P(spread),
        P(None, spread),
        P(spread),
    )
    return jax.shard_map(
        shards, mesh=mesh, in_specs=in_specs, out_specs=P("group", "ctx", None), check_vma=False
    )
```

time: 344 us -> 258 us (0.75)
  blocking collectives: 178 us -> 22.9 us
  starting transfers between devices: 24.7 us -> 80.7 us
  waiting for transfers between devices: 16.2 us -> 35.2 us
  between operations: 14.1 us -> 1.02 us
  Pallas kernels: 93.7 us -> 104 us
  local copies, waits for them, and re-layouts: 15.3 us -> 7.46 us
  other arithmetic: 1.01 us -> 5.58 us
    all_gather x4 -> x0, blocking collectives: 156 us -> none  [everywhere(): return lax.all_gather(lax.all_gather(shard, 'group'), 'ctx')]
    ppermute x0 -> x28, starting transfers between devices: none -> 66.7 us  [fetch(): return lax.ppermute(value, ('group', 'ctx'), route)]
    ppermute x0 -> x28, waiting for transfers between devices: none -> 14.8 us  [fetch(): return lax.ppermute(value, ('group', 'ctx'), route)]
    ppermute x1, starting transfers between devices: 18.7 us -> 7.06 us  [shards(): rim = lax.ppermute(edge, 'ctx', [(i, i + 1) for i in range(blocks - 1)])]
    pallas_call x1, Pallas kernels: 44.9 us -> 56.5 us  [scan_pass(): pl.pallas_call(scan_kernel, grid_spec=pltpu.PrefetchScalarGridSpec(num_sc...]
    slice x6 -> x3, local copies, waits for them, and re-layouts: 5.8 us -> 0.79 us  [the longest x1 0.69 us: shards(): a_log[:1]]
    broadcast_in_dim x4 -> x1, local copies, waits for them, and re-layouts: 4.09 us -> 0.01 us  [shards(): jnp.zeros((width, fill), xproj_weight.dtype)]
  transfers between devices with their start and end apart: 4 -> 30, of which waited for: 1 -> 11; matrix products, arithmetic and copies ran while one was open for 3% -> 2% of each run, Pallas kernels for 4% -> 4%
where the time goes in v2:
time: 258 us; the launch traced here: 257 us
  Pallas kernels  104 us (40%)
  starting transfers between devices  80.7 us (31%)
  waiting for transfers between devices  35.2 us (14%)
  blocking collectives  22.9 us (9%)
  local copies, waits for them, and re-layouts  7.46 us (3%)
  other arithmetic  5.58 us (2%)
    ppermute x28, starting transfers between devices, fetch(): return lax.ppermute(value, ('group', 'ctx'), route)  66.7 us
    pallas_call x1, Pallas kernels, scan_pass(): pl.pallas_call(scan_kernel, grid_spec=pltpu.PrefetchScalarGridSpec(num_sc...  56.5 us
    pallas_call x1, Pallas kernels, gate_pass(): pl.pallas_call(gate_kernel, grid_spec=pltpu.PrefetchScalarGridSpec(num_sc...  35.5 us
    all_to_all x1, blocking collectives, shards(): hin = lax.all_to_all(hin, 'ctx', split_axis=0, concat_axis=0, tiled=True)  22.9 us
    all_to_all x1, waiting for transfers between devices, shards(): ends = lax.all_to_all(ends, 'ctx', split_axis=0, concat_axis=0, tiled=True)  19.1 us
    ppermute x28, waiting for transfers between devices, fetch(): return lax.ppermute(value, ('group', 'ctx'), route)  14.8 us
    pallas_call x1, Pallas kernels, convolve(): pl.pallas_call(conv_kernel, grid_spec=pltpu.PrefetchScalarGridSpec(num_sc...  9.87 us
    ppermute x1, starting transfers between devices, shards(): rim = lax.ppermute(edge, 'ctx', [(i, i + 1) for i in range(blocks - 1)])  7.06 us
  transfers between devices with their start and end apart: 30, of which 11 were waited for; matrix products, arithmetic and copies ran while one was open for 2% of the time, Pallas kernels for 4%

profile of v2, /device:TPU:1, one launch (start us, length us, event | category | flops | bytes accessed | tf_op | source)
XLA Modules:
  0.0 256.7 jit_solution(17012494289002169746)
XLA Ops:
  0.0 0.7 slice.44
  0.7 1.5 concatenate.58
  2.3 7.8 %collective-permute-start.1 = (f32[1,8,128]{2,1,0:T(8,128)S(1)}, f32[1,8,128]{2,1,0:T(8,128)S(1)}, u32[]{:S(2)}, u32[]{:S(2)}) collective-permute-start(f32[1,8,128]{2,1,0:T(8,128)S(1)} %pad.5), channel_id=1, source_target_pairs={{4,0},{5,1},{132,128},{133,129},{6,2},{7,3},{134,130},{135,131},{0... | collective-permute-start | bytes 12296 | tf_op jit(solution)/shard_map/ppermute | solution.py:338
  10.1 0.9 collective-permute-done.1
  11.1 1.2 collective-permute-start.2
  12.3 0.8 maximum_bitcast_fusion.1
  13.0 0.8 collective-permute-start.9
  14.5 2.5 collective-permute-start.3
  17.1 1.6 collective-permute-done.3
  18.7 0.8 broadcast_select_fusion.21
  19.6 2.4 collective-permute-start.10
  22.0 3.8 %collective-permute-start.4 = (f32[8,8,128]{2,1,0:T(8,128)S(1)}, f32[8,8,128]{2,1,0:T(8,128)S(1)}, u32[]{:S(2)}, u32[]{:S(2)}) collective-permute-start(f32[8,8,128]{2,1,0:T(8,128)S(1)} %pad_maximum_fusion.10), channel_id=1, source_target_pairs={{1,0},{0,1},{129,128},{128,129},{3,2},{2,3},{131,130},{130,131},{5... | collective-permute-start | bytes 98312 | tf_op jit(solution)/shard_map/ppermute | solution.py:338
  25.9 4.4 %collective-permute-start.11 = (bf16[4,32,640]{2,1,0:T(8,128)(2,1)S(1)}, bf16[4,32,640]{2,1,0:T(8,128)(2,1)S(1)}, u32[]{:S(2)}, u32[]{:S(2)}) collective-permute-start(bf16[4,32,640]{2,1,0:T(8,128)(2,1)S(1)} %pad_maximum_fusion.6), channel_id=1, source_target_pairs={{4,0},{5,1},{132,128},{133,129},{6,2},{7,3},{134,130},{135,131},{0... | collective-permute-start | bytes 491528 | tf_op jit(solution)/shard_map/ppermute | solution.py:338
  30.2 1.2 collective-permute-start.5
  31.5 2.7 %collective-permute-done.11 = bf16[4,32,640]{2,1,0:T(8,128)(2,1)S(1)} collective-permute-done((bf16[4,32,640]{2,1,0:T(8,128)(2,1)S(1)}, bf16[4,32,640]{2,1,0:T(8,128)(2,1)S(1)}, u32[]{:S(2)}, u32[]{:S(2)}) %collective-permute-start.11) | collective-permute-done | bytes 163872 | tf_op jit(solution)/shard_map/ppermute | solution.py:338
  34.2 7.4 %collective-permute-start.12 = (bf16[8,32,640]{2,1,0:T(8,128)(2,1)S(1)}, bf16[8,32,640]{2,1,0:T(8,128)(2,1)S(1)}, u32[]{:S(2)}, u32[]{:S(2)}) collective-permute-start(bf16[8,32,640]{2,1,0:T(8,128)(2,1)S(1)} %pad_maximum_fusion.4), channel_id=1, source_target_pairs={{1,0},{0,1},{129,128},{128,129},{3,2},{2,3},{131,130},{130,131},{5... | collective-permute-start | bytes 983048 | tf_op jit(solution)/shard_map/ppermute | solution.py:338
  41.6 1.4 collective-permute-start.6
  43.2 0.9 collective-permute-start.18
  44.1 1.4 collective-permute-done.6
  45.5 1.4 collective-permute-start.13
  46.9 2.7 %collective-permute-start.7 = (f32[64,8,128]{2,1,0:T(8,128)S(1)}, f32[64,8,128]{2,1,0:T(8,128)S(1)}, u32[]{:S(2)}, u32[]{:S(2)}) collective-permute-start(f32[64,8,128]{2,1,0:T(8,128)S(1)} %pad_maximum_fusion.5), channel_id=1, source_target_pairs={{64,0},{65,1},{192,128},{193,129},{66,2},{67,3},{194,130},{195,131... | collective-permute-start | bytes 786440 | tf_op jit(solution)/shard_map/ppermute | solution.py:338
  49.6 0.8 collective-permute-done.18
  50.6 2.2 collective-permute-done.13
  52.8 0.9 collective-permute-start.15
  53.7 10.9 %collective-permute-start.14 = (bf16[1,2,4,2,16,640]{5,4,3,2,1,0:T(8,128)(2,1)S(1)}, bf16[1,2,4,2,16,640]{5,4,3,2,1,0:T(8,128)(2,1)S(1)}, u32[]{:S(2)}, u32[]{:S(2)}) collective-permute-start(bf16[1,2,4,2,16,640]{5,4,3,2,1,0:T(8,128)(2,1)S(1)} %collective-permute-done.13), channel_id=1, source_target_pairs={{1,0},{0,1},{129,128},{128,129},{3,2},{2,3},{131,130},{130,131},{5... | collective-permute-start | bytes 983048 | tf_op jit(solution)/shard_map/ppermute | solution.py:338
  65.1 0.8 collective-permute-start.21
  65.9 1.6 collective-permute-start.16
  69.0 1.0 collective-permute-start.17
  70.0 1.0 bitcast_select_fusion
  71.0 7.1 %collective-permute-start = (bf16[3,8192]{1,0:T(4,128)(2,1)S(1)}, bf16[3,8192]{1,0:T(4,128)(2,1)S(1)}, u32[]{:S(2)}, u32[]{:S(2)}) collective-permute-start(bf16[3,8192]{1,0:T(4,128)(2,1)S(1)} %bitcast_select_fusion), channel_id=1, source_target_pairs={{0,1},{1,2},{2,3},{3,4},{4,5},{5,6},{6,7},{7,8},{8,9},{9,10},{10,1... | collective-permute-start | bytes 147464 | tf_op jit(solution)/shard_map/ppermute | solution.py:399
  78.1 1.3 collective-permute-done
  79.4 0.7 concatenate.57.rim_ref
  80.2 1.1 maximum_bitcast_fusion.raw_ref
  81.2 9.9 %convolve.1 = (bf16[256,8192]{1,0:T(8,128)(2,1)}, f32[24,64,128]{2,1,0:T(8,128)}) custom-call(s32[1]{0:T(128)} %bitcast.23.len_ref, bf16[256,8192]{1,0:T(8,128)(2,1)} %bitcast.25, bf16[8,8192]{1,0:T(8,128)(2,1)} %concatenate.57.rim_ref, f32[2048,128]{1,0:T(8,128)} %maximum_bitcast_fusion.raw_ref), custom_call_target="tpu_custom_call" | custom-call | tf_op jit(solution)/shard_map/convolve/pallas_call | solution.py:55
  91.5 0.8 copy-done.4
  92.3 6.1 %collective-permute-start.23 = (bf16[4,2,4,2,16,640]{5,4,3,2,1,0:T(8,128)(2,1)S(1)}, bf16[4,2,4,2,16,640]{5,4,3,2,1,0:T(8,128)(2,1)S(1)}, u32[]{:S(2)}, u32[]{:S(2)}) collective-permute-start(bf16[4,2,4,2,16,640]{5,4,3,2,1,0:T(8,128)(2,1)S(1)} %collective-permute-done.17.refs_1_), channel_id=1, source_target_pairs={{1,0},{0,1},{129,128},{128,129},{3,2},{2,3},{131,130},{130,131},{5... | collective-permute-start | bytes 3932168 | tf_op jit(solution)/shard_map/ppermute | solution.py:338
  98.5 3.5 %collective-permute-done.24.refs_3_ = bf16[4,1,4,2,16,640]{5,4,3,2,1,0:T(8,128)(2,1)S(1)} collective-permute-done((bf16[4,1,4,2,16,640]{5,4,3,2,1,0:T(8,128)(2,1)S(1)}, bf16[4,1,4,2,16,640]{5,4,3,2,1,0:T(8,128)(2,1)S(1)}, u32[]{:S(2)}, u32[]{:S(2)}) %collective-permute-start.24) | collective-permute-done | bytes 655392 | tf_op jit(solution)/shard_map/ppermute | solution.py:338
  101.9 4.1 %collective-permute-start.25 = (bf16[4,1,4,2,16,640]{5,4,3,2,1,0:T(8,128)(2,1)S(1)}, bf16[4,1,4,2,16,640]{5,4,3,2,1,0:T(8,128)(2,1)S(1)}, u32[]{:S(2)}, u32[]{:S(2)}) collective-permute-start(bf16[4,1,4,2,16,640]{5,4,3,2,1,0:T(8,128)(2,1)S(1)} %collective-permute-done.24.refs_3_), channel_id=1, source_target_pairs={{1,0},{0,1},{129,128},{128,129},{3,2},{2,3},{131,130},{130,131},{5... | collective-permute-start | bytes 1966088 | tf_op jit(solution)/shard_map/ppermute | solution.py:338
  106.0 2.6 %collective-permute-start.28 = (bf16[4,1,4,2,16,640]{5,4,3,2,1,0:T(8,128)(2,1)S(1)}, bf16[4,1,4,2,16,640]{5,4,3,2,1,0:T(8,128)(2,1)S(1)}, u32[]{:S(2)}, u32[]{:S(2)}) collective-permute-start(bf16[4,1,4,2,16,640]{5,4,3,2,1,0:T(8,128)(2,1)S(1)} %collective-permute-done.27.refs_8_), channel_id=1, source_target_pairs={{1,0},{0,1},{129,128},{128,129},{3,2},{2,3},{131,130},{130,131},{5... | collective-permute-start | bytes 1966088 | tf_op jit(solution)/shard_map/ppermute | solution.py:338
  109.3 1.1 collective-permute-done.28.refs_9_
  110.4 0.8 copy-done.11
  112.2 56.5 %scan_pass.1 = (f32[256,64,128]{2,1,0:T(8,128)}, f32[256,64,128]{2,1,0:T(8,128)}, f32[32,40,128]{2,1,0:T(8,128)}, f32[4096,128]{1,0:T(8,128)}) custom-call(s32[4]{0:T(128)} %pad_add_fusion.info_ref.len_ref, f32[24,64,128]{2,1,0:T(8,128)} %get-tuple-element.14.par_ref, bf16[256,8192]{1,0:T(8,128)(2,1)} %get-tuple-element.16.act_ref, ...), custom_call_target="tpu_custom_call" | custom-call | tf_op jit(solution)/shard_map/scan_pass/pallas_call | solution.py:208
  168.7 7.0 %all-to-all-start = ((f32[32,40,128]{2,1,0:T(8,128)}), f32[32,40,128]{2,1,0:T(8,128)S(1)}, u32[]{:S(2)}, u32[]{:S(2)}) async-start(f32[32,40,128]{2,1,0:T(8,128)} %get-tuple-element.21), calls=%async_computation | async-start | bytes 1310720 | tf_op jit(solution)/shard_map/all_to_all | solution.py:432
  176.4 19.1 %all-to-all-done.end_ref = f32[32,40,128]{2,1,0:T(8,128)S(1)} async-done(((f32[32,40,128]{2,1,0:T(8,128)}), f32[32,40,128]{2,1,0:T(8,128)S(1)}, u32[]{:S(2)}, u32[]{:S(2)}) %all-to-all-start) | async-done | bytes 655392 | tf_op jit(solution)/shard_map/all_to_all | solution.py:432
  195.4 0.8 copy-done.5
  196.3 2.0 prefix.1
  198.2 22.9 %all_to_all.10.hin_ref = f32[32,32,128]{2,1,0:T(8,128)} all-to-all(f32[32,32,128]{2,1,0:T(8,128)} %prefix.1), channel_id=1, replica_groups=mesh['group'=8,'ctx'=32] {'ctx'}, dimensions={0} | all-to-all | bytes 1048576 | tf_op jit(solution)/shard_map/all_to_all | solution.py:434
  221.2 35.5 %gate_pass.1 = bf16[256,8192]{1,0:T(8,128)(2,1)} custom-call(s32[4]{0:T(128)} %pad_add_fusion.info_ref.len_ref, f32[256,64,128]{2,1,0:T(8,128)} %get-tuple-element.19.y_ref, f32[256,64,128]{2,1,0:T(8,128)} %get-tuple-element.20.cum_ref, f32[32,32,128]{2,1,0:T(8,128)} %all_to_all.10.hin_ref, f32[24,64,128]{2,1,0:T(8,128)} %get-tuple-element.14.par_ref, ...), custom_call_target="tpu_custom_call" | custom-call | tf_op jit(solution)/shard_map/gate_pass/pallas_call | solution.py:300
  (88 shorter events, 5.5 us)
Async XLA Ops:
  2.3 8.8 %collective-permute-start.1 = (f32[1,8,128]{2,1,0:T(8,128)S(1)}, f32[1,8,128]{2,1,0:T(8,128)S(1)}, u32[]{:S(2)}, u32[]{:S(2)}) collective-permute-start(f32[1,8,128]{2,1,0:T(8,128)S(1)} %pad.5), channel_id=1, source_target_pairs={{4,0},{5,1},{132,128},{133,129},{6,2},{7,3},{134,130},{135,131},{0... | collective-permute-start | bytes 12296 | tf_op jit(solution)/shard_map/ppermute | solution.py:338
  11.1 3.5 %collective-permute-start.2 = (f32[2,8,128]{2,1,0:T(8,128)S(1)}, f32[2,8,128]{2,1,0:T(8,128)S(1)}, u32[]{:S(2)}, u32[]{:S(2)}) collective-permute-start(f32[2,8,128]{2,1,0:T(8,128)S(1)} %pad_maximum_fusion.12), channel_id=1, source_target_pairs={{8,0},{9,1},{136,128},{137,129},{10,2},{11,3},{138,130},{139,131},... | collective-permute-start | bytes 24584 | tf_op jit(solution)/shard_map/ppermute | solution.py:338
  13.0 5.7 %collective-permute-start.9 = (bf16[1,32,640]{2,1,0:T(8,128)(2,1)S(1)}, bf16[1,32,640]{2,1,0:T(8,128)(2,1)S(1)}, u32[]{:S(2)}, u32[]{:S(2)}) collective-permute-start(bf16[1,32,640]{2,1,0:T(8,128)(2,1)S(1)} %maximum_bitcast_fusion.1), channel_id=1, source_target_pairs={{128,0},{129,1},{0,128},{1,129},{130,2},{131,3},{2,130},{3,131},{1... | collective-permute-start | bytes 122888 | tf_op jit(solution)/shard_map/ppermute | solution.py:338
  14.5 4.2 %collective-permute-start.3 = (f32[4,8,128]{2,1,0:T(8,128)S(1)}, f32[4,8,128]{2,1,0:T(8,128)S(1)}, u32[]{:S(2)}, u32[]{:S(2)}) collective-permute-start(f32[4,8,128]{2,1,0:T(8,128)S(1)} %pad_maximum_fusion.11), channel_id=1, source_target_pairs={{16,0},{17,1},{144,128},{145,129},{18,2},{19,3},{146,130},{147,131... | collective-permute-start | bytes 49160 | tf_op jit(solution)/shard_map/ppermute | solution.py:338
  19.6 6.3 %collective-permute-start.10 = (bf16[2,32,640]{2,1,0:T(8,128)(2,1)S(1)}, bf16[2,32,640]{2,1,0:T(8,128)(2,1)S(1)}, u32[]{:S(2)}, u32[]{:S(2)}) collective-permute-start(bf16[2,32,640]{2,1,0:T(8,128)(2,1)S(1)} %pad_maximum_fusion.8), channel_id=1, source_target_pairs={{2,0},{3,1},{130,128},{131,129},{0,2},{1,3},{128,130},{129,131},{6... | collective-permute-start | bytes 245768 | tf_op jit(solution)/shard_map/ppermute | solution.py:338
  22.0 8.2 %collective-permute-start.4 = (f32[8,8,128]{2,1,0:T(8,128)S(1)}, f32[8,8,128]{2,1,0:T(8,128)S(1)}, u32[]{:S(2)}, u32[]{:S(2)}) collective-permute-start(f32[8,8,128]{2,1,0:T(8,128)S(1)} %pad_maximum_fusion.10), channel_id=1, source_target_pairs={{1,0},{0,1},{129,128},{128,129},{3,2},{2,3},{131,130},{130,131},{5... | collective-permute-start | bytes 98312 | tf_op jit(solution)/shard_map/ppermute | solution.py:338
  25.9 8.3 %collective-permute-start.11 = (bf16[4,32,640]{2,1,0:T(8,128)(2,1)S(1)}, bf16[4,32,640]{2,1,0:T(8,128)(2,1)S(1)}, u32[]{:S(2)}, u32[]{:S(2)}) collective-permute-start(bf16[4,32,640]{2,1,0:T(8,128)(2,1)S(1)} %pad_maximum_fusion.6), channel_id=1, source_target_pairs={{4,0},{5,1},{132,128},{133,129},{6,2},{7,3},{134,130},{135,131},{0... | collective-permute-start | bytes 491528 | tf_op jit(solution)/shard_map/ppermute | solution.py:338
  30.2 11.3 %collective-permute-start.5 = (f32[16,8,128]{2,1,0:T(8,128)S(1)}, f32[16,8,128]{2,1,0:T(8,128)S(1)}, u32[]{:S(2)}, u32[]{:S(2)}) collective-permute-start(f32[16,8,128]{2,1,0:T(8,128)S(1)} %pad_maximum_fusion.9), channel_id=1, source_target_pairs={{2,0},{3,1},{130,128},{131,129},{0,2},{1,3},{128,130},{129,131},{6... | collective-permute-start | bytes 196616 | tf_op jit(solution)/shard_map/ppermute | solution.py:338
  34.2 8.8 %collective-permute-start.12 = (bf16[8,32,640]{2,1,0:T(8,128)(2,1)S(1)}, bf16[8,32,640]{2,1,0:T(8,128)(2,1)S(1)}, u32[]{:S(2)}, u32[]{:S(2)}) collective-permute-start(bf16[8,32,640]{2,1,0:T(8,128)(2,1)S(1)} %pad_maximum_fusion.4), channel_id=1, source_target_pairs={{1,0},{0,1},{129,128},{128,129},{3,2},{2,3},{131,130},{130,131},{5... | collective-permute-start | bytes 983048 | tf_op jit(solution)/shard_map/ppermute | solution.py:338
  41.6 3.9 %collective-permute-start.6 = (f32[32,8,128]{2,1,0:T(8,128)S(1)}, f32[32,8,128]{2,1,0:T(8,128)S(1)}, u32[]{:S(2)}, u32[]{:S(2)}) collective-permute-start(f32[32,8,128]{2,1,0:T(8,128)S(1)} %pad_maximum_fusion.7), channel_id=1, source_target_pairs={{32,0},{33,1},{160,128},{161,129},{34,2},{35,3},{162,130},{163,131... | collective-permute-start | bytes 393224 | tf_op jit(solution)/shard_map/ppermute | solution.py:338
  43.2 7.2 %collective-permute-start.18 = (bf16[1,2,4,2,16,640]{5,4,3,2,1,0:T(8,128)(2,1)S(1)}, bf16[1,2,4,2,16,640]{5,4,3,2,1,0:T(8,128)(2,1)S(1)}, u32[]{:S(2)}, u32[]{:S(2)}) collective-permute-start(bf16[1,2,4,2,16,640]{5,4,3,2,1,0:T(8,128)(2,1)S(1)} %get-tuple-element.27), channel_id=1, source_target_pairs={{8,0},{25,1},{136,128},{153,129},{10,2},{27,3},{138,130},{155,131}... | collective-permute-start | bytes 983048 | tf_op jit(solution)/shard_map/ppermute | solution.py:338
  45.5 7.3 %collective-permute-start.13 = (bf16[1,2,4,2,16,640]{5,4,3,2,1,0:T(8,128)(2,1)S(1)}, bf16[1,2,4,2,16,640]{5,4,3,2,1,0:T(8,128)(2,1)S(1)}, u32[]{:S(2)}, u32[]{:S(2)}) collective-permute-start(bf16[1,2,4,2,16,640]{5,4,3,2,1,0:T(8,128)(2,1)S(1)} %get-tuple-element.28), channel_id=1, source_target_pairs={{32,0},{97,1},{160,128},{225,129},{34,2},{99,3},{162,130},{227,131... | collective-permute-start | bytes 983048 | tf_op jit(solution)/shard_map/ppermute | solution.py:338
  46.9 17.7 %collective-permute-start.7 = (f32[64,8,128]{2,1,0:T(8,128)S(1)}, f32[64,8,128]{2,1,0:T(8,128)S(1)}, u32[]{:S(2)}, u32[]{:S(2)}) collective-permute-start(f32[64,8,128]{2,1,0:T(8,128)S(1)} %pad_maximum_fusion.5), channel_id=1, source_target_pairs={{64,0},{65,1},{192,128},{193,129},{66,2},{67,3},{194,130},{195,131... | collective-permute-start | bytes 786440 | tf_op jit(solution)/shard_map/ppermute | solution.py:338
  50.5 14.6 %collective-permute-start.20 = (bf16[1,1,4,2,16,640]{5,4,3,2,1,0:T(8,128)(2,1)S(1)}, bf16[1,1,4,2,16,640]{5,4,3,2,1,0:T(8,128)(2,1)S(1)}, u32[]{:S(2)}, u32[]{:S(2)}) collective-permute-start(bf16[1,1,4,2,16,640]{5,4,3,2,1,0:T(8,128)(2,1)S(1)} %slice_select_fusion.2), channel_id=1, source_target_pairs={{8,0},{25,1},{136,128},{153,129},{10,2},{27,3},{138,130},{155,131}... | collective-permute-start | bytes 491528 | tf_op jit(solution)/shard_map/ppermute | solution.py:338
  52.8 13.0 %collective-permute-start.15 = (bf16[1,1,4,2,16,640]{5,4,3,2,1,0:T(8,128)(2,1)S(1)}, bf16[1,1,4,2,16,640]{5,4,3,2,1,0:T(8,128)(2,1)S(1)}, u32[]{:S(2)}, u32[]{:S(2)}) collective-permute-start(bf16[1,1,4,2,16,640]{5,4,3,2,1,0:T(8,128)(2,1)S(1)} %slice_select_fusion.3), channel_id=1, source_target_pairs={{32,0},{97,1},{160,128},{225,129},{34,2},{99,3},{162,130},{227,131... | collective-permute-start | bytes 491528 | tf_op jit(solution)/shard_map/ppermute | solution.py:338
  53.7 13.8 %collective-permute-start.14 = (bf16[1,2,4,2,16,640]{5,4,3,2,1,0:T(8,128)(2,1)S(1)}, bf16[1,2,4,2,16,640]{5,4,3,2,1,0:T(8,128)(2,1)S(1)}, u32[]{:S(2)}, u32[]{:S(2)}) collective-permute-start(bf16[1,2,4,2,16,640]{5,4,3,2,1,0:T(8,128)(2,1)S(1)} %collective-permute-done.13), channel_id=1, source_target_pairs={{1,0},{0,1},{129,128},{128,129},{3,2},{2,3},{131,130},{130,131},{5... | collective-permute-start | bytes 983048 | tf_op jit(solution)/shard_map/ppermute | solution.py:338
  64.6 2.8 %collective-permute-start.19 = (bf16[1,2,4,2,16,640]{5,4,3,2,1,0:T(8,128)(2,1)S(1)}, bf16[1,2,4,2,16,640]{5,4,3,2,1,0:T(8,128)(2,1)S(1)}, u32[]{:S(2)}, u32[]{:S(2)}) collective-permute-start(bf16[1,2,4,2,16,640]{5,4,3,2,1,0:T(8,128)(2,1)S(1)} %collective-permute-done.18), channel_id=1, source_target_pairs={{1,0},{0,1},{129,128},{128,129},{3,2},{2,3},{131,130},{130,131},{5... | collective-permute-start | bytes 983048 | tf_op jit(solution)/shard_map/ppermute | solution.py:338
  64.7 15.3 %collective-permute-start.8 = (f32[128,8,128]{2,1,0:T(8,128)S(1)}, f32[128,8,128]{2,1,0:T(8,128)S(1)}, u32[]{:S(2)}, u32[]{:S(2)}) collective-permute-start(f32[128,8,128]{2,1,0:T(8,128)S(1)} %pad_maximum_fusion.3), channel_id=1, source_target_pairs={{128,0},{129,1},{0,128},{1,129},{130,2},{131,3},{2,130},{3,131},{1... | collective-permute-start | bytes 1572872 | tf_op jit(solution)/shard_map/ppermute | solution.py:338
  65.1 2.5 collective-permute-start.21
  65.9 2.6 %collective-permute-start.16 = (bf16[1,1,4,2,16,640]{5,4,3,2,1,0:T(8,128)(2,1)S(1)}, bf16[1,1,4,2,16,640]{5,4,3,2,1,0:T(8,128)(2,1)S(1)}, u32[]{:S(2)}, u32[]{:S(2)}) collective-permute-start(bf16[1,1,4,2,16,640]{5,4,3,2,1,0:T(8,128)(2,1)S(1)} %collective-permute-done.15), channel_id=1, source_target_pairs={{1,0},{0,1},{129,128},{128,129},{3,2},{2,3},{131,130},{130,131},{5... | collective-permute-start | bytes 491528 | tf_op jit(solution)/shard_map/ppermute | solution.py:338
  67.9 1.1 copy-start.1
  67.9 23.2 %collective-permute-start.22 = (bf16[4,2,4,2,16,640]{5,4,3,2,1,0:T(8,128)(2,1)S(1)}, bf16[4,2,4,2,16,640]{5,4,3,2,1,0:T(8,128)(2,1)S(1)}, u32[]{:S(2)}, u32[]{:S(2)}) collective-permute-start(bf16[4,2,4,2,16,640]{5,4,3,2,1,0:T(8,128)(2,1)S(1)} %pad_maximum_fusion.1.refs_5_), channel_id=1, source_target_pairs={{32,0},{97,1},{160,128},{225,129},{34,2},{99,3},{162,130},{227,131... | collective-permute-start | bytes 3932168 | tf_op jit(solution)/shard_map/ppermute | solution.py:338
  69.0 12.3 %copy-start.3 = (bf16[4,2,4,2,16,640]{5,4,3,2,1,0:T(8,128)(2,1)}, bf16[4,2,4,2,16,640]{5,4,3,2,1,0:T(8,128)(2,1)S(1)}, u32[]{:S(2)}) copy-start(bf16[4,2,4,2,16,640]{5,4,3,2,1,0:T(8,128)(2,1)S(1)} %pad_maximum_fusion.refs_0_) | copy-start | bytes 3932164
  69.0 22.1 %collective-permute-start.17 = (bf16[4,2,4,2,16,640]{5,4,3,2,1,0:T(8,128)(2,1)S(1)}, bf16[4,2,4,2,16,640]{5,4,3,2,1,0:T(8,128)(2,1)S(1)}, u32[]{:S(2)}, u32[]{:S(2)}) collective-permute-start(bf16[4,2,4,2,16,640]{5,4,3,2,1,0:T(8,128)(2,1)S(1)} %pad_maximum_fusion.refs_0_), channel_id=1, source_target_pairs={{8,0},{25,1},{136,128},{153,129},{10,2},{27,3},{138,130},{155,131}... | collective-permute-start | bytes 3932168 | tf_op jit(solution)/shard_map/ppermute | solution.py:338
  71.0 8.4 %collective-permute-start = (bf16[3,8192]{1,0:T(4,128)(2,1)S(1)}, bf16[3,8192]{1,0:T(4,128)(2,1)S(1)}, u32[]{:S(2)}, u32[]{:S(2)}) collective-permute-start(bf16[3,8192]{1,0:T(4,128)(2,1)S(1)} %bitcast_select_fusion), channel_id=1, source_target_pairs={{0,1},{1,2},{2,3},{3,4},{4,5},{5,6},{6,7},{7,8},{8,9},{9,10},{10,1... | collective-permute-start | bytes 147464 | tf_op jit(solution)/shard_map/ppermute | solution.py:399
  91.1 7.3 %copy-start.2 = (bf16[4,2,4,2,16,640]{5,4,3,2,1,0:T(8,128)(2,1)}, bf16[4,2,4,2,16,640]{5,4,3,2,1,0:T(8,128)(2,1)S(1)}, u32[]{:S(2)}) copy-start(bf16[4,2,4,2,16,640]{5,4,3,2,1,0:T(8,128)(2,1)S(1)} %collective-permute-done.22.refs_6_) | copy-start | bytes 3932164
  91.1 1.2 copy-start.4
  91.2 10.7 %collective-permute-start.24 = (bf16[4,1,4,2,16,640]{5,4,3,2,1,0:T(8,128)(2,1)S(1)}, bf16[4,1,4,2,16,640]{5,4,3,2,1,0:T(8,128)(2,1)S(1)}, u32[]{:S(2)}, u32[]{:S(2)}) collective-permute-start(bf16[4,1,4,2,16,640]{5,4,3,2,1,0:T(8,128)(2,1)S(1)} %slice_select_fusion.1), channel_id=1, source_target_pairs={{8,0},{25,1},{136,128},{153,129},{10,2},{27,3},{138,130},{155,131}... | collective-permute-start | bytes 1966088 | tf_op jit(solution)/shard_map/ppermute | solution.py:338
  91.4 14.6 %collective-permute-start.27 = (bf16[4,1,4,2,16,640]{5,4,3,2,1,0:T(8,128)(2,1)S(1)}, bf16[4,1,4,2,16,640]{5,4,3,2,1,0:T(8,128)(2,1)S(1)}, u32[]{:S(2)}, u32[]{:S(2)}) collective-permute-start(bf16[4,1,4,2,16,640]{5,4,3,2,1,0:T(8,128)(2,1)S(1)} %slice_select_fusion), channel_id=1, source_target_pairs={{32,0},{97,1},{160,128},{225,129},{34,2},{99,3},{162,130},{227,131... | collective-permute-start | bytes 1966088 | tf_op jit(solution)/shard_map/ppermute | solution.py:338
  92.3 18.1 %collective-permute-start.23 = (bf16[4,2,4,2,16,640]{5,4,3,2,1,0:T(8,128)(2,1)S(1)}, bf16[4,2,4,2,16,640]{5,4,3,2,1,0:T(8,128)(2,1)S(1)}, u32[]{:S(2)}, u32[]{:S(2)}) collective-permute-start(bf16[4,2,4,2,16,640]{5,4,3,2,1,0:T(8,128)(2,1)S(1)} %collective-permute-done.17.refs_1_), channel_id=1, source_target_pairs={{1,0},{0,1},{129,128},{128,129},{3,2},{2,3},{131,130},{130,131},{5... | collective-permute-start | bytes 3932168 | tf_op jit(solution)/shard_map/ppermute | solution.py:338
  98.4 12.0 %collective-permute-start.26 = (bf16[4,2,4,2,16,640]{5,4,3,2,1,0:T(8,128)(2,1)S(1)}, bf16[4,2,4,2,16,640]{5,4,3,2,1,0:T(8,128)(2,1)S(1)}, u32[]{:S(2)}, u32[]{:S(2)}) collective-permute-start(bf16[4,2,4,2,16,640]{5,4,3,2,1,0:T(8,128)(2,1)S(1)} %collective-permute-done.22.refs_6_), channel_id=1, source_target_pairs={{1,0},{0,1},{129,128},{128,129},{3,2},{2,3},{131,130},{130,131},{5... | collective-permute-start | bytes 3932168 | tf_op jit(solution)/shard_map/ppermute | solution.py:338
  101.9 8.5 %copy-start.8 = (bf16[4,1,4,2,16,640]{5,4,3,2,1,0:T(8,128)(2,1)}, bf16[4,1,4,2,16,640]{5,4,3,2,1,0:T(8,128)(2,1)S(1)}, u32[]{:S(2)}) copy-start(bf16[4,1,4,2,16,640]{5,4,3,2,1,0:T(8,128)(2,1)S(1)} %collective-permute-done.24.refs_3_) | copy-start | bytes 1966084
  101.9 7.3 %collective-permute-start.25 = (bf16[4,1,4,2,16,640]{5,4,3,2,1,0:T(8,128)(2,1)S(1)}, bf16[4,1,4,2,16,640]{5,4,3,2,1,0:T(8,128)(2,1)S(1)}, u32[]{:S(2)}, u32[]{:S(2)}) collective-permute-start(bf16[4,1,4,2,16,640]{5,4,3,2,1,0:T(8,128)(2,1)S(1)} %collective-permute-done.24.refs_3_), channel_id=1, source_target_pairs={{1,0},{0,1},{129,128},{128,129},{3,2},{2,3},{131,130},{130,131},{5... | collective-permute-start | bytes 1966088 | tf_op jit(solution)/shard_map/ppermute | solution.py:338
  106.0 4.4 %copy-start.9 = (bf16[4,1,4,2,16,640]{5,4,3,2,1,0:T(8,128)(2,1)}, bf16[4,1,4,2,16,640]{5,4,3,2,1,0:T(8,128)(2,1)S(1)}, u32[]{:S(2)}) copy-start(bf16[4,1,4,2,16,640]{5,4,3,2,1,0:T(8,128)(2,1)S(1)} %collective-permute-done.27.refs_8_) | copy-start | bytes 1966084
  106.0 4.4 %collective-permute-start.28 = (bf16[4,1,4,2,16,640]{5,4,3,2,1,0:T(8,128)(2,1)S(1)}, bf16[4,1,4,2,16,640]{5,4,3,2,1,0:T(8,128)(2,1)S(1)}, u32[]{:S(2)}, u32[]{:S(2)}) collective-permute-start(bf16[4,1,4,2,16,640]{5,4,3,2,1,0:T(8,128)(2,1)S(1)} %collective-permute-done.27.refs_8_), channel_id=1, source_target_pairs={{1,0},{0,1},{129,128},{128,129},{3,2},{2,3},{131,130},{130,131},{5... | collective-permute-start | bytes 1966088 | tf_op jit(solution)/shard_map/ppermute | solution.py:338
  109.2 1.2 copy-start.10
  110.4 0.9 copy-start.11
  110.4 1.2 copy-start.6
  110.4 1.8 copy-start.7
  168.7 7.0 %copy-start = (f32[24,64,128]{2,1,0:T(8,128)S(1)}, f32[24,64,128]{2,1,0:T(8,128)}, u32[]{:S(2)}) copy-start(f32[24,64,128]{2,1,0:T(8,128)} %get-tuple-element.14.par_ref) | copy-start | bytes 2359300
  168.7 26.7 %all-to-all-start = ((f32[32,40,128]{2,1,0:T(8,128)}), f32[32,40,128]{2,1,0:T(8,128)S(1)}, u32[]{:S(2)}, u32[]{:S(2)}) async-start(f32[32,40,128]{2,1,0:T(8,128)} %get-tuple-element.21), calls=%async_computation | async-start | bytes 1310720 | tf_op jit(solution)/shard_map/all_to_all | solution.py:432
  195.4 0.8 copy-start.5

commit v3 on v2

--- a/solution.py
+++ b/solution.py
@@ -26,52 +26,6 @@
 
 def per_step(count):
     return pl.BlockSpec((count, ROWS, LANES), lambda i, *_: (0, i, 0))
-
-
-def conv_kernel(len_ref, x_ref, rim_ref, raw_ref, act_ref, par_ref, pad_ref):
-    tok, width = x_ref.shape
-    quarter = LANES // 4
-    spot = lax.broadcasted_iota(jnp.int32, (ROWS, LANES), 1) // quarter
-    for r in range(par_ref.shape[0] // 4):
-        rows = [raw_ref[pl.ds(q * 64 + r, ROWS, stride=8), :] for q in range(4)]
-        for j in range(4):
-            turned = [rows[q] if q == j else pltpu.roll(rows[q], ((q - j) % 4) * quarter, 1) for q in range(4)]
-            low = jnp.where(spot == 0, turned[0], turned[1])
-            high = jnp.where(spot == 2, turned[2], turned[3])
-            par_ref[4 * r + j] = jnp.where(spot < 2, low, high)
-    keep = lax.broadcasted_iota(jnp.int32, (tok, LANES), 0) < len_ref[0]
-    for g in range(width // LANES):
-        cols = slice(g * LANES, (g + 1) * LANES)
-        pad_ref[0:8, :] = rim_ref[:, cols].astype(jnp.float32)
-        pad_ref[8 : 8 + tok, :] = jnp.where(keep, x_ref[:, cols].astype(jnp.float32), 0.0)
-        total = par_ref[4, g : g + 1, :] + par_ref[0, g : g + 1, :] * pad_ref[5 : 5 + tok, :]
-        for k in range(1, 4):
-            total = total + par_ref[k, g : g + 1, :] * pad_ref[5 + k : 5 + k + tok, :]
-        act_ref[:, cols] = (total * sigmoid(total)).astype(jnp.bfloat16)
-
-
-def convolve(length, x, rim, raw, count):
-    tok, chans = x.shape
-    return pl.pallas_call(
-        conv_kernel,
-        grid_spec=pltpu.PrefetchScalarGridSpec(
-            num_scalar_prefetch=1,
-            grid=(chans // WIDE,),
-            in_specs=[
-                pl.BlockSpec((tok, WIDE), lambda i, *_: (0, i)),
-                pl.BlockSpec((8, WIDE), lambda i, *_: (0, i)),
-                pl.BlockSpec((256, LANES), lambda i, *_: (i, 0)),
-            ],
-            out_specs=[pl.BlockSpec((tok, WIDE), lambda i, *_: (0, i)), per_step(count)],
-            scratch_shapes=[pltpu.VMEM((tok + 8, LANES), jnp.float32)],
-        ),
-        out_shape=[
-            jax.ShapeDtypeStruct((tok, chans), jnp.bfloat16),
-            jax.ShapeDtypeStruct((count, chans // LANES, LANES), jnp.float32),
-        ],
-        compiler_params=settings(),
-        name="convolve",
-    )(length, x, rim, raw)
 
 
 def piece_specs(pieces):
@@ -110,19 +64,41 @@
                         w_ref[(own_x + q) & 3, h, first + core, half : 2 * half, :] = ref[q, core, h, 0]
 
 
-def scan_kernel(info_ref, par_ref, act_ref, *refs):
-    *piece_refs, y_ref, cum_ref, end_ref, c_ref, sum_scr, low_scr, b_scr, act_scr, d_scr, x_scr, a_scr, w_scr = refs
+def scan_kernel(info_ref, x_ref, rim_ref, *refs):
+    *piece_refs, act_ref, par_ref, y_ref, cum_ref, end_ref, c_ref = refs[:-10]
+    sum_scr, low_scr, b_scr, act_scr, par_scr, pad_scr, d_scr, x_scr, a_scr, w_scr = refs[-10:]
     step = pl.program_id(0)
     many = act_scr.shape[0]
     tok, rank = low_scr.shape
     states = a_scr.shape[0]
+    keep = lax.broadcasted_iota(jnp.int32, (tok, LANES), 0) < info_ref[0]
 
     @pl.when(step < many)
     def _():
         assemble(step, info_ref, piece_refs, w_scr.at[step])
+        count = par_scr.shape[1] // ROWS
+        after = rank + 2 * states
+        for g in range(ROWS):
+            cols = slice(g * LANES, (g + 1) * LANES)
+            beside = w_scr[step, g // 2, 2 * (g % 2) : 2 * (g % 2) + 2].reshape(LANES, w_scr.shape[-1])
+            beside = beside[:, after - after % LANES : after - after % LANES + LANES].astype(jnp.float32).T
+            at = after % LANES
+            parts = [beside[at + k * count : at + (k + 1) * count] for k in range(3)]
+            vectors = (parts[0] + parts[1]) + parts[2]
+            par_scr[step, pl.ds(g, count, stride=ROWS), :] = vectors
+            par_ref[:, g, :] = vectors
+            pad = jnp.concatenate(
+                [rim_ref[:, cols].astype(jnp.float32), jnp.where(keep, x_ref[:, cols].astype(jnp.float32), 0.0)], axis=0
+            )
+            pad_scr[g % 2] = pad
+            total = vectors[4:5] + vectors[0:1] * pad_scr[g % 2, 5 : 5 + tok, :]
+            for k in range(1, 4):
+                total = total + vectors[k : k + 1] * pad_scr[g % 2, 5 + k : 5 + k + tok, :]
+            act = (total * sigmoid(total)).astype(jnp.bfloat16)
+            act_ref[:, cols] = act
+            act_scr[step, :, cols] = act
         weight = w_scr[step].reshape(WIDE, w_scr.shape[-1])[:, : sum_scr.shape[1]]
-        act_scr[step] = act_ref[...]
-        part = jnp.dot(act_ref[...], weight, preferred_element_type=jnp.float32)
+        part = jnp.dot(act_scr[step], weight, preferred_element_type=jnp.float32)
 
         @pl.when(step == 0)
         def _():
@@ -142,7 +118,6 @@
     @pl.when(step >= many)
     def _():
         at = step - many
-        keep = lax.broadcasted_iota(jnp.int32, (tok, LANES), 0) < info_ref[0]
         raw = lax.dot_general(
             low_scr[...],
             w_scr[at].reshape(WIDE, w_scr.shape[-1])[:, w_scr.shape[-1] - rank :],
@@ -151,14 +126,16 @@
         )
         for g in range(ROWS):
             cols = slice(g * LANES, (g + 1) * LANES)
-            v = raw[:, cols] + par_ref[5, g : g + 1, :]
+            v = raw[:, cols] + par_scr[at, 5 * ROWS + g : 5 * ROWS + g + 1, :]
             soft = jnp.maximum(v, 0.0) + jnp.log1p(jnp.exp(-jnp.abs(v)))
             d = jnp.where(keep, soft, 0.0)
             place = slice(g * 8, (g + 1) * 8)
             d_scr[:, place, :] = d.reshape(tok // 8, 8, LANES)
             dx = d * act_scr[at, :, cols].astype(jnp.float32)
             x_scr[:, place, :] = dx.reshape(tok // 8, 8, LANES)
-        a_scr[...] = jnp.exp(par_ref[VECTORS : VECTORS + states]) * (-LOG2E)
+        for n in range(states):
+            row = (VECTORS + n) * ROWS
+            a_scr[n] = jnp.exp(par_scr[at, row : row + ROWS, :]) * (-LOG2E)
 
         def block(i, carry):
             hs, cum = carry
@@ -191,8 +168,8 @@
                 end_ref[q, row : row + 2, :] = cum[pair]
 
 
-def scan_pass(info, pars, act, pieces, rank, states):
-    tok, chans = act.shape
+def scan_pass(info, x, rim, pieces, rank, states, count):
+    tok, chans = x.shape
     rows, cols = pieces[0].shape[4:]
     many = chans // WIDE
     groups = chans // LANES
@@ -211,11 +188,13 @@
             num_scalar_prefetch=1,
             grid=(2 * many,),
             in_specs=[
-                turn((pars.shape[0], ROWS, LANES), 1),
                 pl.BlockSpec((tok, WIDE), lambda i, s: (0, jnp.minimum(i, many - 1))),
+                pl.BlockSpec((8, WIDE), lambda i, s: (0, jnp.minimum(i, many - 1))),
                 *piece_specs(pieces),
             ],
             out_specs=[
+                pl.BlockSpec((tok, WIDE), lambda i, s: (0, jnp.minimum(i, many - 1))),
+                pl.BlockSpec((count, ROWS, LANES), lambda i, s: (0, jnp.minimum(i, many - 1), 0)),
                 turn((tok, ROWS, LANES), 1),
                 turn((tok, ROWS, LANES), 1),
                 turn((ROWS // 2, sent, LANES), 0),
@@ -226,6 +205,8 @@
                 pltpu.VMEM((tok, rank), jnp.bfloat16),
                 pltpu.VMEM((tok * states, LANES), jnp.float32),
                 pltpu.VMEM((many, tok, WIDE), jnp.bfloat16),
+                pltpu.VMEM((many, count * ROWS, LANES), jnp.float32),
+                pltpu.VMEM((2, tok + 8, LANES), jnp.float32),
                 pltpu.VMEM((tok // 8, 8 * ROWS, LANES), jnp.float32),
                 pltpu.VMEM((tok // 8, 8 * ROWS, LANES), jnp.float32),
                 pltpu.VMEM((states, ROWS, LANES), jnp.float32),
@@ -233,6 +214,8 @@
             ],
         ),
         out_shape=[
+            jax.ShapeDtypeStruct((tok, chans), jnp.bfloat16),
+            jax.ShapeDtypeStruct((count, groups, LANES), jnp.float32),
             jax.ShapeDtypeStruct((tok, groups, LANES), jnp.float32),
             jax.ShapeDtypeStruct((tok, groups, LANES), jnp.float32),
             jax.ShapeDtypeStruct((groups // 2, sent, LANES), jnp.float32),
@@ -240,7 +223,7 @@
         ],
         compiler_params=settings(),
         name="scan_pass",
-    )(info, pars, act, *pieces)
+    )(info, x, rim, *pieces)
 
 
 def prefix_kernel(end_ref, alog_ref, in_ref):
@@ -399,35 +382,27 @@
     rim = lax.ppermute(edge, "ctx", [(i, i + 1) for i in range(blocks - 1)])
     rim = jnp.concatenate([jnp.zeros((8 - (taps - 1), chans), x.dtype), rim], axis=0)
 
-    small = jnp.concatenate(
-        [conv_weight, conv_bias[None], dt_bias[None], skip_gain[None], a_log, a_log[:1]], axis=0
-    )
-    width = small.shape[1]
-    count = small.shape[0]
-    small = small.reshape(1, count // 4, 4 * width)
-    small = jnp.pad(small, ((0, 0), (0, 8 - count // 4), (0, 0)))
-    for axis, bit in (("z", 4), ("x", 1), ("x", 2), ("core", 1), ("z", 2), ("y", 1), ("y", 2), ("z", 1)):
-        small = double(small, axis, bit, own[axis])
-    small = small.reshape(-1, LANES)
-
-    fill = -(xproj_weight.shape[1] + rank) % LANES
-    mats = jnp.concatenate(
-        [xproj_weight, jnp.zeros((width, fill), xproj_weight.dtype), dtproj_weight.T], axis=1
-    )[None]
+    small = jnp.concatenate([conv_weight, conv_bias[None], dt_bias[None], skip_gain[None], a_log, a_log[:1]], axis=0).T
+    width, count = small.shape
+    high = lax.reduce_precision(small, 8, 7)
+    middle = lax.reduce_precision(small - high, 8, 7)
+    last = (small - high) - middle
+    parts = [v.astype(jnp.bfloat16) for v in (high, middle, last)]
+    fill = -(xproj_weight.shape[1] + 3 * count + rank) % LANES
+    parts += [jnp.zeros((width, fill), jnp.bfloat16), dtproj_weight.T]
+    mats = jnp.concatenate([xproj_weight, *parts], axis=1)[None]
     for axis, bit in (("z", 1), ("z", 2), ("z", 4), ("core", 1)):
         mats = double(mats, axis, bit, own[axis])
     mats = mats.reshape(1, 2, 4, 2, *mats.shape[1:])
     upper = row_of_four(mats[..., : width // 2, :], "y", own_core)
     lower = row_of_four(mats[..., width // 2 :, :], "x", own_core)
-    near_x, near_y = fetch(upper, onward("x")), fetch(lower, onward("y"))
-    act, pars = convolve(length, x, rim, small, count)
-    near_x, near_y, act = lax.optimization_barrier((near_x, near_y, act))
     pieces = []
-    for value, near, axis in ((upper, near_x, "x"), (lower, near_y, "y")):
+    for value, axis in ((upper, "x"), (lower, "y")):
+        near = fetch(value, onward(axis))
         far = farther(near, axis, own_core)
         pieces += [value, near, swap(near), far, swap(far)]
 
-    y, cum, ends, c_wide = scan_pass(info, pars, act, pieces, rank, states)
+    act, pars, y, cum, ends, c_wide = scan_pass(info, x, rim, pieces, rank, states, count)
     mine = lax.dynamic_slice_in_dim(pars[VECTORS : VECTORS + states], 2 * ctx, 2, axis=1).reshape(2 * states, LANES)
     ends = lax.all_to_all(ends, "ctx", split_axis=0, concat_axis=0, tiled=True)
     hin = prefix(ends, mine)

time: 258 us -> 244 us (0.946)
  starting transfers between devices: 80.7 us -> 49.9 us
  waiting for transfers between devices: 35.2 us -> 59.3 us
  Pallas kernels: 104 us -> 98.9 us
    ppermute x28 -> x20, starting transfers between devices: 66.7 us -> 36.2 us  [fetch(): return lax.ppermute(value, ('group', 'ctx'), route)]
    ppermute x28 -> x20, waiting for transfers between devices: 14.8 us -> 38.6 us  [fetch(): return lax.ppermute(value, ('group', 'ctx'), route)]
    pallas_call x1 -> x0, Pallas kernels: 9.87 us -> none  [convolve(): pl.pallas_call(conv_kernel, grid_spec=pltpu.PrefetchScalarGridSpec(num_sc...]
    ppermute x1, starting transfers between devices: 7.06 us -> 1.92 us  [shards(): rim = lax.ppermute(edge, 'ctx', [(i, i + 1) for i in range(blocks - 1)])]
    pallas_call x1, Pallas kernels: 56.5 us -> 61.4 us  [scan_pass(): pl.pallas_call(scan_kernel, grid_spec=pltpu.PrefetchScalarGridSpec(num_sc...]
    all_to_all x1, starting transfers between devices: 6.96 us -> 11.8 us  [shards(): ends = lax.all_to_all(ends, 'ctx', split_axis=0, concat_axis=0, tiled=True)]
  transfers between devices with their start and end apart: 30 -> 22, of which waited for: 11 -> 14; matrix products, arithmetic and copies ran while one was open for 2% -> 2% of each run, Pallas kernels for 4% -> 0%
where the time goes in v3:
time: 244 us; the launch traced here: 243 us
  Pallas kernels  98.9 us (41%)
  waiting for transfers between devices  59.3 us (24%)
  starting transfers between devices  49.9 us (20%)
  blocking collectives  22.8 us (9%)
  local copies, waits for them, and re-layouts  7.3 us (3%)
  other arithmetic  4.05 us (2%)
    pallas_call x1, Pallas kernels, scan_pass(): pl.pallas_call(scan_kernel, grid_spec=pltpu.PrefetchScalarGridSpec(num_sc...  61.4 us
    ppermute x20, waiting for transfers between devices, fetch(): return lax.ppermute(value, ('group', 'ctx'), route)  38.6 us
    ppermute x20, starting transfers between devices, fetch(): return lax.ppermute(value, ('group', 'ctx'), route)  36.2 us
    pallas_call x1, Pallas kernels, gate_pass(): pl.pallas_call(gate_kernel, grid_spec=pltpu.PrefetchScalarGridSpec(num_sc...  35.5 us
    all_to_all x1, blocking collectives, shards(): hin = lax.all_to_all(hin, 'ctx', split_axis=0, concat_axis=0, tiled=True)  22.8 us
    all_to_all x1, waiting for transfers between devices, shards(): ends = lax.all_to_all(ends, 'ctx', split_axis=0, concat_axis=0, tiled=True)  20 us
    all_to_all x1, starting transfers between devices, shards(): ends = lax.all_to_all(ends, 'ctx', split_axis=0, concat_axis=0, tiled=True)  11.8 us
  transfers between devices with their start and end apart: 22, of which 14 were waited for; matrix products, arithmetic and copies ran while one was open for 2% of the time, Pallas kernels for 0%

profile of v3, /device:TPU:1, one launch (start us, length us, event | category | flops | bytes accessed | tf_op | source)
XLA Modules:
  0.0 243.1 jit_solution(13745911670768860972)
XLA Ops:
  0.0 0.7 slice.44
  0.7 1.5 concatenate.34
  2.5 0.8 concatenate.35
  3.3 2.5 %collective-permute-start.1 = (bf16[1,32,640]{2,1,0:T(8,128)(2,1)S(1)}, bf16[1,32,640]{2,1,0:T(8,128)(2,1)S(1)}, u32[]{:S(2)}, u32[]{:S(2)}) collective-permute-start(bf16[1,32,640]{2,1,0:T(8,128)(2,1)S(1)} %bitcast.31), channel_id=1, source_target_pairs={{128,0},{129,1},{0,128},{1,129},{130,2},{131,3},{2,130},{3,131},{1... | collective-permute-start | bytes 122888 | tf_op jit(solution)/shard_map/ppermute | solution.py:321
  5.9 1.4 collective-permute-done.1
  7.3 3.1 %collective-permute-start.2 = (bf16[2,32,640]{2,1,0:T(8,128)(2,1)S(1)}, bf16[2,32,640]{2,1,0:T(8,128)(2,1)S(1)}, u32[]{:S(2)}, u32[]{:S(2)}) collective-permute-start(bf16[2,32,640]{2,1,0:T(8,128)(2,1)S(1)} %pad_maximum_fusion.5), channel_id=1, source_target_pairs={{2,0},{3,1},{130,128},{131,129},{0,2},{1,3},{128,130},{129,131},{6... | collective-permute-start | bytes 245768 | tf_op jit(solution)/shard_map/ppermute | solution.py:321
  10.4 1.8 collective-permute-done.2
  12.3 7.1 %collective-permute-start.3 = (bf16[4,32,640]{2,1,0:T(8,128)(2,1)S(1)}, bf16[4,32,640]{2,1,0:T(8,128)(2,1)S(1)}, u32[]{:S(2)}, u32[]{:S(2)}) collective-permute-start(bf16[4,32,640]{2,1,0:T(8,128)(2,1)S(1)} %pad_maximum_fusion.4), channel_id=1, source_target_pairs={{4,0},{5,1},{132,128},{133,129},{6,2},{7,3},{134,130},{135,131},{0... | collective-permute-start | bytes 491528 | tf_op jit(solution)/shard_map/ppermute | solution.py:321
  19.3 2.7 %collective-permute-done.3 = bf16[4,32,640]{2,1,0:T(8,128)(2,1)S(1)} collective-permute-done((bf16[4,32,640]{2,1,0:T(8,128)(2,1)S(1)}, bf16[4,32,640]{2,1,0:T(8,128)(2,1)S(1)}, u32[]{:S(2)}, u32[]{:S(2)}) %collective-permute-start.3) | collective-permute-done | bytes 163872 | tf_op jit(solution)/shard_map/ppermute | solution.py:321
  22.1 6.0 %collective-permute-start.4 = (bf16[8,32,640]{2,1,0:T(8,128)(2,1)S(1)}, bf16[8,32,640]{2,1,0:T(8,128)(2,1)S(1)}, u32[]{:S(2)}, u32[]{:S(2)}) collective-permute-start(bf16[8,32,640]{2,1,0:T(8,128)(2,1)S(1)} %pad_maximum_fusion.3), channel_id=1, source_target_pairs={{1,0},{0,1},{129,128},{128,129},{3,2},{2,3},{131,130},{130,131},{5... | collective-permute-start | bytes 983048 | tf_op jit(solution)/shard_map/ppermute | solution.py:321
  28.1 1.3 collective-permute-done.4
  29.6 1.1 collective-permute-start.13
  30.7 1.3 collective-permute-start.5
  32.0 4.8 %collective-permute-done.13 = bf16[1,2,4,2,16,640]{5,4,3,2,1,0:T(8,128)(2,1)S(1)} collective-permute-done((bf16[1,2,4,2,16,640]{5,4,3,2,1,0:T(8,128)(2,1)S(1)}, bf16[1,2,4,2,16,640]{5,4,3,2,1,0:T(8,128)(2,1)S(1)}, u32[]{:S(2)}, u32[]{:S(2)}) %collective-permute-start.13) | collective-permute-done | bytes 327712 | tf_op jit(solution)/shard_map/ppermute | solution.py:321
  36.8 0.2 collective-permute-start.15
  37.0 0.9 collective-permute-done.5
  37.9 3.1 %collective-permute-start.6 = (bf16[1,2,4,2,16,640]{5,4,3,2,1,0:T(8,128)(2,1)S(1)}, bf16[1,2,4,2,16,640]{5,4,3,2,1,0:T(8,128)(2,1)S(1)}, u32[]{:S(2)}, u32[]{:S(2)}) collective-permute-start(bf16[1,2,4,2,16,640]{5,4,3,2,1,0:T(8,128)(2,1)S(1)} %collective-permute-done.5), channel_id=1, source_target_pairs={{1,0},{0,1},{129,128},{128,129},{3,2},{2,3},{131,130},{130,131},{5... | collective-permute-start | bytes 983048 | tf_op jit(solution)/shard_map/ppermute | solution.py:321
  41.0 1.4 collective-permute-start.7
  42.4 1.7 collective-permute-start.14
  44.1 2.4 collective-permute-done.7
  46.6 0.4 collective-permute-start.8
  47.0 1.0 collective-permute-done.8
  48.0 0.2 pad_maximum_fusion.refs_0_
  48.5 0.2 pad_maximum_fusion.1.refs_5_
  48.7 0.6 copy-done
  49.3 0.8 collective-permute-start.17
  50.1 15.9 %collective-permute-done.9.refs_1_ = bf16[4,2,4,2,16,640]{5,4,3,2,1,0:T(8,128)(2,1)S(1)} collective-permute-done((bf16[4,2,4,2,16,640]{5,4,3,2,1,0:T(8,128)(2,1)S(1)}, bf16[4,2,4,2,16,640]{5,4,3,2,1,0:T(8,128)(2,1)S(1)}, u32[]{:S(2)}, u32[]{:S(2)}) %collective-permute-start.9) | collective-permute-done | bytes 1310752 | tf_op jit(solution)/shard_map/ppermute | solution.py:321
  66.2 1.6 collective-permute-done.17.refs_6_
  67.8 1.4 slice_select_fusion
  70.0 4.9 %collective-permute-start.10 = (bf16[4,2,4,2,16,640]{5,4,3,2,1,0:T(8,128)(2,1)S(1)}, bf16[4,2,4,2,16,640]{5,4,3,2,1,0:T(8,128)(2,1)S(1)}, u32[]{:S(2)}, u32[]{:S(2)}) collective-permute-start(bf16[4,2,4,2,16,640]{5,4,3,2,1,0:T(8,128)(2,1)S(1)} %collective-permute-done.9.refs_1_), channel_id=1, source_target_pairs={{1,0},{0,1},{129,128},{128,129},{3,2},{2,3},{131,130},{130,131},{5... | collective-permute-start | bytes 3932168 | tf_op jit(solution)/shard_map/ppermute | solution.py:321
  75.0 1.8 collective-permute-done.11.refs_3_
  76.8 0.2 collective-permute-start.12
  77.1 3.0 %collective-permute-done.19.refs_8_ = bf16[4,1,4,2,16,640]{5,4,3,2,1,0:T(8,128)(2,1)} collective-permute-done((bf16[4,1,4,2,16,640]{5,4,3,2,1,0:T(8,128)(2,1)S(1)}, bf16[4,1,4,2,16,640]{5,4,3,2,1,0:T(8,128)(2,1)}, u32[]{:S(2)}, u32[]{:S(2)}) %collective-permute-start.19) | collective-permute-done | bytes 655392 | tf_op jit(solution)/shard_map/ppermute | solution.py:321
  80.0 2.0 collective-permute-start.20
  82.0 1.0 bitcast_select_fusion
  83.0 1.9 collective-permute-start
  85.0 0.7 pad_add_fusion.info_ref.len_ref
  85.6 0.6 collective-permute-done
  86.3 0.7 concatenate.33.rim_ref
  87.0 1.1 copy-done.5
  88.1 61.4 %scan_pass.1 = (bf16[256,8192]{1,0:T(8,128)(2,1)}, f32[24,64,128]{2,1,0:T(8,128)}, f32[256,64,128]{2,1,0:T(8,128)}, f32[256,64,128]{2,1,0:T(8,128)}, f32[32,40,128]{2,1,0:T(8,128)}, /*index=5*/f32[4096,128]{1,0:T(8,128)}) custom-call(s32[4]{0:T(128)} %pad_add_fusion.info_ref.len_ref, bf16[256,8192]{1,0:T(8,128)(2,1)} %bitcast.28, ...), custom_call_target="tpu_custom_call" | custom-call | tf_op jit(solution)/shard_map/scan_pass/pallas_call | solution.py:185
  149.5 11.8 %all-to-all-start = ((f32[32,40,128]{2,1,0:T(8,128)}), f32[32,40,128]{2,1,0:T(8,128)S(1)}, u32[]{:S(2)}, u32[]{:S(2)}) async-start(f32[32,40,128]{2,1,0:T(8,128)} %get-tuple-element.13), calls=%async_computation | async-start | bytes 1310720 | tf_op jit(solution)/shard_map/all_to_all | solution.py:407
  161.4 0.6 constant_dynamic-slice_fusion
  162.0 20.0 %all-to-all-done.end_ref = f32[32,40,128]{2,1,0:T(8,128)S(1)} async-done(((f32[32,40,128]{2,1,0:T(8,128)}), f32[32,40,128]{2,1,0:T(8,128)S(1)}, u32[]{:S(2)}, u32[]{:S(2)}) %all-to-all-start) | async-done | bytes 655392 | tf_op jit(solution)/shard_map/all_to_all | solution.py:407
  182.0 0.8 copy-done.3
  182.8 2.0 prefix.1
  184.8 22.8 %all_to_all.10.hin_ref = f32[32,32,128]{2,1,0:T(8,128)} all-to-all(f32[32,32,128]{2,1,0:T(8,128)} %prefix.1), channel_id=1, replica_groups=mesh['group'=8,'ctx'=32] {'ctx'}, dimensions={0} | all-to-all | bytes 1048576 | tf_op jit(solution)/shard_map/all_to_all | solution.py:409
  207.6 35.5 %gate_pass.1 = bf16[256,8192]{1,0:T(8,128)(2,1)} custom-call(s32[4]{0:T(128)} %pad_add_fusion.info_ref.len_ref, f32[256,64,128]{2,1,0:T(8,128)} %get-tuple-element.11.y_ref, f32[256,64,128]{2,1,0:T(8,128)} %get-tuple-element.12.cum_ref, f32[32,32,128]{2,1,0:T(8,128)} %all_to_all.10.hin_ref, f32[24,64,128]{2,1,0:T(8,128)} %get-tuple-element.14.par_ref, ...), custom_call_target="tpu_custom_call" | custom-call | tf_op jit(solution)/shard_map/gate_pass/pallas_call | solution.py:283
  (47 shorter events, 1.4 us)
Async XLA Ops:
  3.3 3.9 %collective-permute-start.1 = (bf16[1,32,640]{2,1,0:T(8,128)(2,1)S(1)}, bf16[1,32,640]{2,1,0:T(8,128)(2,1)S(1)}, u32[]{:S(2)}, u32[]{:S(2)}) collective-permute-start(bf16[1,32,640]{2,1,0:T(8,128)(2,1)S(1)} %bitcast.31), channel_id=1, source_target_pairs={{128,0},{129,1},{0,128},{1,129},{130,2},{131,3},{2,130},{3,131},{1... | collective-permute-start | bytes 122888 | tf_op jit(solution)/shard_map/ppermute | solution.py:321
  7.3 4.9 %collective-permute-start.2 = (bf16[2,32,640]{2,1,0:T(8,128)(2,1)S(1)}, bf16[2,32,640]{2,1,0:T(8,128)(2,1)S(1)}, u32[]{:S(2)}, u32[]{:S(2)}) collective-permute-start(bf16[2,32,640]{2,1,0:T(8,128)(2,1)S(1)} %pad_maximum_fusion.5), channel_id=1, source_target_pairs={{2,0},{3,1},{130,128},{131,129},{0,2},{1,3},{128,130},{129,131},{6... | collective-permute-start | bytes 245768 | tf_op jit(solution)/shard_map/ppermute | solution.py:321
  12.3 9.8 %collective-permute-start.3 = (bf16[4,32,640]{2,1,0:T(8,128)(2,1)S(1)}, bf16[4,32,640]{2,1,0:T(8,128)(2,1)S(1)}, u32[]{:S(2)}, u32[]{:S(2)}) collective-permute-start(bf16[4,32,640]{2,1,0:T(8,128)(2,1)S(1)} %pad_maximum_fusion.4), channel_id=1, source_target_pairs={{4,0},{5,1},{132,128},{133,129},{6,2},{7,3},{134,130},{135,131},{0... | collective-permute-start | bytes 491528 | tf_op jit(solution)/shard_map/ppermute | solution.py:321
  22.1 7.2 %collective-permute-start.4 = (bf16[8,32,640]{2,1,0:T(8,128)(2,1)S(1)}, bf16[8,32,640]{2,1,0:T(8,128)(2,1)S(1)}, u32[]{:S(2)}, u32[]{:S(2)}) collective-permute-start(bf16[8,32,640]{2,1,0:T(8,128)(2,1)S(1)} %pad_maximum_fusion.3), channel_id=1, source_target_pairs={{1,0},{0,1},{129,128},{128,129},{3,2},{2,3},{131,130},{130,131},{5... | collective-permute-start | bytes 983048 | tf_op jit(solution)/shard_map/ppermute | solution.py:321
  29.6 7.2 %collective-permute-start.13 = (bf16[1,2,4,2,16,640]{5,4,3,2,1,0:T(8,128)(2,1)S(1)}, bf16[1,2,4,2,16,640]{5,4,3,2,1,0:T(8,128)(2,1)S(1)}, u32[]{:S(2)}, u32[]{:S(2)}) collective-permute-start(bf16[1,2,4,2,16,640]{5,4,3,2,1,0:T(8,128)(2,1)S(1)} %get-tuple-element.19), channel_id=1, source_target_pairs={{8,0},{25,1},{136,128},{153,129},{10,2},{27,3},{138,130},{155,131}... | collective-permute-start | bytes 983048 | tf_op jit(solution)/shard_map/ppermute | solution.py:321
  30.7 7.2 %collective-permute-start.5 = (bf16[1,2,4,2,16,640]{5,4,3,2,1,0:T(8,128)(2,1)S(1)}, bf16[1,2,4,2,16,640]{5,4,3,2,1,0:T(8,128)(2,1)S(1)}, u32[]{:S(2)}, u32[]{:S(2)}) collective-permute-start(bf16[1,2,4,2,16,640]{5,4,3,2,1,0:T(8,128)(2,1)S(1)} %get-tuple-element.20), channel_id=1, source_target_pairs={{32,0},{97,1},{160,128},{225,129},{34,2},{99,3},{162,130},{227,131... | collective-permute-start | bytes 983048 | tf_op jit(solution)/shard_map/ppermute | solution.py:321
  36.8 7.3 %collective-permute-start.15 = (bf16[1,1,4,2,16,640]{5,4,3,2,1,0:T(8,128)(2,1)S(1)}, bf16[1,1,4,2,16,640]{5,4,3,2,1,0:T(8,128)(2,1)S(1)}, u32[]{:S(2)}, u32[]{:S(2)}) collective-permute-start(bf16[1,1,4,2,16,640]{5,4,3,2,1,0:T(8,128)(2,1)S(1)} %slice_select_fusion.2), channel_id=1, source_target_pairs={{8,0},{25,1},{136,128},{153,129},{10,2},{27,3},{138,130},{155,131}... | collective-permute-start | bytes 491528 | tf_op jit(solution)/shard_map/ppermute | solution.py:321
  37.9 9.1 %collective-permute-start.6 = (bf16[1,2,4,2,16,640]{5,4,3,2,1,0:T(8,128)(2,1)S(1)}, bf16[1,2,4,2,16,640]{5,4,3,2,1,0:T(8,128)(2,1)S(1)}, u32[]{:S(2)}, u32[]{:S(2)}) collective-permute-start(bf16[1,2,4,2,16,640]{5,4,3,2,1,0:T(8,128)(2,1)S(1)} %collective-permute-done.5), channel_id=1, source_target_pairs={{1,0},{0,1},{129,128},{128,129},{3,2},{2,3},{131,130},{130,131},{5... | collective-permute-start | bytes 983048 | tf_op jit(solution)/shard_map/ppermute | solution.py:321
  41.0 5.5 %collective-permute-start.7 = (bf16[1,1,4,2,16,640]{5,4,3,2,1,0:T(8,128)(2,1)S(1)}, bf16[1,1,4,2,16,640]{5,4,3,2,1,0:T(8,128)(2,1)S(1)}, u32[]{:S(2)}, u32[]{:S(2)}) collective-permute-start(bf16[1,1,4,2,16,640]{5,4,3,2,1,0:T(8,128)(2,1)S(1)} %slice_select_fusion.3), channel_id=1, source_target_pairs={{32,0},{97,1},{160,128},{225,129},{34,2},{99,3},{162,130},{227,131... | collective-permute-start | bytes 491528 | tf_op jit(solution)/shard_map/ppermute | solution.py:321
  42.4 5.9 %collective-permute-start.14 = (bf16[1,2,4,2,16,640]{5,4,3,2,1,0:T(8,128)(2,1)S(1)}, bf16[1,2,4,2,16,640]{5,4,3,2,1,0:T(8,128)(2,1)S(1)}, u32[]{:S(2)}, u32[]{:S(2)}) collective-permute-start(bf16[1,2,4,2,16,640]{5,4,3,2,1,0:T(8,128)(2,1)S(1)} %collective-permute-done.13), channel_id=1, source_target_pairs={{1,0},{0,1},{129,128},{128,129},{3,2},{2,3},{131,130},{130,131},{5... | collective-permute-start | bytes 983048 | tf_op jit(solution)/shard_map/ppermute | solution.py:321
  44.1 4.3 %collective-permute-start.16 = (bf16[1,1,4,2,16,640]{5,4,3,2,1,0:T(8,128)(2,1)S(1)}, bf16[1,1,4,2,16,640]{5,4,3,2,1,0:T(8,128)(2,1)S(1)}, u32[]{:S(2)}, u32[]{:S(2)}) collective-permute-start(bf16[1,1,4,2,16,640]{5,4,3,2,1,0:T(8,128)(2,1)S(1)} %collective-permute-done.15), channel_id=1, source_target_pairs={{1,0},{0,1},{129,128},{128,129},{3,2},{2,3},{131,130},{130,131},{5... | collective-permute-start | bytes 491528 | tf_op jit(solution)/shard_map/ppermute | solution.py:321
  46.6 1.4 collective-permute-start.8
  48.2 1.1 copy-start
  48.3 17.7 %collective-permute-start.9 = (bf16[4,2,4,2,16,640]{5,4,3,2,1,0:T(8,128)(2,1)S(1)}, bf16[4,2,4,2,16,640]{5,4,3,2,1,0:T(8,128)(2,1)S(1)}, u32[]{:S(2)}, u32[]{:S(2)}) collective-permute-start(bf16[4,2,4,2,16,640]{5,4,3,2,1,0:T(8,128)(2,1)S(1)} %pad_maximum_fusion.refs_0_), channel_id=1, source_target_pairs={{8,0},{25,1},{136,128},{153,129},{10,2},{27,3},{138,130},{155,131}... | collective-permute-start | bytes 3932168 | tf_op jit(solution)/shard_map/ppermute | solution.py:321
  49.3 19.9 %copy-start.2 = (bf16[4,2,4,2,16,640]{5,4,3,2,1,0:T(8,128)(2,1)}, bf16[4,2,4,2,16,640]{5,4,3,2,1,0:T(8,128)(2,1)S(1)}, u32[]{:S(2)}) copy-start(bf16[4,2,4,2,16,640]{5,4,3,2,1,0:T(8,128)(2,1)S(1)} %pad_maximum_fusion.1.refs_5_) | copy-start | bytes 3932164
  49.3 18.5 %collective-permute-start.17 = (bf16[4,2,4,2,16,640]{5,4,3,2,1,0:T(8,128)(2,1)S(1)}, bf16[4,2,4,2,16,640]{5,4,3,2,1,0:T(8,128)(2,1)}, u32[]{:S(2)}, u32[]{:S(2)}) collective-permute-start(bf16[4,2,4,2,16,640]{5,4,3,2,1,0:T(8,128)(2,1)S(1)} %pad_maximum_fusion.1.refs_5_), channel_id=1, source_target_pairs={{32,0},{97,1},{160,128},{225,129},{34,2},{99,3},{162,130},{227,131... | collective-permute-start | bytes 3932168 | tf_op jit(solution)/shard_map/ppermute | solution.py:321
  66.0 3.9 %copy-start.1 = (bf16[4,2,4,2,16,640]{5,4,3,2,1,0:T(8,128)(2,1)}, bf16[4,2,4,2,16,640]{5,4,3,2,1,0:T(8,128)(2,1)S(1)}, u32[]{:S(2)}) copy-start(bf16[4,2,4,2,16,640]{5,4,3,2,1,0:T(8,128)(2,1)S(1)} %collective-permute-done.9.refs_1_) | copy-start | bytes 3932164
  66.1 10.7 %collective-permute-start.11 = (bf16[4,1,4,2,16,640]{5,4,3,2,1,0:T(8,128)(2,1)S(1)}, bf16[4,1,4,2,16,640]{5,4,3,2,1,0:T(8,128)(2,1)S(1)}, u32[]{:S(2)}, u32[]{:S(2)}) collective-permute-start(bf16[4,1,4,2,16,640]{5,4,3,2,1,0:T(8,128)(2,1)S(1)} %slice_select_fusion.1), channel_id=1, source_target_pairs={{8,0},{25,1},{136,128},{153,129},{10,2},{27,3},{138,130},{155,131}... | collective-permute-start | bytes 1966088 | tf_op jit(solution)/shard_map/ppermute | solution.py:321
  69.2 10.8 %collective-permute-start.19 = (bf16[4,1,4,2,16,640]{5,4,3,2,1,0:T(8,128)(2,1)S(1)}, bf16[4,1,4,2,16,640]{5,4,3,2,1,0:T(8,128)(2,1)}, u32[]{:S(2)}, u32[]{:S(2)}) collective-permute-start(bf16[4,1,4,2,16,640]{5,4,3,2,1,0:T(8,128)(2,1)S(1)} %slice_select_fusion), channel_id=1, source_target_pairs={{32,0},{97,1},{160,128},{225,129},{34,2},{99,3},{162,130},{227,131... | collective-permute-start | bytes 1966088 | tf_op jit(solution)/shard_map/ppermute | solution.py:321
  70.0 17.0 %collective-permute-start.10 = (bf16[4,2,4,2,16,640]{5,4,3,2,1,0:T(8,128)(2,1)S(1)}, bf16[4,2,4,2,16,640]{5,4,3,2,1,0:T(8,128)(2,1)S(1)}, u32[]{:S(2)}, u32[]{:S(2)}) collective-permute-start(bf16[4,2,4,2,16,640]{5,4,3,2,1,0:T(8,128)(2,1)S(1)} %collective-permute-done.9.refs_1_), channel_id=1, source_target_pairs={{1,0},{0,1},{129,128},{128,129},{3,2},{2,3},{131,130},{130,131},{5... | collective-permute-start | bytes 3932168 | tf_op jit(solution)/shard_map/ppermute | solution.py:321
  74.9 12.1 %collective-permute-start.18 = (bf16[4,2,4,2,16,640]{5,4,3,2,1,0:T(8,128)(2,1)}, bf16[4,2,4,2,16,640]{5,4,3,2,1,0:T(8,128)(2,1)}, u32[]{:S(2)}, u32[]{:S(2)}) collective-permute-start(bf16[4,2,4,2,16,640]{5,4,3,2,1,0:T(8,128)(2,1)} %collective-permute-done.17.refs_6_), channel_id=1, source_target_pairs={{1,0},{0,1},{129,128},{128,129},{3,2},{2,3},{131,130},{130,131},{5... | collective-permute-start | bytes 3932168 | tf_op jit(solution)/shard_map/ppermute | solution.py:321
  76.8 10.2 %copy-start.6 = (bf16[4,1,4,2,16,640]{5,4,3,2,1,0:T(8,128)(2,1)}, bf16[4,1,4,2,16,640]{5,4,3,2,1,0:T(8,128)(2,1)S(1)}, u32[]{:S(2)}) copy-start(bf16[4,1,4,2,16,640]{5,4,3,2,1,0:T(8,128)(2,1)S(1)} %collective-permute-done.11.refs_3_) | copy-start | bytes 1966084
  76.8 10.2 %collective-permute-start.12 = (bf16[4,1,4,2,16,640]{5,4,3,2,1,0:T(8,128)(2,1)S(1)}, bf16[4,1,4,2,16,640]{5,4,3,2,1,0:T(8,128)(2,1)}, u32[]{:S(2)}, u32[]{:S(2)}) collective-permute-start(bf16[4,1,4,2,16,640]{5,4,3,2,1,0:T(8,128)(2,1)S(1)} %collective-permute-done.11.refs_3_), channel_id=1, source_target_pairs={{1,0},{0,1},{129,128},{128,129},{3,2},{2,3},{131,130},{130,131},{5... | collective-permute-start | bytes 1966088 | tf_op jit(solution)/shard_map/ppermute | solution.py:321
  80.0 7.0 %collective-permute-start.20 = (bf16[4,1,4,2,16,640]{5,4,3,2,1,0:T(8,128)(2,1)}, bf16[4,1,4,2,16,640]{5,4,3,2,1,0:T(8,128)(2,1)}, u32[]{:S(2)}, u32[]{:S(2)}) collective-permute-start(bf16[4,1,4,2,16,640]{5,4,3,2,1,0:T(8,128)(2,1)} %collective-permute-done.19.refs_8_), channel_id=1, source_target_pairs={{1,0},{0,1},{129,128},{128,129},{3,2},{2,3},{131,130},{130,131},{5... | collective-permute-start | bytes 1966088 | tf_op jit(solution)/shard_map/ppermute | solution.py:321
  83.0 3.2 %collective-permute-start = (bf16[3,8192]{1,0:T(4,128)(2,1)S(1)}, bf16[3,8192]{1,0:T(4,128)(2,1)S(1)}, u32[]{:S(2)}, u32[]{:S(2)}) collective-permute-start(bf16[3,8192]{1,0:T(4,128)(2,1)S(1)} %bitcast_select_fusion), channel_id=1, source_target_pairs={{0,1},{1,2},{2,3},{3,4},{4,5},{5,6},{6,7},{7,8},{8,9},{9,10},{10,1... | collective-permute-start | bytes 147464 | tf_op jit(solution)/shard_map/ppermute | solution.py:382
  87.0 1.1 copy-start.5
  149.5 11.8 %copy-start.4 = (f32[24,64,128]{2,1,0:T(8,128)S(1)}, f32[24,64,128]{2,1,0:T(8,128)}, u32[]{:S(2)}) copy-start(f32[24,64,128]{2,1,0:T(8,128)} %get-tuple-element.14.par_ref) | copy-start | bytes 2359300
  149.5 32.4 %all-to-all-start = ((f32[32,40,128]{2,1,0:T(8,128)}), f32[32,40,128]{2,1,0:T(8,128)S(1)}, u32[]{:S(2)}, u32[]{:S(2)}) async-start(f32[32,40,128]{2,1,0:T(8,128)} %get-tuple-element.13), calls=%async_computation | async-start | bytes 1310720 | tf_op jit(solution)/shard_map/all_to_all | solution.py:407
  182.0 0.8 copy-start.3

commit v4 on v3

--- a/solution.py
+++ b/solution.py
@@ -14,6 +14,11 @@
 
 def sigmoid(v):
     return 1.0 / (1.0 + jnp.exp(-v))
+
+
+def log_one_plus(u):
+    w = 1.0 + u
+    return jnp.log(w) + (u - (w - 1.0))
 
 
 def settings():
@@ -127,7 +132,7 @@
         for g in range(ROWS):
             cols = slice(g * LANES, (g + 1) * LANES)
             v = raw[:, cols] + par_scr[at, 5 * ROWS + g : 5 * ROWS + g + 1, :]
-            soft = jnp.maximum(v, 0.0) + jnp.log1p(jnp.exp(-jnp.abs(v)))
+            soft = jnp.maximum(v, 0.0) + log_one_plus(jnp.exp(-jnp.abs(v)))
             d = jnp.where(keep, soft, 0.0)
             place = slice(g * 8, (g + 1) * 8)
             d_scr[:, place, :] = d.reshape(tok // 8, 8, LANES)
@@ -226,6 +231,41 @@
     )(info, x, rim, *pieces)
 
 
+def combine_kernel(info_ref, ends_ref, other_ref, par_ref, out_ref, a_scr):
+    pairs, sent, _ = out_ref.shape
+    rows = sent - 8
+    for p in range(pairs):
+        for n in range(rows // 2):
+            a_scr[p, 2 * n : 2 * n + 2, :] = par_ref[VECTORS + n, 2 * p : 2 * p + 2, :]
+    earlier = info_ref[3] == 0
+    for p in range(pairs):
+        own, other = ends_ref[p], other_ref[p]
+        head, tail = jnp.where(earlier, own, other), jnp.where(earlier, other, own)
+        spent = tail[rows:]
+        for r in range(0, rows, 8):
+            decay = jnp.exp2(jnp.exp(a_scr[p, r : r + 8, :]) * (-LOG2E) * spent)
+            out_ref[p, r : r + 8, :] = decay * head[r : r + 8] + tail[r : r + 8]
+        out_ref[p, rows:, :] = head[rows:] + spent
+
+
+def combine(info, ends, other, pars):
+    pairs, sent, _ = ends.shape
+    half = pl.BlockSpec((pairs // 2, sent, LANES), lambda i, s: (s[3], 0, 0))
+    return pl.pallas_call(
+        combine_kernel,
+        grid_spec=pltpu.PrefetchScalarGridSpec(
+            num_scalar_prefetch=1,
+            grid=(1,),
+            in_specs=[half, half, pl.BlockSpec((pars.shape[0], pairs, LANES), lambda i, s: (0, s[3], 0))],
+            out_specs=whole((pairs // 2, sent, LANES)),
+            scratch_shapes=[pltpu.VMEM((pairs // 2, sent - 8, LANES), jnp.float32)],
+        ),
+        out_shape=jax.ShapeDtypeStruct((pairs // 2, sent, LANES), jnp.float32),
+        compiler_params=settings(),
+        name="combine",
+    )(info, ends, other, pars)
+
+
 def prefix_kernel(end_ref, alog_ref, in_ref):
     blocks = end_ref.shape[0]
     rows = alog_ref.shape[0]
@@ -246,13 +286,34 @@
     )(ends, alog)
 
 
-def gate_kernel(len_ref, y_ref, cum_ref, hin_ref, par_ref, act_ref, z_ref, c_ref, out_ref, y_scr, a_scr, h_scr):
+def gate_kernel(
+    info_ref, y_ref, cum_ref, hin_ref, hin_too_ref, other_ref, par_ref, act_ref, z_ref, c_ref, out_ref, y_scr, a_scr, h_scr, e_scr
+):
     tok = act_ref.shape[0]
     states = a_scr.shape[0]
     a_scr[...] = jnp.exp(par_ref[VECTORS : VECTORS + states]) * (-LOG2E)
-    for q in range(ROWS // 2):
+    core = info_ref[3]
+    own_half = pl.program_id(0) // 4 == core
+
+    @pl.when(own_half)
+    def _():
+        for q in range(ROWS // 2):
+            for n in range(states):
+                h_scr[n, 2 * q : 2 * q + 2, :] = hin_ref[q, 2 * n : 2 * n + 2, :]
+
+    @pl.when(jnp.logical_not(own_half))
+    def _():
+        for q in range(ROWS // 2):
+            for n in range(states):
+                h_scr[n, 2 * q : 2 * q + 2, :] = hin_too_ref[q, 2 * n : 2 * n + 2, :]
+
+    @pl.when(core == 1)
+    def _():
+        for q in range(ROWS // 2):
+            for n in range(states + 1):
+                e_scr[n, 2 * q : 2 * q + 2, :] = other_ref[q, 2 * n : 2 * n + 2, :]
         for n in range(states):
-            h_scr[n, 2 * q : 2 * q + 2, :] = hin_ref[q, 2 * n : 2 * n + 2, :]
+            h_scr[n] = jnp.exp2(a_scr[n] * e_scr[states]) * h_scr[n] + e_scr[n]
 
     def block(i, carry):
         for o in range(8):
@@ -267,7 +328,7 @@
         return carry
 
     lax.fori_loop(0, tok // 8, block, 0)
-    keep = lax.broadcasted_iota(jnp.int32, (tok, LANES), 0) < len_ref[0]
+    keep = lax.broadcasted_iota(jnp.int32, (tok, LANES), 0) < info_ref[0]
     for g in range(ROWS):
         cols = slice(g * LANES, (g + 1) * LANES)
         y = y_scr[:, g * 8 : (g + 1) * 8, :].reshape(tok, LANES)
@@ -276,7 +337,7 @@
         out_ref[:, cols] = jnp.where(keep, out, 0.0).astype(jnp.bfloat16)
 
 
-def gate_pass(info, y, cum, hin, pars, act, z, c_wide):
+def gate_pass(info, y, cum, hin, hin_too, other, pars, act, z, c_wide):
     tok, chans = act.shape
     states = c_wide.shape[0] // tok
     columns = pl.BlockSpec((tok, WIDE), lambda i, *_: (0, i))
@@ -288,7 +349,9 @@
             in_specs=[
                 per_step(tok),
                 per_step(tok),
-                pl.BlockSpec((ROWS // 2, 2 * states, LANES), lambda i, *_: (i, 0, 0)),
+                pl.BlockSpec((ROWS // 2, 2 * states, LANES), lambda i, *_: (i % 4, 0, 0)),
+                pl.BlockSpec((ROWS // 2, 2 * states, LANES), lambda i, *_: (i % 4, 0, 0)),
+                pl.BlockSpec((ROWS // 2, other.shape[1], LANES), lambda i, *_: (i, 0, 0)),
                 per_step(pars.shape[0]),
                 columns,
                 columns,
@@ -299,12 +362,13 @@
                 pltpu.VMEM((tok // 8, 8 * ROWS, LANES), jnp.float32),
                 pltpu.VMEM((states, ROWS, LANES), jnp.float32),
                 pltpu.VMEM((states, ROWS, LANES), jnp.float32),
+                pltpu.VMEM((states + 1, ROWS, LANES), jnp.float32),
             ],
         ),
         out_shape=jax.ShapeDtypeStruct((tok, chans), jnp.bfloat16),
         compiler_params=settings(),
         name="gate_pass",
-    )(info, y, cum, hin, pars, act, z, c_wide)
+    )(info, y, cum, hin, hin_too, other, pars, act, z, c_wide)
 
 
 def device(x, y, z, core):
@@ -359,6 +423,11 @@
     zero = own_core == 0
     far = jnp.concatenate([jnp.where(zero, far, far_too), jnp.where(zero, far_too, far)], axis=1)
     return jnp.concatenate([value, jnp.where(zero, near, near_too), far, jnp.where(zero, near_too, near)], axis=0)
+
+
+def exchange(value):
+    groups = [list(range(core, 32, 2)) for core in range(2)]
+    return lax.all_to_all(value, "ctx", split_axis=0, concat_axis=0, tiled=True, axis_index_groups=groups)
 
 
 def shards(
@@ -391,7 +460,8 @@
     fill = -(xproj_weight.shape[1] + 3 * count + rank) % LANES
     parts += [jnp.zeros((width, fill), jnp.bfloat16), dtproj_weight.T]
     mats = jnp.concatenate([xproj_weight, *parts], axis=1)[None]
-    for axis, bit in (("z", 1), ("z", 2), ("z", 4), ("core", 1)):
+    mats, rim = lax.optimization_barrier((double(mats, "z", 1, own_z), rim))
+    for axis, bit in (("z", 2), ("z", 4), ("core", 1)):
         mats = double(mats, axis, bit, own[axis])
     mats = mats.reshape(1, 2, 4, 2, *mats.shape[1:])
     upper = row_of_four(mats[..., : width // 2, :], "y", own_core)
@@ -403,11 +473,13 @@
         pieces += [value, near, swap(near), far, swap(far)]
 
     act, pars, y, cum, ends, c_wide = scan_pass(info, x, rim, pieces, rank, states, count)
-    mine = lax.dynamic_slice_in_dim(pars[VECTORS : VECTORS + states], 2 * ctx, 2, axis=1).reshape(2 * states, LANES)
-    ends = lax.all_to_all(ends, "ctx", split_axis=0, concat_axis=0, tiled=True)
-    hin = prefix(ends, mine)
-    hin = lax.all_to_all(hin, "ctx", split_axis=0, concat_axis=0, tiled=True)
-    out = gate_pass(info, y, cum, hin, pars, act, z, c_wide)
+    other = swap(ends)
+    chip = combine(info, ends, other, pars)
+    place = 2 * ((ctx & 1) * (blocks // 2) + (ctx >> 1))
+    mine = lax.dynamic_slice_in_dim(pars[VECTORS : VECTORS + states], place, 2, axis=1).reshape(2 * states, LANES)
+    chip = exchange(chip)
+    hin = exchange(prefix(chip, mine))
+    out = gate_pass(info, y, cum, hin, swap(hin), other, pars, act, z, c_wide)
     return out[None]
 
 

time: 244 us -> 237 us (0.971)
  blocking collectives: 22.8 us -> 14.4 us
  starting transfers between devices: 49.9 us -> 43.3 us
  waiting for transfers between devices: 59.3 us -> 64.2 us
  Pallas kernels: 98.9 us -> 102 us
    ppermute x20 -> x22, waiting for transfers between devices: 38.6 us -> 50.9 us  [fetch(): return lax.ppermute(value, ('group', 'ctx'), route)]
    all_to_all x1, blocking collectives: 22.8 us -> 14.4 us  [exchange(): lax.all_to_all(value, 'ctx', split_axis=0, concat_axis=0, tiled=True, axi...]
    all_to_all x1, waiting for transfers between devices: 20 us -> 12 us  [exchange(): lax.all_to_all(value, 'ctx', split_axis=0, concat_axis=0, tiled=True, axi...]
    all_to_all x1, starting transfers between devices: 11.8 us -> 5.11 us  [exchange(): lax.all_to_all(value, 'ctx', split_axis=0, concat_axis=0, tiled=True, axi...]
    ppermute x1, starting transfers between devices: 1.92 us -> 5.74 us  [shards(): rim = lax.ppermute(edge, 'ctx', [(i, i + 1) for i in range(blocks - 1)])]
    ppermute x20 -> x22, starting transfers between devices: 36.2 us -> 32.5 us  [fetch(): return lax.ppermute(value, ('group', 'ctx'), route)]
    pallas_call x0 -> x1, Pallas kernels: none -> 2.9 us  [combine(): pl.pallas_call(combine_kernel, grid_spec=pltpu.PrefetchScalarGridSpec(num...]
  transfers between devices with their start and end apart: 22 -> 24, of which waited for: 14 -> 16; matrix products, arithmetic and copies ran while one was open for 2% -> 2% of each run, Pallas kernels for 0% -> 0%
where the time goes in v4:
time: 237 us; the launch traced here: 236 us
  Pallas kernels  102 us (43%)
  waiting for transfers between devices  64.2 us (27%)
  starting transfers between devices  43.3 us (18%)
  blocking collectives  14.4 us (6%)
  local copies, waits for them, and re-layouts  7.04 us (3%)
  other arithmetic  3.96 us (2%)
    pallas_call x1, Pallas kernels, scan_pass(): pl.pallas_call(scan_kernel, grid_spec=pltpu.PrefetchScalarGridSpec(num_sc...  60.7 us
    ppermute x22, waiting for transfers between devices, fetch(): return lax.ppermute(value, ('group', 'ctx'), route)  50.9 us
    pallas_call x1, Pallas kernels, gate_pass(): pl.pallas_call(gate_kernel, grid_spec=pltpu.PrefetchScalarGridSpec(num_sc...  36.5 us
    ppermute x22, starting transfers between devices, fetch(): return lax.ppermute(value, ('group', 'ctx'), route)  32.5 us
    all_to_all x1, blocking collectives, exchange(): lax.all_to_all(value, 'ctx', split_axis=0, concat_axis=0, tiled=True, axi...  14.4 us
    all_to_all x1, waiting for transfers between devices, exchange(): lax.all_to_all(value, 'ctx', split_axis=0, concat_axis=0, tiled=True, axi...  12 us
    ppermute x1, starting transfers between devices, shards(): rim = lax.ppermute(edge, 'ctx', [(i, i + 1) for i in range(blocks - 1)])  5.74 us
    all_to_all x1, starting transfers between devices, exchange(): lax.all_to_all(value, 'ctx', split_axis=0, concat_axis=0, tiled=True, axi...  5.11 us
  transfers between devices with their start and end apart: 24, of which 16 were waited for; matrix products, arithmetic and copies ran while one was open for 2% of the time, Pallas kernels for 0%

profile of v4, /device:TPU:1, one launch (start us, length us, event | category | flops | bytes accessed | tf_op | source)
XLA Modules:
  0.0 235.6 jit_solution(15652238764079594614)
XLA Ops:
  0.0 0.7 slice.42
  0.7 1.5 concatenate.33
  2.5 0.8 concatenate.34
  3.3 2.5 %collective-permute-start = (bf16[1,32,640]{2,1,0:T(8,128)(2,1)S(1)}, bf16[1,32,640]{2,1,0:T(8,128)(2,1)S(1)}, u32[]{:S(2)}, u32[]{:S(2)}) collective-permute-start(bf16[1,32,640]{2,1,0:T(8,128)(2,1)S(1)} %bitcast.31), channel_id=1, source_target_pairs={{128,0},{129,1},{0,128},{1,129},{130,2},{131,3},{2,130},{3,131},{1... | collective-permute-start | bytes 122888 | tf_op jit(solution)/shard_map/ppermute | solution.py:385
  6.5 1.0 bitcast_select_fusion
  7.5 5.7 %collective-permute-start.1 = (bf16[3,8192]{1,0:T(4,128)(2,1)S(1)}, bf16[3,8192]{1,0:T(4,128)(2,1)S(1)}, u32[]{:S(2)}, u32[]{:S(2)}) collective-permute-start(bf16[3,8192]{1,0:T(4,128)(2,1)S(1)} %bitcast_select_fusion), channel_id=1, source_target_pairs={{0,1},{1,2},{2,3},{3,4},{4,5},{5,6},{6,7},{7,8},{8,9},{9,10},{10,1... | collective-permute-start | bytes 147464 | tf_op jit(solution)/shard_map/ppermute | solution.py:451
  13.4 1.2 collective-permute-done.1
  14.6 0.7 concatenate.36.rim_ref
  15.3 3.3 %collective-permute-start.2 = (bf16[2,32,640]{2,1,0:T(8,128)(2,1)S(1)}, bf16[2,32,640]{2,1,0:T(8,128)(2,1)S(1)}, u32[]{:S(2)}, u32[]{:S(2)}) collective-permute-start(bf16[2,32,640]{2,1,0:T(8,128)(2,1)S(1)} %pad_maximum_fusion.5), channel_id=1, source_target_pairs={{2,0},{3,1},{130,128},{131,129},{0,2},{1,3},{128,130},{129,131},{6... | collective-permute-start | bytes 245768 | tf_op jit(solution)/shard_map/ppermute | solution.py:385
  18.6 4.5 %collective-permute-done.2 = bf16[2,32,640]{2,1,0:T(8,128)(2,1)S(1)} collective-permute-done((bf16[2,32,640]{2,1,0:T(8,128)(2,1)S(1)}, bf16[2,32,640]{2,1,0:T(8,128)(2,1)S(1)}, u32[]{:S(2)}, u32[]{:S(2)}) %collective-permute-start.2) | collective-permute-done | bytes 81952 | tf_op jit(solution)/shard_map/ppermute | solution.py:385
  23.1 1.6 collective-permute-start.3
  24.7 8.6 %collective-permute-done.3 = bf16[4,32,640]{2,1,0:T(8,128)(2,1)S(1)} collective-permute-done((bf16[4,32,640]{2,1,0:T(8,128)(2,1)S(1)}, bf16[4,32,640]{2,1,0:T(8,128)(2,1)S(1)}, u32[]{:S(2)}, u32[]{:S(2)}) %collective-permute-start.3) | collective-permute-done | bytes 163872 | tf_op jit(solution)/shard_map/ppermute | solution.py:385
  33.4 2.7 %collective-permute-start.4 = (bf16[8,32,640]{2,1,0:T(8,128)(2,1)S(1)}, bf16[8,32,640]{2,1,0:T(8,128)(2,1)S(1)}, u32[]{:S(2)}, u32[]{:S(2)}) collective-permute-start(bf16[8,32,640]{2,1,0:T(8,128)(2,1)S(1)} %pad_maximum_fusion.3), channel_id=1, source_target_pairs={{1,0},{0,1},{129,128},{128,129},{3,2},{2,3},{131,130},{130,131},{5... | collective-permute-start | bytes 983048 | tf_op jit(solution)/shard_map/ppermute | solution.py:385
  36.2 1.3 collective-permute-done.4
  37.7 1.4 collective-permute-start.5
  39.1 5.7 %collective-permute-done.13 = bf16[1,2,4,2,16,640]{5,4,3,2,1,0:T(8,128)(2,1)S(1)} collective-permute-done((bf16[1,2,4,2,16,640]{5,4,3,2,1,0:T(8,128)(2,1)S(1)}, bf16[1,2,4,2,16,640]{5,4,3,2,1,0:T(8,128)(2,1)S(1)}, u32[]{:S(2)}, u32[]{:S(2)}) %collective-permute-start.13) | collective-permute-done | bytes 327712 | tf_op jit(solution)/shard_map/ppermute | solution.py:385
  45.0 2.1 collective-permute-start.6
  47.1 1.4 collective-permute-start.7
  48.5 1.7 collective-permute-start.14
  50.6 2.0 collective-permute-done.7
  52.6 0.4 collective-permute-start.8
  53.1 1.0 collective-permute-done.8
  54.3 1.1 collective-permute-start.9
  56.1 15.9 %collective-permute-done.9.refs_1_ = bf16[4,2,4,2,16,640]{5,4,3,2,1,0:T(8,128)(2,1)S(1)} collective-permute-done((bf16[4,2,4,2,16,640]{5,4,3,2,1,0:T(8,128)(2,1)S(1)}, bf16[4,2,4,2,16,640]{5,4,3,2,1,0:T(8,128)(2,1)S(1)}, u32[]{:S(2)}, u32[]{:S(2)}) %collective-permute-start.9) | collective-permute-done | bytes 1310752 | tf_op jit(solution)/shard_map/ppermute | solution.py:385
  72.5 1.9 collective-permute-done.17.refs_6_
  74.4 1.4 slice_select_fusion
  76.1 5.0 %collective-permute-start.10 = (bf16[4,2,4,2,16,640]{5,4,3,2,1,0:T(8,128)(2,1)S(1)}, bf16[4,2,4,2,16,640]{5,4,3,2,1,0:T(8,128)(2,1)S(1)}, u32[]{:S(2)}, u32[]{:S(2)}) collective-permute-start(bf16[4,2,4,2,16,640]{5,4,3,2,1,0:T(8,128)(2,1)S(1)} %collective-permute-done.9.refs_1_), channel_id=1, source_target_pairs={{1,0},{0,1},{129,128},{128,129},{3,2},{2,3},{131,130},{130,131},{5... | collective-permute-start | bytes 3932168 | tf_op jit(solution)/shard_map/ppermute | solution.py:385
  81.1 1.9 collective-permute-done.11.refs_3_
  83.0 0.5 collective-permute-start.12
  83.5 3.3 %collective-permute-done.19.refs_8_ = bf16[4,1,4,2,16,640]{5,4,3,2,1,0:T(8,128)(2,1)} collective-permute-done((bf16[4,1,4,2,16,640]{5,4,3,2,1,0:T(8,128)(2,1)S(1)}, bf16[4,1,4,2,16,640]{5,4,3,2,1,0:T(8,128)(2,1)}, u32[]{:S(2)}, u32[]{:S(2)}) %collective-permute-start.19) | collective-permute-done | bytes 655392 | tf_op jit(solution)/shard_map/ppermute | solution.py:385
  86.8 2.4 %collective-permute-start.20 = (bf16[4,1,4,2,16,640]{5,4,3,2,1,0:T(8,128)(2,1)}, bf16[4,1,4,2,16,640]{5,4,3,2,1,0:T(8,128)(2,1)}, u32[]{:S(2)}, u32[]{:S(2)}) collective-permute-start(bf16[4,1,4,2,16,640]{5,4,3,2,1,0:T(8,128)(2,1)} %collective-permute-done.19.refs_8_), channel_id=1, source_target_pairs={{1,0},{0,1},{129,128},{128,129},{3,2},{2,3},{131,130},{130,131},{5... | collective-permute-start | bytes 1966088 | tf_op jit(solution)/shard_map/ppermute | solution.py:385
  89.2 0.6 pad_add_fusion.info_ref
  89.8 1.5 collective-permute-done.20.refs_9_
  91.3 60.7 %scan_pass.1 = (bf16[256,8192]{1,0:T(8,128)(2,1)}, f32[24,64,128]{2,1,0:T(8,128)}, f32[256,64,128]{2,1,0:T(8,128)}, f32[256,64,128]{2,1,0:T(8,128)}, f32[32,40,128]{2,1,0:T(8,128)}, /*index=5*/f32[4096,128]{1,0:T(8,128)}) custom-call(s32[4]{0:T(128)} %pad_add_fusion.info_ref, bf16[256,8192]{1,0:T(8,128)(2,1)} %bitcast.28, ...), custom_call_target="tpu_custom_call" | custom-call | tf_op jit(solution)/shard_map/scan_pass/pallas_call | solution.py:190
  151.9 0.5 collective-permute-start.21
  152.4 1.9 collective-permute-done.21.other_ref
  154.3 0.8 copy-done.4
  155.2 2.9 %combine.1 = f32[16,40,128]{2,1,0:T(8,128)} custom-call(s32[4]{0:T(128)} %pad_add_fusion.info_ref, f32[32,40,128]{2,1,0:T(8,128)} %get-tuple-element.17.ends_ref, f32[32,40,128]{2,1,0:T(8,128)} %copy-done.4, f32[24,64,128]{2,1,0:T(8,128)} %get-tuple-element.18.par_ref), custom_call_target="tpu_custom_call" | custom-call | tf_op jit(solution)/shard_map/combine/pallas_call | solution.py:254
  158.1 5.1 %all-to-all-start = ((f32[16,40,128]{2,1,0:T(8,128)}), f32[16,40,128]{2,1,0:T(8,128)S(1)}, u32[]{:S(2)}, u32[]{:S(2)}) async-start(f32[16,40,128]{2,1,0:T(8,128)} %combine.1), calls=%async_computation | async-start | bytes 655360 | tf_op jit(solution)/shard_map/all_to_all | solution.py:430
  163.3 0.6 constant_dynamic-slice_fusion
  163.9 12.0 %all-to-all-done.end_ref = f32[16,40,128]{2,1,0:T(8,128)S(1)} async-done(((f32[16,40,128]{2,1,0:T(8,128)}), f32[16,40,128]{2,1,0:T(8,128)S(1)}, u32[]{:S(2)}, u32[]{:S(2)}) %all-to-all-start) | async-done | bytes 327712 | tf_op jit(solution)/shard_map/all_to_all | solution.py:430
  175.9 0.7 copy-done.6
  176.6 1.7 prefix.1
  178.4 14.4 %all_to_all.10.hin_ref = f32[16,32,128]{2,1,0:T(8,128)S(1)} all-to-all(f32[16,32,128]{2,1,0:T(8,128)} %prefix.1), channel_id=1, replica_groups={{0,2,4,6,8,10,12,14,16,18,20,22,24,26,28,30},{1,3,5,7,9,11,13,15,17,19,..., dimensions={0} | all-to-all | bytes 524288 | tf_op jit(solution)/shard_map/all_to_all | solution.py:430
  192.8 4.5 %collective-permute-start.22 = (f32[16,32,128]{2,1,0:T(8,128)S(1)}, f32[16,32,128]{2,1,0:T(8,128)S(1)}, u32[]{:S(2)}, u32[]{:S(2)}) collective-permute-start(f32[16,32,128]{2,1,0:T(8,128)S(1)} %all_to_all.10.hin_ref), channel_id=1, source_target_pairs={{1,0},{0,1},{129,128},{128,129},{3,2},{2,3},{131,130},{130,131},{5... | collective-permute-start | bytes 786440 | tf_op jit(solution)/shard_map/ppermute | solution.py:385
  197.2 1.2 collective-permute-done.22.hin_too_ref
  198.4 0.7 copy-done.8
  199.1 36.5 %gate_pass.1 = bf16[256,8192]{1,0:T(8,128)(2,1)} custom-call(s32[4]{0:T(128)} %pad_add_fusion.info_ref, f32[256,64,128]{2,1,0:T(8,128)} %get-tuple-element.15.y_ref, f32[256,64,128]{2,1,0:T(8,128)} %get-tuple-element.16.cum_ref, f32[16,32,128]{2,1,0:T(8,128)} %copy-done.7, f32[16,32,128]{2,1,0:T(8,128)} %copy-done.8, f32[32,40,128]{2,1,0:T(8,128)} %copy-done.4, ...), custom_call_target="tpu_custom_call" | custom-call | tf_op jit(solution)/shard_map/gate_pass/pallas_call | solution.py:344
  (56 shorter events, 3.0 us)
Async XLA Ops:
  3.3 10.0 %collective-permute-start = (bf16[1,32,640]{2,1,0:T(8,128)(2,1)S(1)}, bf16[1,32,640]{2,1,0:T(8,128)(2,1)S(1)}, u32[]{:S(2)}, u32[]{:S(2)}) collective-permute-start(bf16[1,32,640]{2,1,0:T(8,128)(2,1)S(1)} %bitcast.31), channel_id=1, source_target_pairs={{128,0},{129,1},{0,128},{1,129},{130,2},{131,3},{2,130},{3,131},{1... | collective-permute-start | bytes 122888 | tf_op jit(solution)/shard_map/ppermute | solution.py:385
  7.5 7.1 %collective-permute-start.1 = (bf16[3,8192]{1,0:T(4,128)(2,1)S(1)}, bf16[3,8192]{1,0:T(4,128)(2,1)S(1)}, u32[]{:S(2)}, u32[]{:S(2)}) collective-permute-start(bf16[3,8192]{1,0:T(4,128)(2,1)S(1)} %bitcast_select_fusion), channel_id=1, source_target_pairs={{0,1},{1,2},{2,3},{3,4},{4,5},{5,6},{6,7},{7,8},{8,9},{9,10},{10,1... | collective-permute-start | bytes 147464 | tf_op jit(solution)/shard_map/ppermute | solution.py:451
  15.3 7.8 %collective-permute-start.2 = (bf16[2,32,640]{2,1,0:T(8,128)(2,1)S(1)}, bf16[2,32,640]{2,1,0:T(8,128)(2,1)S(1)}, u32[]{:S(2)}, u32[]{:S(2)}) collective-permute-start(bf16[2,32,640]{2,1,0:T(8,128)(2,1)S(1)} %pad_maximum_fusion.5), channel_id=1, source_target_pairs={{2,0},{3,1},{130,128},{131,129},{0,2},{1,3},{128,130},{129,131},{6... | collective-permute-start | bytes 245768 | tf_op jit(solution)/shard_map/ppermute | solution.py:385
  23.1 10.2 %collective-permute-start.3 = (bf16[4,32,640]{2,1,0:T(8,128)(2,1)S(1)}, bf16[4,32,640]{2,1,0:T(8,128)(2,1)S(1)}, u32[]{:S(2)}, u32[]{:S(2)}) collective-permute-start(bf16[4,32,640]{2,1,0:T(8,128)(2,1)S(1)} %pad_maximum_fusion.4), channel_id=1, source_target_pairs={{4,0},{5,1},{132,128},{133,129},{6,2},{7,3},{134,130},{135,131},{0... | collective-permute-start | bytes 491528 | tf_op jit(solution)/shard_map/ppermute | solution.py:385
  33.4 4.0 %collective-permute-start.4 = (bf16[8,32,640]{2,1,0:T(8,128)(2,1)S(1)}, bf16[8,32,640]{2,1,0:T(8,128)(2,1)S(1)}, u32[]{:S(2)}, u32[]{:S(2)}) collective-permute-start(bf16[8,32,640]{2,1,0:T(8,128)(2,1)S(1)} %pad_maximum_fusion.3), channel_id=1, source_target_pairs={{1,0},{0,1},{129,128},{128,129},{3,2},{2,3},{131,130},{130,131},{5... | collective-permute-start | bytes 983048 | tf_op jit(solution)/shard_map/ppermute | solution.py:385
  37.7 7.2 %collective-permute-start.13 = (bf16[1,2,4,2,16,640]{5,4,3,2,1,0:T(8,128)(2,1)S(1)}, bf16[1,2,4,2,16,640]{5,4,3,2,1,0:T(8,128)(2,1)S(1)}, u32[]{:S(2)}, u32[]{:S(2)}) collective-permute-start(bf16[1,2,4,2,16,640]{5,4,3,2,1,0:T(8,128)(2,1)S(1)} %get-tuple-element.23), channel_id=1, source_target_pairs={{8,0},{25,1},{136,128},{153,129},{10,2},{27,3},{138,130},{155,131}... | collective-permute-start | bytes 983048 | tf_op jit(solution)/shard_map/ppermute | solution.py:385
  37.7 7.3 %collective-permute-start.5 = (bf16[1,2,4,2,16,640]{5,4,3,2,1,0:T(8,128)(2,1)S(1)}, bf16[1,2,4,2,16,640]{5,4,3,2,1,0:T(8,128)(2,1)S(1)}, u32[]{:S(2)}, u32[]{:S(2)}) collective-permute-start(bf16[1,2,4,2,16,640]{5,4,3,2,1,0:T(8,128)(2,1)S(1)} %get-tuple-element.24), channel_id=1, source_target_pairs={{32,0},{97,1},{160,128},{225,129},{34,2},{99,3},{162,130},{227,131... | collective-permute-start | bytes 983048 | tf_op jit(solution)/shard_map/ppermute | solution.py:385
  44.9 5.5 %collective-permute-start.15 = (bf16[1,1,4,2,16,640]{5,4,3,2,1,0:T(8,128)(2,1)S(1)}, bf16[1,1,4,2,16,640]{5,4,3,2,1,0:T(8,128)(2,1)S(1)}, u32[]{:S(2)}, u32[]{:S(2)}) collective-permute-start(bf16[1,1,4,2,16,640]{5,4,3,2,1,0:T(8,128)(2,1)S(1)} %slice_select_fusion.2), channel_id=1, source_target_pairs={{8,0},{25,1},{136,128},{153,129},{10,2},{27,3},{138,130},{155,131}... | collective-permute-start | bytes 491528 | tf_op jit(solution)/shard_map/ppermute | solution.py:385
  45.0 8.0 %collective-permute-start.6 = (bf16[1,2,4,2,16,640]{5,4,3,2,1,0:T(8,128)(2,1)S(1)}, bf16[1,2,4,2,16,640]{5,4,3,2,1,0:T(8,128)(2,1)S(1)}, u32[]{:S(2)}, u32[]{:S(2)}) collective-permute-start(bf16[1,2,4,2,16,640]{5,4,3,2,1,0:T(8,128)(2,1)S(1)} %collective-permute-done.5), channel_id=1, source_target_pairs={{1,0},{0,1},{129,128},{128,129},{3,2},{2,3},{131,130},{130,131},{5... | collective-permute-start | bytes 983048 | tf_op jit(solution)/shard_map/ppermute | solution.py:385
  47.1 5.5 %collective-permute-start.7 = (bf16[1,1,4,2,16,640]{5,4,3,2,1,0:T(8,128)(2,1)S(1)}, bf16[1,1,4,2,16,640]{5,4,3,2,1,0:T(8,128)(2,1)S(1)}, u32[]{:S(2)}, u32[]{:S(2)}) collective-permute-start(bf16[1,1,4,2,16,640]{5,4,3,2,1,0:T(8,128)(2,1)S(1)} %slice_select_fusion.3), channel_id=1, source_target_pairs={{32,0},{97,1},{160,128},{225,129},{34,2},{99,3},{162,130},{227,131... | collective-permute-start | bytes 491528 | tf_op jit(solution)/shard_map/ppermute | solution.py:385
  48.5 7.0 %collective-permute-start.14 = (bf16[1,2,4,2,16,640]{5,4,3,2,1,0:T(8,128)(2,1)S(1)}, bf16[1,2,4,2,16,640]{5,4,3,2,1,0:T(8,128)(2,1)S(1)}, u32[]{:S(2)}, u32[]{:S(2)}) collective-permute-start(bf16[1,2,4,2,16,640]{5,4,3,2,1,0:T(8,128)(2,1)S(1)} %collective-permute-done.13), channel_id=1, source_target_pairs={{1,0},{0,1},{129,128},{128,129},{3,2},{2,3},{131,130},{130,131},{5... | collective-permute-start | bytes 983048 | tf_op jit(solution)/shard_map/ppermute | solution.py:385
  50.4 5.2 %collective-permute-start.16 = (bf16[1,1,4,2,16,640]{5,4,3,2,1,0:T(8,128)(2,1)S(1)}, bf16[1,1,4,2,16,640]{5,4,3,2,1,0:T(8,128)(2,1)S(1)}, u32[]{:S(2)}, u32[]{:S(2)}) collective-permute-start(bf16[1,1,4,2,16,640]{5,4,3,2,1,0:T(8,128)(2,1)S(1)} %collective-permute-done.15), channel_id=1, source_target_pairs={{1,0},{0,1},{129,128},{128,129},{3,2},{2,3},{131,130},{130,131},{5... | collective-permute-start | bytes 491528 | tf_op jit(solution)/shard_map/ppermute | solution.py:385
  52.6 1.4 collective-permute-start.8
  54.3 1.5 copy-start.1
  54.3 17.7 %collective-permute-start.9 = (bf16[4,2,4,2,16,640]{5,4,3,2,1,0:T(8,128)(2,1)S(1)}, bf16[4,2,4,2,16,640]{5,4,3,2,1,0:T(8,128)(2,1)S(1)}, u32[]{:S(2)}, u32[]{:S(2)}) collective-permute-start(bf16[4,2,4,2,16,640]{5,4,3,2,1,0:T(8,128)(2,1)S(1)} %pad_maximum_fusion.refs_0_), channel_id=1, source_target_pairs={{8,0},{25,1},{136,128},{153,129},{10,2},{27,3},{138,130},{155,131}... | collective-permute-start | bytes 3932168 | tf_op jit(solution)/shard_map/ppermute | solution.py:385
  55.8 20.0 %copy-start.3 = (bf16[4,2,4,2,16,640]{5,4,3,2,1,0:T(8,128)(2,1)}, bf16[4,2,4,2,16,640]{5,4,3,2,1,0:T(8,128)(2,1)S(1)}, u32[]{:S(2)}) copy-start(bf16[4,2,4,2,16,640]{5,4,3,2,1,0:T(8,128)(2,1)S(1)} %pad_maximum_fusion.1.refs_5_) | copy-start | bytes 3932164
  55.8 18.6 %collective-permute-start.17 = (bf16[4,2,4,2,16,640]{5,4,3,2,1,0:T(8,128)(2,1)S(1)}, bf16[4,2,4,2,16,640]{5,4,3,2,1,0:T(8,128)(2,1)}, u32[]{:S(2)}, u32[]{:S(2)}) collective-permute-start(bf16[4,2,4,2,16,640]{5,4,3,2,1,0:T(8,128)(2,1)S(1)} %pad_maximum_fusion.1.refs_5_), channel_id=1, source_target_pairs={{32,0},{97,1},{160,128},{225,129},{34,2},{99,3},{162,130},{227,131... | collective-permute-start | bytes 3932168 | tf_op jit(solution)/shard_map/ppermute | solution.py:385
  72.1 4.0 %copy-start.2 = (bf16[4,2,4,2,16,640]{5,4,3,2,1,0:T(8,128)(2,1)}, bf16[4,2,4,2,16,640]{5,4,3,2,1,0:T(8,128)(2,1)S(1)}, u32[]{:S(2)}) copy-start(bf16[4,2,4,2,16,640]{5,4,3,2,1,0:T(8,128)(2,1)S(1)} %collective-permute-done.9.refs_1_) | copy-start | bytes 3932164
  72.2 10.8 %collective-permute-start.11 = (bf16[4,1,4,2,16,640]{5,4,3,2,1,0:T(8,128)(2,1)S(1)}, bf16[4,1,4,2,16,640]{5,4,3,2,1,0:T(8,128)(2,1)}, u32[]{:S(2)}, u32[]{:S(2)}) collective-permute-start(bf16[4,1,4,2,16,640]{5,4,3,2,1,0:T(8,128)(2,1)S(1)} %slice_select_fusion.1), channel_id=1, source_target_pairs={{8,0},{25,1},{136,128},{153,129},{10,2},{27,3},{138,130},{155,131}... | collective-permute-start | bytes 1966088 | tf_op jit(solution)/shard_map/ppermute | solution.py:385
  75.8 11.0 %collective-permute-start.19 = (bf16[4,1,4,2,16,640]{5,4,3,2,1,0:T(8,128)(2,1)S(1)}, bf16[4,1,4,2,16,640]{5,4,3,2,1,0:T(8,128)(2,1)}, u32[]{:S(2)}, u32[]{:S(2)}) collective-permute-start(bf16[4,1,4,2,16,640]{5,4,3,2,1,0:T(8,128)(2,1)S(1)} %slice_select_fusion), channel_id=1, source_target_pairs={{32,0},{97,1},{160,128},{225,129},{34,2},{99,3},{162,130},{227,131... | collective-permute-start | bytes 1966088 | tf_op jit(solution)/shard_map/ppermute | solution.py:385
  76.1 13.7 %collective-permute-start.10 = (bf16[4,2,4,2,16,640]{5,4,3,2,1,0:T(8,128)(2,1)S(1)}, bf16[4,2,4,2,16,640]{5,4,3,2,1,0:T(8,128)(2,1)S(1)}, u32[]{:S(2)}, u32[]{:S(2)}) collective-permute-start(bf16[4,2,4,2,16,640]{5,4,3,2,1,0:T(8,128)(2,1)S(1)} %collective-permute-done.9.refs_1_), channel_id=1, source_target_pairs={{1,0},{0,1},{129,128},{128,129},{3,2},{2,3},{131,130},{130,131},{5... | collective-permute-start | bytes 3932168 | tf_op jit(solution)/shard_map/ppermute | solution.py:385
  81.1 10.2 %collective-permute-start.18 = (bf16[4,2,4,2,16,640]{5,4,3,2,1,0:T(8,128)(2,1)}, bf16[4,2,4,2,16,640]{5,4,3,2,1,0:T(8,128)(2,1)}, u32[]{:S(2)}, u32[]{:S(2)}) collective-permute-start(bf16[4,2,4,2,16,640]{5,4,3,2,1,0:T(8,128)(2,1)} %collective-permute-done.17.refs_6_), channel_id=1, source_target_pairs={{1,0},{0,1},{129,128},{128,129},{3,2},{2,3},{131,130},{130,131},{5... | collective-permute-start | bytes 3932168 | tf_op jit(solution)/shard_map/ppermute | solution.py:385
  83.0 6.8 %collective-permute-start.12 = (bf16[4,1,4,2,16,640]{5,4,3,2,1,0:T(8,128)(2,1)}, bf16[4,1,4,2,16,640]{5,4,3,2,1,0:T(8,128)(2,1)}, u32[]{:S(2)}, u32[]{:S(2)}) collective-permute-start(bf16[4,1,4,2,16,640]{5,4,3,2,1,0:T(8,128)(2,1)} %collective-permute-done.11.refs_3_), channel_id=1, source_target_pairs={{1,0},{0,1},{129,128},{128,129},{3,2},{2,3},{131,130},{130,131},{5... | collective-permute-start | bytes 1966088 | tf_op jit(solution)/shard_map/ppermute | solution.py:385
  86.8 4.5 %collective-permute-start.20 = (bf16[4,1,4,2,16,640]{5,4,3,2,1,0:T(8,128)(2,1)}, bf16[4,1,4,2,16,640]{5,4,3,2,1,0:T(8,128)(2,1)}, u32[]{:S(2)}, u32[]{:S(2)}) collective-permute-start(bf16[4,1,4,2,16,640]{5,4,3,2,1,0:T(8,128)(2,1)} %collective-permute-done.19.refs_8_), channel_id=1, source_target_pairs={{1,0},{0,1},{129,128},{128,129},{3,2},{2,3},{131,130},{130,131},{5... | collective-permute-start | bytes 1966088 | tf_op jit(solution)/shard_map/ppermute | solution.py:385
  89.8 1.5 copy-start.5
  151.9 2.4 %collective-permute-start.21 = (f32[32,40,128]{2,1,0:T(8,128)}, f32[32,40,128]{2,1,0:T(8,128)S(1)}, u32[]{:S(2)}, u32[]{:S(2)}) collective-permute-start(f32[32,40,128]{2,1,0:T(8,128)} %get-tuple-element.17.ends_ref), channel_id=1, source_target_pairs={{1,0},{0,1},{129,128},{128,129},{3,2},{2,3},{131,130},{130,131},{5... | collective-permute-start | bytes 1966088 | tf_op jit(solution)/shard_map/ppermute | solution.py:385
  154.3 0.9 copy-start.4
  155.2 8.0 %copy-start = (f32[24,64,128]{2,1,0:T(8,128)S(1)}, f32[24,64,128]{2,1,0:T(8,128)}, u32[]{:S(2)}) copy-start(f32[24,64,128]{2,1,0:T(8,128)} %get-tuple-element.18.par_ref) | copy-start | bytes 2359300
  158.1 17.8 %all-to-all-start = ((f32[16,40,128]{2,1,0:T(8,128)}), f32[16,40,128]{2,1,0:T(8,128)S(1)}, u32[]{:S(2)}, u32[]{:S(2)}) async-start(f32[16,40,128]{2,1,0:T(8,128)} %combine.1), calls=%async_computation | async-start | bytes 655360 | tf_op jit(solution)/shard_map/all_to_all | solution.py:430
  175.9 0.7 copy-start.6
  192.8 5.6 %copy-start.7 = (f32[16,32,128]{2,1,0:T(8,128)}, f32[16,32,128]{2,1,0:T(8,128)S(1)}, u32[]{:S(2)}) copy-start(f32[16,32,128]{2,1,0:T(8,128)S(1)} %all_to_all.10.hin_ref) | copy-start | bytes 786436
  192.8 5.6 %collective-permute-start.22 = (f32[16,32,128]{2,1,0:T(8,128)S(1)}, f32[16,32,128]{2,1,0:T(8,128)S(1)}, u32[]{:S(2)}, u32[]{:S(2)}) collective-permute-start(f32[16,32,128]{2,1,0:T(8,128)S(1)} %all_to_all.10.hin_ref), channel_id=1, source_target_pairs={{1,0},{0,1},{129,128},{128,129},{3,2},{2,3},{131,130},{130,131},{5... | collective-permute-start | bytes 786440 | tf_op jit(solution)/shard_map/ppermute | solution.py:385
  198.4 0.7 copy-start.8

commit v5 on v4

--- a/solution.py
+++ b/solution.py
@@ -36,13 +36,13 @@
 def piece_specs(pieces):
     specs = []
     for k, p in enumerate(pieces):
-        rest = (p.shape[1], p.shape[2], 1, *p.shape[4:])
+        rest = (p.shape[1], 1, *p.shape[3:])
         if k < len(pieces) // 2:
             specs.append(
-                pl.BlockSpec((1, *rest), lambda i, s: ((jnp.minimum(i, 7) - s[2]) & 3, 0, 0, jnp.minimum(i, 7) // 4, 0, 0))
+                pl.BlockSpec((1, *rest), lambda i, s: ((jnp.minimum(i, 7) - s[2]) & 3, 0, jnp.minimum(i, 7) // 4, 0, 0, 0))
             )
         else:
-            specs.append(pl.BlockSpec((4, *rest), lambda i, s: (0, 0, 0, jnp.minimum(i, 7) // 4, 0, 0)))
+            specs.append(pl.BlockSpec((4, *rest), lambda i, s: (0, 0, jnp.minimum(i, 7) // 4, 0, 0, 0)))
     return specs
 
 
@@ -56,8 +56,8 @@
     for j, ref in enumerate(piece_refs[:many]):
         at = (own_x + away[j]) & 3
         for core in range(ref.shape[1]):
-            for h in range(ref.shape[2]):
-                w_ref[at, h, first[j] + core, 0:half, :] = ref[0, core, h, 0]
+            for h in range(4):
+                w_ref[at, (0, 2, 1, 3)[h], first[j] + core, 0:half, :] = ref[0, core, 0, h]
     wanted = (step - own_y) & 3
     for j, ref in enumerate(piece_refs[many:]):
 
@@ -65,8 +65,8 @@
         def _(ref=ref, first=first[j]):
             for q in range(4):
                 for core in range(ref.shape[1]):
-                    for h in range(ref.shape[2]):
-                        w_ref[(own_x + q) & 3, h, first + core, half : 2 * half, :] = ref[q, core, h, 0]
+                    for h in range(4):
+                        w_ref[(own_x + q) & 3, (0, 2, 1, 3)[h], first + core, half : 2 * half, :] = ref[q, core, 0, h]
 
 
 def scan_kernel(info_ref, x_ref, rim_ref, *refs):
@@ -286,8 +286,28 @@
     )(ends, alog)
 
 
+def factor_kernel(info_ref, z_ref, out_ref):
+    keep = lax.broadcasted_iota(jnp.int32, z_ref.shape, 0) < info_ref[0]
+    z = z_ref[...].astype(jnp.float32)
+    out_ref[...] = jnp.where(keep, z * sigmoid(z), 0.0)
+
+
+def gate_factor(info, z):
+    tok, chans = z.shape
+    columns = pl.BlockSpec((tok, WIDE), lambda i, *_: (0, i))
+    return pl.pallas_call(
+        factor_kernel,
+        grid_spec=pltpu.PrefetchScalarGridSpec(
+            num_scalar_prefetch=1, grid=(chans // WIDE,), in_specs=[columns], out_specs=columns
+        ),
+        out_shape=jax.ShapeDtypeStruct((tok, chans), jnp.float32),
+        compiler_params=settings(),
+        name="gate_factor",
+    )(info, z)
+
+
 def gate_kernel(
-    info_ref, y_ref, cum_ref, hin_ref, hin_too_ref, other_ref, par_ref, act_ref, z_ref, c_ref, out_ref, y_scr, a_scr, h_scr, e_scr
+    info_ref, y_ref, cum_ref, hin_ref, hin_too_ref, other_ref, par_ref, act_ref, factor_ref, c_ref, out_ref, y_scr, a_scr, h_scr, e_scr
 ):
     tok = act_ref.shape[0]
     states = a_scr.shape[0]
@@ -328,16 +348,14 @@
         return carry
 
     lax.fori_loop(0, tok // 8, block, 0)
-    keep = lax.broadcasted_iota(jnp.int32, (tok, LANES), 0) < info_ref[0]
     for g in range(ROWS):
         cols = slice(g * LANES, (g + 1) * LANES)
         y = y_scr[:, g * 8 : (g + 1) * 8, :].reshape(tok, LANES)
-        z = z_ref[:, cols].astype(jnp.float32)
-        out = (y + par_ref[6, g : g + 1, :] * act_ref[:, cols].astype(jnp.float32)) * (z * sigmoid(z))
-        out_ref[:, cols] = jnp.where(keep, out, 0.0).astype(jnp.bfloat16)
-
-
-def gate_pass(info, y, cum, hin, hin_too, other, pars, act, z, c_wide):
+        direct = par_ref[6, g : g + 1, :] * act_ref[:, cols].astype(jnp.float32)
+        out_ref[:, cols] = ((y + direct) * factor_ref[:, cols]).astype(jnp.bfloat16)
+
+
+def gate_pass(info, y, cum, hin, hin_too, other, pars, act, factor, c_wide):
     tok, chans = act.shape
     states = c_wide.shape[0] // tok
     columns = pl.BlockSpec((tok, WIDE), lambda i, *_: (0, i))
@@ -368,7 +386,7 @@
         out_shape=jax.ShapeDtypeStruct((tok, chans), jnp.bfloat16),
         compiler_params=settings(),
         name="gate_pass",
-    )(info, y, cum, hin, hin_too, other, pars, act, z, c_wide)
+    )(info, y, cum, hin, hin_too, other, pars, act, factor, c_wide)
 
 
 def device(x, y, z, core):
@@ -460,15 +478,16 @@
     fill = -(xproj_weight.shape[1] + 3 * count + rank) % LANES
     parts += [jnp.zeros((width, fill), jnp.bfloat16), dtproj_weight.T]
     mats = jnp.concatenate([xproj_weight, *parts], axis=1)[None]
-    mats, rim = lax.optimization_barrier((double(mats, "z", 1, own_z), rim))
-    for axis, bit in (("z", 2), ("z", 4), ("core", 1)):
+    mats, rim = lax.optimization_barrier((double(mats, "z", 4, own_z), rim))
+    for axis, bit in (("z", 2), ("z", 1), ("core", 1)):
         mats = double(mats, axis, bit, own[axis])
-    mats = mats.reshape(1, 2, 4, 2, *mats.shape[1:])
+    mats = mats.reshape(1, 2, 2, 4, *mats.shape[1:])
     upper = row_of_four(mats[..., : width // 2, :], "y", own_core)
     lower = row_of_four(mats[..., width // 2 :, :], "x", own_core)
+    nears = fetch(upper, onward("x")), fetch(lower, onward("y"))
+    *nears, factor = lax.optimization_barrier((*nears, gate_factor(info, z)))
     pieces = []
-    for value, axis in ((upper, "x"), (lower, "y")):
-        near = fetch(value, onward(axis))
+    for value, near, axis in ((upper, nears[0], "x"), (lower, nears[1], "y")):
         far = farther(near, axis, own_core)
         pieces += [value, near, swap(near), far, swap(far)]
 
@@ -479,7 +498,7 @@
     mine = lax.dynamic_slice_in_dim(pars[VECTORS : VECTORS + states], place, 2, axis=1).reshape(2 * states, LANES)
     chip = exchange(chip)
     hin = exchange(prefix(chip, mine))
-    out = gate_pass(info, y, cum, hin, swap(hin), other, pars, act, z, c_wide)
+    out = gate_pass(info, y, cum, hin, swap(hin), other, pars, act, factor, c_wide)
     return out[None]
 
 

time: 237 us -> 238 us (level)
  waiting for transfers between devices: 64.2 us -> 50.3 us
  Pallas kernels: 102 us -> 108 us
  blocking collectives: 14.4 us -> 17.3 us
  starting transfers between devices: 43.3 us -> 46.1 us
    ppermute x22, waiting for transfers between devices: 50.9 us -> 36.9 us  [fetch(): return lax.ppermute(value, ('group', 'ctx'), route)]
    pallas_call x0 -> x1, Pallas kernels: none -> 8.78 us  [gate_factor(): pl.pallas_call(factor_kernel, grid_spec=pltpu.PrefetchScalarGridSpec(num_...]
    ppermute x22, starting transfers between devices: 32.5 us -> 38.7 us  [fetch(): return lax.ppermute(value, ('group', 'ctx'), route)]
    all_to_all x1, blocking collectives: 14.4 us -> 17.3 us  [exchange(): lax.all_to_all(value, 'ctx', split_axis=0, concat_axis=0, tiled=True, axi...]
  transfers between devices with their start and end apart: 24 -> 24, of which waited for: 16 -> 14; matrix products, arithmetic and copies ran while one was open for 2% -> 2% of each run, Pallas kernels for 0% -> 4%
where the time goes in v5:
time: 238 us; the launch traced here: 237 us
  Pallas kernels  108 us (45%)
  waiting for transfers between devices  50.3 us (21%)
  starting transfers between devices  46.1 us (19%)
  blocking collectives  17.3 us (7%)
  local copies, waits for them, and re-layouts  8.71 us (4%)
  other arithmetic  5.15 us (2%)
    pallas_call x1, Pallas kernels, scan_pass(): pl.pallas_call(scan_kernel, grid_spec=pltpu.PrefetchScalarGridSpec(num_sc...  60.4 us
    ppermute x22, starting transfers between devices, fetch(): return lax.ppermute(value, ('group', 'ctx'), route)  38.7 us
    ppermute x22, waiting for transfers between devices, fetch(): return lax.ppermute(value, ('group', 'ctx'), route)  36.9 us
    pallas_call x1, Pallas kernels, gate_pass(): pl.pallas_call(gate_kernel, grid_spec=pltpu.PrefetchScalarGridSpec(num_sc...  34.3 us
    all_to_all x1, blocking collectives, exchange(): lax.all_to_all(value, 'ctx', split_axis=0, concat_axis=0, tiled=True, axi...  17.3 us
    all_to_all x1, waiting for transfers between devices, exchange(): lax.all_to_all(value, 'ctx', split_axis=0, concat_axis=0, tiled=True, axi...  12.2 us
    pallas_call x1, Pallas kernels, gate_factor(): pl.pallas_call(factor_kernel, grid_spec=pltpu.PrefetchScalarGridSpec(num_...  8.78 us
  transfers between devices with their start and end apart: 24, of which 14 were waited for; matrix products, arithmetic and copies ran while one was open for 2% of the time, Pallas kernels for 4%

profile of v5, /device:TPU:1, one launch (start us, length us, event | category | flops | bytes accessed | tf_op | source)
XLA Modules:
  0.0 236.8 jit_solution(9633045457633749120)
XLA Ops:
  0.0 0.7 slice.42
  0.7 1.5 concatenate.33
  2.5 0.8 concatenate.34
  3.3 7.8 %collective-permute-start = (bf16[1,32,640]{2,1,0:T(8,128)(2,1)S(1)}, bf16[1,32,640]{2,1,0:T(8,128)(2,1)S(1)}, u32[]{:S(2)}, u32[]{:S(2)}) collective-permute-start(bf16[1,32,640]{2,1,0:T(8,128)(2,1)S(1)} %bitcast.31), channel_id=1, source_target_pairs={{4,0},{5,1},{132,128},{133,129},{6,2},{7,3},{134,130},{135,131},{0... | collective-permute-start | bytes 122888 | tf_op jit(solution)/shard_map/ppermute | solution.py:403
  11.8 1.0 bitcast_select_fusion
  12.8 3.9 %collective-permute-start.1 = (bf16[3,8192]{1,0:T(4,128)(2,1)S(1)}, bf16[3,8192]{1,0:T(4,128)(2,1)S(1)}, u32[]{:S(2)}, u32[]{:S(2)}) collective-permute-start(bf16[3,8192]{1,0:T(4,128)(2,1)S(1)} %bitcast_select_fusion), channel_id=1, source_target_pairs={{0,1},{1,2},{2,3},{3,4},{4,5},{5,6},{6,7},{7,8},{8,9},{9,10},{10,1... | collective-permute-start | bytes 147464 | tf_op jit(solution)/shard_map/ppermute | solution.py:469
  16.8 1.2 collective-permute-done.1
  18.1 0.7 concatenate.36.rim_ref
  18.8 5.6 %collective-permute-done.2 = bf16[2,32,640]{2,1,0:T(8,128)(2,1)S(1)} collective-permute-done((bf16[2,32,640]{2,1,0:T(8,128)(2,1)S(1)}, bf16[2,32,640]{2,1,0:T(8,128)(2,1)S(1)}, u32[]{:S(2)}, u32[]{:S(2)}) %collective-permute-start.2) | collective-permute-done | bytes 81952 | tf_op jit(solution)/shard_map/ppermute | solution.py:403
  24.6 4.2 %collective-permute-done.3 = bf16[4,32,640]{2,1,0:T(8,128)(2,1)S(1)} collective-permute-done((bf16[4,32,640]{2,1,0:T(8,128)(2,1)S(1)}, bf16[4,32,640]{2,1,0:T(8,128)(2,1)S(1)}, u32[]{:S(2)}, u32[]{:S(2)}) %collective-permute-start.3) | collective-permute-done | bytes 163872 | tf_op jit(solution)/shard_map/ppermute | solution.py:403
  28.8 3.1 %collective-permute-start.4 = (bf16[8,32,640]{2,1,0:T(8,128)(2,1)S(1)}, bf16[8,32,640]{2,1,0:T(8,128)(2,1)S(1)}, u32[]{:S(2)}, u32[]{:S(2)}) collective-permute-start(bf16[8,32,640]{2,1,0:T(8,128)(2,1)S(1)} %pad_maximum_fusion.3), channel_id=1, source_target_pairs={{1,0},{0,1},{129,128},{128,129},{3,2},{2,3},{131,130},{130,131},{5... | collective-permute-start | bytes 983048 | tf_op jit(solution)/shard_map/ppermute | solution.py:403
  31.9 1.3 collective-permute-done.4
  33.4 3.6 %collective-permute-start.10 = (bf16[1,2,2,4,16,640]{5,4,3,2,1,0:T(8,128)(2,1)S(1)}, bf16[1,2,2,4,16,640]{5,4,3,2,1,0:T(8,128)(2,1)S(1)}, u32[]{:S(2)}, u32[]{:S(2)}) collective-permute-start(bf16[1,2,2,4,16,640]{5,4,3,2,1,0:T(8,128)(2,1)S(1)} %get-tuple-element.29), channel_id=1, source_target_pairs={{8,0},{25,1},{136,128},{153,129},{10,2},{27,3},{138,130},{155,131}... | collective-permute-start | bytes 983048 | tf_op jit(solution)/shard_map/ppermute | solution.py:403
  37.0 1.3 collective-permute-start.5
  38.3 4.4 %collective-permute-done.10 = bf16[1,2,2,4,16,640]{5,4,3,2,1,0:T(8,128)(2,1)S(1)} collective-permute-done((bf16[1,2,2,4,16,640]{5,4,3,2,1,0:T(8,128)(2,1)S(1)}, bf16[1,2,2,4,16,640]{5,4,3,2,1,0:T(8,128)(2,1)S(1)}, u32[]{:S(2)}, u32[]{:S(2)}) %collective-permute-start.10) | collective-permute-done | bytes 327712 | tf_op jit(solution)/shard_map/ppermute | solution.py:403
  43.4 4.0 %collective-permute-start.11 = (bf16[1,2,2,4,16,640]{5,4,3,2,1,0:T(8,128)(2,1)S(1)}, bf16[1,2,2,4,16,640]{5,4,3,2,1,0:T(8,128)(2,1)S(1)}, u32[]{:S(2)}, u32[]{:S(2)}) collective-permute-start(bf16[1,2,2,4,16,640]{5,4,3,2,1,0:T(8,128)(2,1)S(1)} %collective-permute-done.10), channel_id=1, source_target_pairs={{1,0},{0,1},{129,128},{128,129},{3,2},{2,3},{131,130},{130,131},{5... | collective-permute-start | bytes 983048 | tf_op jit(solution)/shard_map/ppermute | solution.py:403
  47.4 1.4 collective-permute-start.7
  48.7 2.2 collective-permute-start.13
  51.0 1.9 collective-permute-done.7
  52.9 0.9 collective-permute-start.8
  53.9 0.9 collective-permute-done.8
  55.2 1.4 pad_maximum_fusion.1.refs_5_
  56.6 0.8 collective-permute-start.14
  57.4 0.6 pad_add_fusion.info_ref
  58.0 8.8 %gate_factor.1.factor_ref = f32[256,8192]{1,0:T(8,128)} custom-call(s32[4]{0:T(128)} %pad_add_fusion.info_ref, bf16[256,8192]{1,0:T(8,128)(2,1)} %bitcast.29), custom_call_target="tpu_custom_call" | custom-call | tf_op jit(solution)/shard_map/gate_factor/pallas_call | solution.py:298
  66.7 6.1 %collective-permute-done.9.refs_1_ = bf16[4,2,2,4,16,640]{5,4,3,2,1,0:T(8,128)(2,1)S(1)} collective-permute-done((bf16[4,2,2,4,16,640]{5,4,3,2,1,0:T(8,128)(2,1)S(1)}, bf16[4,2,2,4,16,640]{5,4,3,2,1,0:T(8,128)(2,1)S(1)}, u32[]{:S(2)}, u32[]{:S(2)}) %collective-permute-start.9) | collective-permute-done | bytes 1310752 | tf_op jit(solution)/shard_map/ppermute | solution.py:403
  72.8 2.5 %collective-permute-done.14.refs_6_ = bf16[4,2,2,4,16,640]{5,4,3,2,1,0:T(8,128)(2,1)} collective-permute-done((bf16[4,2,2,4,16,640]{5,4,3,2,1,0:T(8,128)(2,1)}, bf16[4,2,2,4,16,640]{5,4,3,2,1,0:T(8,128)(2,1)}, u32[]{:S(2)}, u32[]{:S(2)}) %collective-permute-start.14) | collective-permute-done | bytes 1310752 | tf_op jit(solution)/shard_map/ppermute | solution.py:403
  75.3 1.4 slice_select_fusion
  77.1 5.1 %collective-permute-start.15 = (bf16[4,2,2,4,16,640]{5,4,3,2,1,0:T(8,128)(2,1)S(1)}, bf16[4,2,2,4,16,640]{5,4,3,2,1,0:T(8,128)(2,1)S(1)}, u32[]{:S(2)}, u32[]{:S(2)}) collective-permute-start(bf16[4,2,2,4,16,640]{5,4,3,2,1,0:T(8,128)(2,1)S(1)} %collective-permute-done.9.refs_1_), channel_id=1, source_target_pairs={{1,0},{0,1},{129,128},{128,129},{3,2},{2,3},{131,130},{130,131},{5... | collective-permute-start | bytes 3932168 | tf_op jit(solution)/shard_map/ppermute | solution.py:403
  82.2 5.2 %collective-permute-done.19.refs_8_ = bf16[4,1,2,4,16,640]{5,4,3,2,1,0:T(8,128)(2,1)S(1)} collective-permute-done((bf16[4,1,2,4,16,640]{5,4,3,2,1,0:T(8,128)(2,1)S(1)}, bf16[4,1,2,4,16,640]{5,4,3,2,1,0:T(8,128)(2,1)S(1)}, u32[]{:S(2)}, u32[]{:S(2)}) %collective-permute-start.19) | collective-permute-done | bytes 655392 | tf_op jit(solution)/shard_map/ppermute | solution.py:403
  87.4 2.0 collective-permute-start.20
  89.5 2.8 %collective-permute-start.17 = (bf16[4,1,2,4,16,640]{5,4,3,2,1,0:T(8,128)(2,1)S(1)}, bf16[4,1,2,4,16,640]{5,4,3,2,1,0:T(8,128)(2,1)S(1)}, u32[]{:S(2)}, u32[]{:S(2)}) collective-permute-start(bf16[4,1,2,4,16,640]{5,4,3,2,1,0:T(8,128)(2,1)S(1)} %collective-permute-done.16.refs_3_), channel_id=1, source_target_pairs={{1,0},{0,1},{129,128},{128,129},{3,2},{2,3},{131,130},{130,131},{5... | collective-permute-start | bytes 1966088 | tf_op jit(solution)/shard_map/ppermute | solution.py:403
  92.3 1.7 collective-permute-done.17.refs_4_
  94.1 0.8 copy-done.11
  95.7 60.4 %scan_pass.1 = (bf16[256,8192]{1,0:T(8,128)(2,1)}, f32[24,64,128]{2,1,0:T(8,128)}, f32[256,64,128]{2,1,0:T(8,128)}, f32[256,64,128]{2,1,0:T(8,128)}, f32[32,40,128]{2,1,0:T(8,128)}, /*index=5*/f32[4096,128]{1,0:T(8,128)}) custom-call(s32[4]{0:T(128)} %pad_add_fusion.info_ref, bf16[256,8192]{1,0:T(8,128)(2,1)} %bitcast.28, ...), custom_call_target="tpu_custom_call" | custom-call | tf_op jit(solution)/shard_map/scan_pass/pallas_call | solution.py:190
  156.6 1.9 collective-permute-done.21.other_ref
  158.6 0.9 copy-done.3
  159.4 2.9 %combine.1 = f32[16,40,128]{2,1,0:T(8,128)} custom-call(s32[4]{0:T(128)} %pad_add_fusion.info_ref, f32[32,40,128]{2,1,0:T(8,128)} %get-tuple-element.22.ends_ref, f32[32,40,128]{2,1,0:T(8,128)} %copy-done.3, f32[24,64,128]{2,1,0:T(8,128)} %get-tuple-element.23.par_ref), custom_call_target="tpu_custom_call" | custom-call | tf_op jit(solution)/shard_map/combine/pallas_call | solution.py:254
  162.3 3.5 %all-to-all-start = ((f32[16,40,128]{2,1,0:T(8,128)}), f32[16,40,128]{2,1,0:T(8,128)S(1)}, u32[]{:S(2)}, u32[]{:S(2)}) async-start(f32[16,40,128]{2,1,0:T(8,128)} %combine.1), calls=%async_computation | async-start | bytes 655360 | tf_op jit(solution)/shard_map/all_to_all | solution.py:448
  166.0 0.6 constant_dynamic-slice_fusion
  166.6 12.2 %all-to-all-done.end_ref = f32[16,40,128]{2,1,0:T(8,128)S(1)} async-done(((f32[16,40,128]{2,1,0:T(8,128)}), f32[16,40,128]{2,1,0:T(8,128)S(1)}, u32[]{:S(2)}, u32[]{:S(2)}) %all-to-all-start) | async-done | bytes 327712 | tf_op jit(solution)/shard_map/all_to_all | solution.py:448
  178.7 0.7 copy-done.6
  179.5 1.7 prefix.1
  181.2 17.3 %all_to_all.10.hin_ref = f32[16,32,128]{2,1,0:T(8,128)S(1)} all-to-all(f32[16,32,128]{2,1,0:T(8,128)} %prefix.1), channel_id=1, replica_groups={{0,2,4,6,8,10,12,14,16,18,20,22,24,26,28,30},{1,3,5,7,9,11,13,15,17,19,..., dimensions={0} | all-to-all | bytes 524288 | tf_op jit(solution)/shard_map/all_to_all | solution.py:448
  198.5 2.1 collective-permute-start.22
  200.6 1.2 collective-permute-done.22.hin_too_ref
  201.7 0.7 copy-done.12
  202.4 34.3 %gate_pass.1 = bf16[256,8192]{1,0:T(8,128)(2,1)} custom-call(s32[4]{0:T(128)} %pad_add_fusion.info_ref, f32[256,64,128]{2,1,0:T(8,128)} %get-tuple-element.20.y_ref, f32[256,64,128]{2,1,0:T(8,128)} %get-tuple-element.21.cum_ref, f32[16,32,128]{2,1,0:T(8,128)} %copy-done.7, f32[16,32,128]{2,1,0:T(8,128)} %copy-done.12, f32[32,40,128]{2,1,0:T(8,128)} %copy-done.3, ...), custom_call_target="tpu_custom_call" | custom-call | tf_op jit(solution)/shard_map/gate_pass/pallas_call | solution.py:362
  (64 shorter events, 3.7 us)
Async XLA Ops:
  3.3 13.5 %collective-permute-start = (bf16[1,32,640]{2,1,0:T(8,128)(2,1)S(1)}, bf16[1,32,640]{2,1,0:T(8,128)(2,1)S(1)}, u32[]{:S(2)}, u32[]{:S(2)}) collective-permute-start(bf16[1,32,640]{2,1,0:T(8,128)(2,1)S(1)} %bitcast.31), channel_id=1, source_target_pairs={{4,0},{5,1},{132,128},{133,129},{6,2},{7,3},{134,130},{135,131},{0... | collective-permute-start | bytes 122888 | tf_op jit(solution)/shard_map/ppermute | solution.py:403
  12.8 5.3 %collective-permute-start.1 = (bf16[3,8192]{1,0:T(4,128)(2,1)S(1)}, bf16[3,8192]{1,0:T(4,128)(2,1)S(1)}, u32[]{:S(2)}, u32[]{:S(2)}) collective-permute-start(bf16[3,8192]{1,0:T(4,128)(2,1)S(1)} %bitcast_select_fusion), channel_id=1, source_target_pairs={{0,1},{1,2},{2,3},{3,4},{4,5},{5,6},{6,7},{7,8},{8,9},{9,10},{10,1... | collective-permute-start | bytes 147464 | tf_op jit(solution)/shard_map/ppermute | solution.py:469
  18.8 5.6 %collective-permute-start.2 = (bf16[2,32,640]{2,1,0:T(8,128)(2,1)S(1)}, bf16[2,32,640]{2,1,0:T(8,128)(2,1)S(1)}, u32[]{:S(2)}, u32[]{:S(2)}) collective-permute-start(bf16[2,32,640]{2,1,0:T(8,128)(2,1)S(1)} %pad_maximum_fusion.5), channel_id=1, source_target_pairs={{2,0},{3,1},{130,128},{131,129},{0,2},{1,3},{128,130},{129,131},{6... | collective-permute-start | bytes 245768 | tf_op jit(solution)/shard_map/ppermute | solution.py:403
  24.5 4.3 %collective-permute-start.3 = (bf16[4,32,640]{2,1,0:T(8,128)(2,1)S(1)}, bf16[4,32,640]{2,1,0:T(8,128)(2,1)S(1)}, u32[]{:S(2)}, u32[]{:S(2)}) collective-permute-start(bf16[4,32,640]{2,1,0:T(8,128)(2,1)S(1)} %pad_maximum_fusion.4), channel_id=1, source_target_pairs={{128,0},{129,1},{0,128},{1,129},{130,2},{131,3},{2,130},{3,131},{1... | collective-permute-start | bytes 491528 | tf_op jit(solution)/shard_map/ppermute | solution.py:403
  28.8 4.4 %collective-permute-start.4 = (bf16[8,32,640]{2,1,0:T(8,128)(2,1)S(1)}, bf16[8,32,640]{2,1,0:T(8,128)(2,1)S(1)}, u32[]{:S(2)}, u32[]{:S(2)}) collective-permute-start(bf16[8,32,640]{2,1,0:T(8,128)(2,1)S(1)} %pad_maximum_fusion.3), channel_id=1, source_target_pairs={{1,0},{0,1},{129,128},{128,129},{3,2},{2,3},{131,130},{130,131},{5... | collective-permute-start | bytes 983048 | tf_op jit(solution)/shard_map/ppermute | solution.py:403
  33.4 9.3 %collective-permute-start.10 = (bf16[1,2,2,4,16,640]{5,4,3,2,1,0:T(8,128)(2,1)S(1)}, bf16[1,2,2,4,16,640]{5,4,3,2,1,0:T(8,128)(2,1)S(1)}, u32[]{:S(2)}, u32[]{:S(2)}) collective-permute-start(bf16[1,2,2,4,16,640]{5,4,3,2,1,0:T(8,128)(2,1)S(1)} %get-tuple-element.29), channel_id=1, source_target_pairs={{8,0},{25,1},{136,128},{153,129},{10,2},{27,3},{138,130},{155,131}... | collective-permute-start | bytes 983048 | tf_op jit(solution)/shard_map/ppermute | solution.py:403
  37.0 10.3 %collective-permute-start.5 = (bf16[1,2,2,4,16,640]{5,4,3,2,1,0:T(8,128)(2,1)S(1)}, bf16[1,2,2,4,16,640]{5,4,3,2,1,0:T(8,128)(2,1)S(1)}, u32[]{:S(2)}, u32[]{:S(2)}) collective-permute-start(bf16[1,2,2,4,16,640]{5,4,3,2,1,0:T(8,128)(2,1)S(1)} %get-tuple-element.30), channel_id=1, source_target_pairs={{32,0},{97,1},{160,128},{225,129},{34,2},{99,3},{162,130},{227,131... | collective-permute-start | bytes 983048 | tf_op jit(solution)/shard_map/ppermute | solution.py:403
  42.8 6.0 %collective-permute-start.12 = (bf16[1,1,2,4,16,640]{5,4,3,2,1,0:T(8,128)(2,1)S(1)}, bf16[1,1,2,4,16,640]{5,4,3,2,1,0:T(8,128)(2,1)S(1)}, u32[]{:S(2)}, u32[]{:S(2)}) collective-permute-start(bf16[1,1,2,4,16,640]{5,4,3,2,1,0:T(8,128)(2,1)S(1)} %slice_select_fusion.2), channel_id=1, source_target_pairs={{8,0},{25,1},{136,128},{153,129},{10,2},{27,3},{138,130},{155,131}... | collective-permute-start | bytes 491528 | tf_op jit(solution)/shard_map/ppermute | solution.py:403
  43.4 10.5 %collective-permute-start.11 = (bf16[1,2,2,4,16,640]{5,4,3,2,1,0:T(8,128)(2,1)S(1)}, bf16[1,2,2,4,16,640]{5,4,3,2,1,0:T(8,128)(2,1)S(1)}, u32[]{:S(2)}, u32[]{:S(2)}) collective-permute-start(bf16[1,2,2,4,16,640]{5,4,3,2,1,0:T(8,128)(2,1)S(1)} %collective-permute-done.10), channel_id=1, source_target_pairs={{1,0},{0,1},{129,128},{128,129},{3,2},{2,3},{131,130},{130,131},{5... | collective-permute-start | bytes 983048 | tf_op jit(solution)/shard_map/ppermute | solution.py:403
  47.3 6.5 %collective-permute-start.6 = (bf16[1,2,2,4,16,640]{5,4,3,2,1,0:T(8,128)(2,1)S(1)}, bf16[1,2,2,4,16,640]{5,4,3,2,1,0:T(8,128)(2,1)S(1)}, u32[]{:S(2)}, u32[]{:S(2)}) collective-permute-start(bf16[1,2,2,4,16,640]{5,4,3,2,1,0:T(8,128)(2,1)S(1)} %collective-permute-done.5), channel_id=1, source_target_pairs={{1,0},{0,1},{129,128},{128,129},{3,2},{2,3},{131,130},{130,131},{5... | collective-permute-start | bytes 983048 | tf_op jit(solution)/shard_map/ppermute | solution.py:403
  47.4 5.5 %collective-permute-start.7 = (bf16[1,1,2,4,16,640]{5,4,3,2,1,0:T(8,128)(2,1)S(1)}, bf16[1,1,2,4,16,640]{5,4,3,2,1,0:T(8,128)(2,1)S(1)}, u32[]{:S(2)}, u32[]{:S(2)}) collective-permute-start(bf16[1,1,2,4,16,640]{5,4,3,2,1,0:T(8,128)(2,1)S(1)} %slice_select_fusion.3), channel_id=1, source_target_pairs={{32,0},{97,1},{160,128},{225,129},{34,2},{99,3},{162,130},{227,131... | collective-permute-start | bytes 491528 | tf_op jit(solution)/shard_map/ppermute | solution.py:403
  48.7 6.4 %collective-permute-start.13 = (bf16[1,1,2,4,16,640]{5,4,3,2,1,0:T(8,128)(2,1)S(1)}, bf16[1,1,2,4,16,640]{5,4,3,2,1,0:T(8,128)(2,1)S(1)}, u32[]{:S(2)}, u32[]{:S(2)}) collective-permute-start(bf16[1,1,2,4,16,640]{5,4,3,2,1,0:T(8,128)(2,1)S(1)} %collective-permute-done.12), channel_id=1, source_target_pairs={{1,0},{0,1},{129,128},{128,129},{3,2},{2,3},{131,130},{130,131},{5... | collective-permute-start | bytes 491528 | tf_op jit(solution)/shard_map/ppermute | solution.py:403
  52.9 1.9 collective-permute-start.8
  55.1 1.5 copy-start.1
  55.1 17.7 %collective-permute-start.9 = (bf16[4,2,2,4,16,640]{5,4,3,2,1,0:T(8,128)(2,1)S(1)}, bf16[4,2,2,4,16,640]{5,4,3,2,1,0:T(8,128)(2,1)S(1)}, u32[]{:S(2)}, u32[]{:S(2)}) collective-permute-start(bf16[4,2,2,4,16,640]{5,4,3,2,1,0:T(8,128)(2,1)S(1)} %pad_maximum_fusion.refs_0_), channel_id=1, source_target_pairs={{8,0},{25,1},{136,128},{153,129},{10,2},{27,3},{138,130},{155,131}... | collective-permute-start | bytes 3932168 | tf_op jit(solution)/shard_map/ppermute | solution.py:403
  56.6 18.7 %collective-permute-start.14 = (bf16[4,2,2,4,16,640]{5,4,3,2,1,0:T(8,128)(2,1)}, bf16[4,2,2,4,16,640]{5,4,3,2,1,0:T(8,128)(2,1)}, u32[]{:S(2)}, u32[]{:S(2)}) collective-permute-start(bf16[4,2,2,4,16,640]{5,4,3,2,1,0:T(8,128)(2,1)} %pad_maximum_fusion.1.refs_5_), channel_id=1, source_target_pairs={{32,0},{97,1},{160,128},{225,129},{34,2},{99,3},{162,130},{227,131... | collective-permute-start | bytes 3932168 | tf_op jit(solution)/shard_map/ppermute | solution.py:403
  72.8 4.3 %copy-start.2 = (bf16[4,2,2,4,16,640]{5,4,3,2,1,0:T(8,128)(2,1)}, bf16[4,2,2,4,16,640]{5,4,3,2,1,0:T(8,128)(2,1)S(1)}, u32[]{:S(2)}) copy-start(bf16[4,2,2,4,16,640]{5,4,3,2,1,0:T(8,128)(2,1)S(1)} %collective-permute-done.9.refs_1_) | copy-start | bytes 3932164
  76.7 10.7 %collective-permute-start.19 = (bf16[4,1,2,4,16,640]{5,4,3,2,1,0:T(8,128)(2,1)S(1)}, bf16[4,1,2,4,16,640]{5,4,3,2,1,0:T(8,128)(2,1)S(1)}, u32[]{:S(2)}, u32[]{:S(2)}) collective-permute-start(bf16[4,1,2,4,16,640]{5,4,3,2,1,0:T(8,128)(2,1)S(1)} %slice_select_fusion), channel_id=1, source_target_pairs={{32,0},{97,1},{160,128},{225,129},{34,2},{99,3},{162,130},{227,131... | collective-permute-start | bytes 1966088 | tf_op jit(solution)/shard_map/ppermute | solution.py:403
  76.9 12.6 %collective-permute-start.16 = (bf16[4,1,2,4,16,640]{5,4,3,2,1,0:T(8,128)(2,1)S(1)}, bf16[4,1,2,4,16,640]{5,4,3,2,1,0:T(8,128)(2,1)S(1)}, u32[]{:S(2)}, u32[]{:S(2)}) collective-permute-start(bf16[4,1,2,4,16,640]{5,4,3,2,1,0:T(8,128)(2,1)S(1)} %slice_select_fusion.1), channel_id=1, source_target_pairs={{8,0},{25,1},{136,128},{153,129},{10,2},{27,3},{138,130},{155,131}... | collective-permute-start | bytes 1966088 | tf_op jit(solution)/shard_map/ppermute | solution.py:403
  77.1 16.9 %collective-permute-start.15 = (bf16[4,2,2,4,16,640]{5,4,3,2,1,0:T(8,128)(2,1)S(1)}, bf16[4,2,2,4,16,640]{5,4,3,2,1,0:T(8,128)(2,1)S(1)}, u32[]{:S(2)}, u32[]{:S(2)}) collective-permute-start(bf16[4,2,2,4,16,640]{5,4,3,2,1,0:T(8,128)(2,1)S(1)} %collective-permute-done.9.refs_1_), channel_id=1, source_target_pairs={{1,0},{0,1},{129,128},{128,129},{3,2},{2,3},{131,130},{130,131},{5... | collective-permute-start | bytes 3932168 | tf_op jit(solution)/shard_map/ppermute | solution.py:403
  82.2 11.8 %collective-permute-start.18 = (bf16[4,2,2,4,16,640]{5,4,3,2,1,0:T(8,128)(2,1)}, bf16[4,2,2,4,16,640]{5,4,3,2,1,0:T(8,128)(2,1)S(1)}, u32[]{:S(2)}, u32[]{:S(2)}) collective-permute-start(bf16[4,2,2,4,16,640]{5,4,3,2,1,0:T(8,128)(2,1)} %collective-permute-done.14.refs_6_), channel_id=1, source_target_pairs={{1,0},{0,1},{129,128},{128,129},{3,2},{2,3},{131,130},{130,131},{5... | collective-permute-start | bytes 3932168 | tf_op jit(solution)/shard_map/ppermute | solution.py:403
  87.4 6.6 %copy-start.8 = (bf16[4,1,2,4,16,640]{5,4,3,2,1,0:T(8,128)(2,1)}, bf16[4,1,2,4,16,640]{5,4,3,2,1,0:T(8,128)(2,1)S(1)}, u32[]{:S(2)}) copy-start(bf16[4,1,2,4,16,640]{5,4,3,2,1,0:T(8,128)(2,1)S(1)} %collective-permute-done.19.refs_8_) | copy-start | bytes 1966084
  87.4 4.9 %collective-permute-start.20 = (bf16[4,1,2,4,16,640]{5,4,3,2,1,0:T(8,128)(2,1)S(1)}, bf16[4,1,2,4,16,640]{5,4,3,2,1,0:T(8,128)(2,1)S(1)}, u32[]{:S(2)}, u32[]{:S(2)}) collective-permute-start(bf16[4,1,2,4,16,640]{5,4,3,2,1,0:T(8,128)(2,1)S(1)} %collective-permute-done.19.refs_8_), channel_id=1, source_target_pairs={{1,0},{0,1},{129,128},{128,129},{3,2},{2,3},{131,130},{130,131},{5... | collective-permute-start | bytes 1966088 | tf_op jit(solution)/shard_map/ppermute | solution.py:403
  89.5 4.6 %copy-start.9 = (bf16[4,1,2,4,16,640]{5,4,3,2,1,0:T(8,128)(2,1)}, bf16[4,1,2,4,16,640]{5,4,3,2,1,0:T(8,128)(2,1)S(1)}, u32[]{:S(2)}) copy-start(bf16[4,1,2,4,16,640]{5,4,3,2,1,0:T(8,128)(2,1)S(1)} %collective-permute-done.16.refs_3_) | copy-start | bytes 1966084
  89.5 4.5 %collective-permute-start.17 = (bf16[4,1,2,4,16,640]{5,4,3,2,1,0:T(8,128)(2,1)S(1)}, bf16[4,1,2,4,16,640]{5,4,3,2,1,0:T(8,128)(2,1)S(1)}, u32[]{:S(2)}, u32[]{:S(2)}) collective-permute-start(bf16[4,1,2,4,16,640]{5,4,3,2,1,0:T(8,128)(2,1)S(1)} %collective-permute-done.16.refs_3_), channel_id=1, source_target_pairs={{1,0},{0,1},{129,128},{128,129},{3,2},{2,3},{131,130},{130,131},{5... | collective-permute-start | bytes 1966088 | tf_op jit(solution)/shard_map/ppermute | solution.py:403
  92.3 1.8 copy-start.10
  94.0 0.8 copy-start.11
  94.0 1.3 copy-start.4
  94.0 1.7 copy-start.5
  156.2 2.4 %collective-permute-start.21 = (f32[32,40,128]{2,1,0:T(8,128)}, f32[32,40,128]{2,1,0:T(8,128)S(1)}, u32[]{:S(2)}, u32[]{:S(2)}) collective-permute-start(f32[32,40,128]{2,1,0:T(8,128)} %get-tuple-element.22.ends_ref), channel_id=1, source_target_pairs={{1,0},{0,1},{129,128},{128,129},{3,2},{2,3},{131,130},{130,131},{5... | collective-permute-start | bytes 1966088 | tf_op jit(solution)/shard_map/ppermute | solution.py:403
  158.6 0.9 copy-start.3
  159.4 6.5 %copy-start = (f32[24,64,128]{2,1,0:T(8,128)S(1)}, f32[24,64,128]{2,1,0:T(8,128)}, u32[]{:S(2)}) copy-start(f32[24,64,128]{2,1,0:T(8,128)} %get-tuple-element.23.par_ref) | copy-start | bytes 2359300
  162.3 16.4 %all-to-all-start = ((f32[16,40,128]{2,1,0:T(8,128)}), f32[16,40,128]{2,1,0:T(8,128)S(1)}, u32[]{:S(2)}, u32[]{:S(2)}) async-start(f32[16,40,128]{2,1,0:T(8,128)} %combine.1), calls=%async_computation | async-start | bytes 655360 | tf_op jit(solution)/shard_map/all_to_all | solution.py:448
  178.7 0.7 copy-start.6
  198.5 3.3 %copy-start.7 = (f32[16,32,128]{2,1,0:T(8,128)}, f32[16,32,128]{2,1,0:T(8,128)S(1)}, u32[]{:S(2)}) copy-start(f32[16,32,128]{2,1,0:T(8,128)S(1)} %all_to_all.10.hin_ref) | copy-start | bytes 786436
  198.5 3.3 %collective-permute-start.22 = (f32[16,32,128]{2,1,0:T(8,128)S(1)}, f32[16,32,128]{2,1,0:T(8,128)S(1)}, u32[]{:S(2)}, u32[]{:S(2)}) collective-permute-start(f32[16,32,128]{2,1,0:T(8,128)S(1)} %all_to_all.10.hin_ref), channel_id=1, source_target_pairs={{1,0},{0,1},{129,128},{128,129},{3,2},{2,3},{131,130},{130,131},{5... | collective-permute-start | bytes 786440 | tf_op jit(solution)/shard_map/ppermute | solution.py:403
  201.7 0.7 copy-start.12

commit v6 on v5

--- a/solution.py
+++ b/solution.py
@@ -78,9 +78,14 @@
     states = a_scr.shape[0]
     keep = lax.broadcasted_iota(jnp.int32, (tok, LANES), 0) < info_ref[0]
 
+    @pl.when(step == 0)
+    def _():
+        sum_scr[...] = jnp.zeros_like(sum_scr)
+
     @pl.when(step < many)
     def _():
         assemble(step, info_ref, piece_refs, w_scr.at[step])
+        acts = []
         count = par_scr.shape[1] // ROWS
         after = rank + 2 * states
         for g in range(ROWS):
@@ -102,17 +107,11 @@
             act = (total * sigmoid(total)).astype(jnp.bfloat16)
             act_ref[:, cols] = act
             act_scr[step, :, cols] = act
-        weight = w_scr[step].reshape(WIDE, w_scr.shape[-1])[:, : sum_scr.shape[1]]
-        part = jnp.dot(act_scr[step], weight, preferred_element_type=jnp.float32)
-
-        @pl.when(step == 0)
-        def _():
-            sum_scr[...] = part
-
-        @pl.when(step > 0)
-        def _():
-            sum_scr[...] += part
-
+            acts.append(act)
+            if g % 2:
+                weight = w_scr[step, g // 2].reshape(2 * LANES, w_scr.shape[-1])[:, : sum_scr.shape[1]]
+                both = jnp.concatenate(acts[-2:], axis=1)
+                sum_scr[...] += jnp.dot(both, weight, preferred_element_type=jnp.float32)
         @pl.when(step == many - 1)
         def _():
             low_scr[...] = sum_scr[:, :rank].astype(jnp.bfloat16)
@@ -411,19 +410,23 @@
     return move
 
 
-def flip(axis, bit):
+def flip(*bits):
     def move(x, y, z, core):
-        return x ^ (bit if axis == "x" else 0), y ^ (bit if axis == "y" else 0), z ^ (bit if axis == "z" else 0), core ^ (
-            bit if axis == "core" else 0
-        )
+        z_bits = sum(bit for axis, bit in bits if axis == "z")
+        core_bits = sum(bit for axis, bit in bits if axis == "core")
+        return x, y, z ^ z_bits, core ^ core_bits
 
     return move
 
 
-def double(value, axis, bit, own):
-    other = fetch(value, flip(axis, bit))
-    low = (own & bit) == 0
-    return jnp.concatenate([jnp.where(low, value, other), jnp.where(low, other, value)], axis=0)
+def four(value, low, high, own):
+    at_low, at_high, at_both = fetch(value, flip(low)), fetch(value, flip(high)), fetch(value, flip(low, high))
+
+    def pair(bit, here, there):
+        zero = (own[bit[0]] & bit[1]) == 0
+        return jnp.concatenate([jnp.where(zero, here, there), jnp.where(zero, there, here)], axis=0)
+
+    return pair(high, pair(low, value, at_low), pair(low, at_high, at_both))
 
 
 def farther(near, axis, own_core):
@@ -431,7 +434,7 @@
 
 
 def swap(value):
-    return fetch(value, flip("core", 1))
+    return fetch(value, flip(("core", 1)))
 
 
 def row_of_four(value, axis, own_core):
@@ -478,9 +481,8 @@
     fill = -(xproj_weight.shape[1] + 3 * count + rank) % LANES
     parts += [jnp.zeros((width, fill), jnp.bfloat16), dtproj_weight.T]
     mats = jnp.concatenate([xproj_weight, *parts], axis=1)[None]
-    mats, rim = lax.optimization_barrier((double(mats, "z", 4, own_z), rim))
-    for axis, bit in (("z", 2), ("z", 1), ("core", 1)):
-        mats = double(mats, axis, bit, own[axis])
+    mats, rim = lax.optimization_barrier((four(mats, ("z", 4), ("z", 2), own), rim))
+    mats = four(mats, ("z", 1), ("core", 1), own)
     mats = mats.reshape(1, 2, 2, 4, *mats.shape[1:])
     upper = row_of_four(mats[..., : width // 2, :], "y", own_core)
     lower = row_of_four(mats[..., width // 2 :, :], "x", own_core)

time: 238 us -> 236 us (level)
  waiting for transfers between devices: 50.3 us -> 46.8 us
  starting transfers between devices: 46.1 us -> 49.5 us
    ppermute x22 -> x24, waiting for transfers between devices: 36.9 us -> 32.9 us  [fetch(): return lax.ppermute(value, ('group', 'ctx'), route)]
    all_to_all x1, starting transfers between devices: 3.54 us -> 6.38 us  [exchange(): lax.all_to_all(value, 'ctx', split_axis=0, concat_axis=0, tiled=True, axi...]
    ppermute x22 -> x24, starting transfers between devices: 38.7 us -> 38.9 us  [fetch(): return lax.ppermute(value, ('group', 'ctx'), route)]
  transfers between devices with their start and end apart: 24 -> 26, of which waited for: 14 -> 14; matrix products, arithmetic and copies ran while one was open for 2% -> 2% of each run, Pallas kernels for 4% -> 4%
where the time goes in v6:
time: 236 us
  Pallas kernels  108 us (46%)
  starting transfers between devices  49.5 us (21%)
  waiting for transfers between devices  46.8 us (20%)
  blocking collectives  16.8 us (7%)
  local copies, waits for them, and re-layouts  8.71 us (4%)
  other arithmetic  5.19 us (2%)
    pallas_call x1, Pallas kernels, scan_pass(): pl.pallas_call(scan_kernel, grid_spec=pltpu.PrefetchScalarGridSpec(num_sc...  59.8 us
    ppermute x24, starting transfers between devices, fetch(): return lax.ppermute(value, ('group', 'ctx'), route)  38.9 us
    pallas_call x1, Pallas kernels, gate_pass(): pl.pallas_call(gate_kernel, grid_spec=pltpu.PrefetchScalarGridSpec(num_sc...  34.3 us
    ppermute x24, waiting for transfers between devices, fetch(): return lax.ppermute(value, ('group', 'ctx'), route)  32.9 us
    all_to_all x1, blocking collectives, exchange(): lax.all_to_all(value, 'ctx', split_axis=0, concat_axis=0, tiled=True, axi...  16.8 us
    all_to_all x1, waiting for transfers between devices, exchange(): lax.all_to_all(value, 'ctx', split_axis=0, concat_axis=0, tiled=True, axi...  12.8 us
    pallas_call x1, Pallas kernels, gate_factor(): pl.pallas_call(factor_kernel, grid_spec=pltpu.PrefetchScalarGridSpec(num_...  8.81 us
    all_to_all x1, starting transfers between devices, exchange(): lax.all_to_all(value, 'ctx', split_axis=0, concat_axis=0, tiled=True, axi...  6.38 us
  transfers between devices with their start and end apart: 26, of which 14 were waited for; matrix products, arithmetic and copies ran while one was open for 2% of the time, Pallas kernels for 4%

profile of v6, /device:TPU:1, one launch (start us, length us, event | category | flops | bytes accessed | tf_op | source)
XLA Modules:
  0.0 235.5 jit_solution(1859428839506989094)
XLA Ops:
  0.0 0.7 slice.42
  0.7 1.5 concatenate.39
  2.5 0.8 concatenate.40
  3.3 6.9 %collective-permute-start.2 = (bf16[1,32,640]{2,1,0:T(8,128)(2,1)S(1)}, bf16[1,32,640]{2,1,0:T(8,128)(2,1)S(1)}, u32[]{:S(2)}, u32[]{:S(2)}) collective-permute-start(bf16[1,32,640]{2,1,0:T(8,128)(2,1)S(1)} %bitcast.31), channel_id=1, source_target_pairs={{6,0},{7,1},{134,128},{135,129},{4,2},{5,3},{132,130},{133,131},{2... | collective-permute-start | bytes 122888 | tf_op jit(solution)/shard_map/ppermute | solution.py:402
  10.3 1.2 collective-permute-start.1
  11.4 1.0 collective-permute-start
  13.1 1.0 bitcast_select_fusion
  14.1 4.2 %collective-permute-start.3 = (bf16[3,8192]{1,0:T(4,128)(2,1)S(1)}, bf16[3,8192]{1,0:T(4,128)(2,1)S(1)}, u32[]{:S(2)}, u32[]{:S(2)}) collective-permute-start(bf16[3,8192]{1,0:T(4,128)(2,1)S(1)} %bitcast_select_fusion), channel_id=1, source_target_pairs={{0,1},{1,2},{2,3},{3,4},{4,5},{5,6},{6,7},{7,8},{8,9},{9,10},{10,1... | collective-permute-start | bytes 147464 | tf_op jit(solution)/shard_map/ppermute | solution.py:472
  18.6 1.1 collective-permute-done.3
  19.6 0.7 concatenate.44.rim_ref
  20.3 1.8 collective-permute-start.4
  22.4 0.6 collective-permute-start.6
  23.1 2.9 %collective-permute-done.4 = bf16[4,32,640]{2,1,0:T(8,128)(2,1)S(1)} collective-permute-done((bf16[4,32,640]{2,1,0:T(8,128)(2,1)S(1)}, bf16[4,32,640]{2,1,0:T(8,128)(2,1)S(1)}, u32[]{:S(2)}, u32[]{:S(2)}) %collective-permute-start.4) | collective-permute-done | bytes 163872 | tf_op jit(solution)/shard_map/ppermute | solution.py:402
  26.0 4.1 %collective-permute-done.6 = bf16[4,32,640]{2,1,0:T(8,128)(2,1)S(1)} collective-permute-done((bf16[4,32,640]{2,1,0:T(8,128)(2,1)S(1)}, bf16[4,32,640]{2,1,0:T(8,128)(2,1)S(1)}, u32[]{:S(2)}, u32[]{:S(2)}) %collective-permute-start.6) | collective-permute-done | bytes 163872 | tf_op jit(solution)/shard_map/ppermute | solution.py:402
  30.4 4.1 %collective-permute-start.12 = (bf16[1,2,2,4,16,640]{5,4,3,2,1,0:T(8,128)(2,1)S(1)}, bf16[1,2,2,4,16,640]{5,4,3,2,1,0:T(8,128)(2,1)S(1)}, u32[]{:S(2)}, u32[]{:S(2)}) collective-permute-start(bf16[1,2,2,4,16,640]{5,4,3,2,1,0:T(8,128)(2,1)S(1)} %get-tuple-element.29), channel_id=1, source_target_pairs={{8,0},{25,1},{136,128},{153,129},{10,2},{27,3},{138,130},{155,131}... | collective-permute-start | bytes 983048 | tf_op jit(solution)/shard_map/ppermute | solution.py:402
  34.5 1.3 collective-permute-start.7
  35.8 4.4 %collective-permute-done.12 = bf16[1,2,2,4,16,640]{5,4,3,2,1,0:T(8,128)(2,1)S(1)} collective-permute-done((bf16[1,2,2,4,16,640]{5,4,3,2,1,0:T(8,128)(2,1)S(1)}, bf16[1,2,2,4,16,640]{5,4,3,2,1,0:T(8,128)(2,1)S(1)}, u32[]{:S(2)}, u32[]{:S(2)}) %collective-permute-start.12) | collective-permute-done | bytes 327712 | tf_op jit(solution)/shard_map/ppermute | solution.py:402
  40.8 3.6 %collective-permute-start.13 = (bf16[1,2,2,4,16,640]{5,4,3,2,1,0:T(8,128)(2,1)S(1)}, bf16[1,2,2,4,16,640]{5,4,3,2,1,0:T(8,128)(2,1)S(1)}, u32[]{:S(2)}, u32[]{:S(2)}) collective-permute-start(bf16[1,2,2,4,16,640]{5,4,3,2,1,0:T(8,128)(2,1)S(1)} %collective-permute-done.12), channel_id=1, source_target_pairs={{1,0},{0,1},{129,128},{128,129},{3,2},{2,3},{131,130},{130,131},{5... | collective-permute-start | bytes 983048 | tf_op jit(solution)/shard_map/ppermute | solution.py:402
  44.4 1.4 collective-permute-start.9
  45.8 2.2 collective-permute-start.15
  48.0 1.9 collective-permute-done.9
  49.9 0.9 collective-permute-start.10
  51.0 0.9 collective-permute-done.10
  52.3 1.4 pad_maximum_fusion.1.refs_5_
  53.6 0.8 collective-permute-start.16
  55.0 8.8 %gate_factor.1.factor_ref = f32[256,8192]{1,0:T(8,128)} custom-call(s32[4]{0:T(128)} %pad_add_fusion.info_ref, bf16[256,8192]{1,0:T(8,128)(2,1)} %bitcast.29), custom_call_target="tpu_custom_call" | custom-call | tf_op jit(solution)/shard_map/gate_factor/pallas_call | solution.py:297
  63.8 6.0 %collective-permute-done.11.refs_1_ = bf16[4,2,2,4,16,640]{5,4,3,2,1,0:T(8,128)(2,1)S(1)} collective-permute-done((bf16[4,2,2,4,16,640]{5,4,3,2,1,0:T(8,128)(2,1)S(1)}, bf16[4,2,2,4,16,640]{5,4,3,2,1,0:T(8,128)(2,1)S(1)}, u32[]{:S(2)}, u32[]{:S(2)}) %collective-permute-start.11) | collective-permute-done | bytes 1310752 | tf_op jit(solution)/shard_map/ppermute | solution.py:402
  69.9 2.5 %collective-permute-done.16.refs_6_ = bf16[4,2,2,4,16,640]{5,4,3,2,1,0:T(8,128)(2,1)} collective-permute-done((bf16[4,2,2,4,16,640]{5,4,3,2,1,0:T(8,128)(2,1)}, bf16[4,2,2,4,16,640]{5,4,3,2,1,0:T(8,128)(2,1)}, u32[]{:S(2)}, u32[]{:S(2)}) %collective-permute-start.16) | collective-permute-done | bytes 1310752 | tf_op jit(solution)/shard_map/ppermute | solution.py:402
  72.4 1.4 slice_select_fusion
  74.2 5.2 %collective-permute-start.17 = (bf16[4,2,2,4,16,640]{5,4,3,2,1,0:T(8,128)(2,1)S(1)}, bf16[4,2,2,4,16,640]{5,4,3,2,1,0:T(8,128)(2,1)S(1)}, u32[]{:S(2)}, u32[]{:S(2)}) collective-permute-start(bf16[4,2,2,4,16,640]{5,4,3,2,1,0:T(8,128)(2,1)S(1)} %collective-permute-done.11.refs_1_), channel_id=1, source_target_pairs={{1,0},{0,1},{129,128},{128,129},{3,2},{2,3},{131,130},{130,131},{5... | collective-permute-start | bytes 3932168 | tf_op jit(solution)/shard_map/ppermute | solution.py:402
  79.4 5.3 %collective-permute-done.21.refs_8_ = bf16[4,1,2,4,16,640]{5,4,3,2,1,0:T(8,128)(2,1)S(1)} collective-permute-done((bf16[4,1,2,4,16,640]{5,4,3,2,1,0:T(8,128)(2,1)S(1)}, bf16[4,1,2,4,16,640]{5,4,3,2,1,0:T(8,128)(2,1)S(1)}, u32[]{:S(2)}, u32[]{:S(2)}) %collective-permute-start.21) | collective-permute-done | bytes 655392 | tf_op jit(solution)/shard_map/ppermute | solution.py:402
  84.6 2.2 collective-permute-start.22
  86.8 2.6 %collective-permute-start.19 = (bf16[4,1,2,4,16,640]{5,4,3,2,1,0:T(8,128)(2,1)S(1)}, bf16[4,1,2,4,16,640]{5,4,3,2,1,0:T(8,128)(2,1)S(1)}, u32[]{:S(2)}, u32[]{:S(2)}) collective-permute-start(bf16[4,1,2,4,16,640]{5,4,3,2,1,0:T(8,128)(2,1)S(1)} %collective-permute-done.18.refs_3_), channel_id=1, source_target_pairs={{1,0},{0,1},{129,128},{128,129},{3,2},{2,3},{131,130},{130,131},{5... | collective-permute-start | bytes 1966088 | tf_op jit(solution)/shard_map/ppermute | solution.py:402
  89.4 1.7 collective-permute-done.19.refs_4_
  91.2 0.8 copy-done.11
  92.9 59.8 %scan_pass.1 = (bf16[256,8192]{1,0:T(8,128)(2,1)}, f32[24,64,128]{2,1,0:T(8,128)}, f32[256,64,128]{2,1,0:T(8,128)}, f32[256,64,128]{2,1,0:T(8,128)}, f32[32,40,128]{2,1,0:T(8,128)}, /*index=5*/f32[4096,128]{1,0:T(8,128)}) custom-call(s32[4]{0:T(128)} %pad_add_fusion.info_ref, bf16[256,8192]{1,0:T(8,128)(2,1)} %bitcast.28, ...), custom_call_target="tpu_custom_call" | custom-call | tf_op jit(solution)/shard_map/scan_pass/pallas_call | solution.py:189
  153.2 1.9 collective-permute-done.23.other_ref
  155.1 0.9 copy-done.3
  155.9 2.9 %combine.1 = f32[16,40,128]{2,1,0:T(8,128)} custom-call(s32[4]{0:T(128)} %pad_add_fusion.info_ref, f32[32,40,128]{2,1,0:T(8,128)} %get-tuple-element.22.ends_ref, f32[32,40,128]{2,1,0:T(8,128)} %copy-done.3, f32[24,64,128]{2,1,0:T(8,128)} %get-tuple-element.23.par_ref), custom_call_target="tpu_custom_call" | custom-call | tf_op jit(solution)/shard_map/combine/pallas_call | solution.py:253
  158.8 6.4 %all-to-all-start = ((f32[16,40,128]{2,1,0:T(8,128)}), f32[16,40,128]{2,1,0:T(8,128)S(1)}, u32[]{:S(2)}, u32[]{:S(2)}) async-start(f32[16,40,128]{2,1,0:T(8,128)} %combine.1), calls=%async_computation | async-start | bytes 655360 | tf_op jit(solution)/shard_map/all_to_all | solution.py:451
  165.9 12.8 %all-to-all-done.end_ref = f32[16,40,128]{2,1,0:T(8,128)S(1)} async-done(((f32[16,40,128]{2,1,0:T(8,128)}), f32[16,40,128]{2,1,0:T(8,128)S(1)}, u32[]{:S(2)}, u32[]{:S(2)}) %all-to-all-start) | async-done | bytes 327712 | tf_op jit(solution)/shard_map/all_to_all | solution.py:451
  178.7 0.7 copy-done.6
  179.4 1.7 prefix.1
  181.2 16.8 %all_to_all.10.hin_ref = f32[16,32,128]{2,1,0:T(8,128)S(1)} all-to-all(f32[16,32,128]{2,1,0:T(8,128)} %prefix.1), channel_id=1, replica_groups={{0,2,4,6,8,10,12,14,16,18,20,22,24,26,28,30},{1,3,5,7,9,11,13,15,17,19,..., dimensions={0} | all-to-all | bytes 524288 | tf_op jit(solution)/shard_map/all_to_all | solution.py:451
  197.9 1.4 collective-permute-start.24
  199.3 1.2 collective-permute-done.24.hin_too_ref
  200.5 0.7 copy-done.12
  201.2 34.3 %gate_pass.1 = bf16[256,8192]{1,0:T(8,128)(2,1)} custom-call(s32[4]{0:T(128)} %pad_add_fusion.info_ref, f32[256,64,128]{2,1,0:T(8,128)} %get-tuple-element.20.y_ref, f32[256,64,128]{2,1,0:T(8,128)} %get-tuple-element.21.cum_ref, f32[16,32,128]{2,1,0:T(8,128)} %copy-done.7, f32[16,32,128]{2,1,0:T(8,128)} %copy-done.12, f32[32,40,128]{2,1,0:T(8,128)} %copy-done.3, ...), custom_call_target="tpu_custom_call" | custom-call | tf_op jit(solution)/shard_map/gate_pass/pallas_call | solution.py:361
  (68 shorter events, 5.3 us)
Async XLA Ops:
  3.3 15.1 %collective-permute-start.2 = (bf16[1,32,640]{2,1,0:T(8,128)(2,1)S(1)}, bf16[1,32,640]{2,1,0:T(8,128)(2,1)S(1)}, u32[]{:S(2)}, u32[]{:S(2)}) collective-permute-start(bf16[1,32,640]{2,1,0:T(8,128)(2,1)S(1)} %bitcast.31), channel_id=1, source_target_pairs={{6,0},{7,1},{134,128},{135,129},{4,2},{5,3},{132,130},{133,131},{2... | collective-permute-start | bytes 122888 | tf_op jit(solution)/shard_map/ppermute | solution.py:402
  10.3 8.2 %collective-permute-start.1 = (bf16[1,32,640]{2,1,0:T(8,128)(2,1)S(1)}, bf16[1,32,640]{2,1,0:T(8,128)(2,1)S(1)}, u32[]{:S(2)}, u32[]{:S(2)}) collective-permute-start(bf16[1,32,640]{2,1,0:T(8,128)(2,1)S(1)} %bitcast.32), channel_id=1, source_target_pairs={{2,0},{3,1},{130,128},{131,129},{0,2},{1,3},{128,130},{129,131},{6... | collective-permute-start | bytes 122888 | tf_op jit(solution)/shard_map/ppermute | solution.py:402
  11.4 7.0 %collective-permute-start = (bf16[1,32,640]{2,1,0:T(8,128)(2,1)S(1)}, bf16[1,32,640]{2,1,0:T(8,128)(2,1)S(1)}, u32[]{:S(2)}, u32[]{:S(2)}) collective-permute-start(bf16[1,32,640]{2,1,0:T(8,128)(2,1)S(1)} %bitcast.33), channel_id=1, source_target_pairs={{4,0},{5,1},{132,128},{133,129},{6,2},{7,3},{134,130},{135,131},{0... | collective-permute-start | bytes 122888 | tf_op jit(solution)/shard_map/ppermute | solution.py:402
  14.1 5.5 %collective-permute-start.3 = (bf16[3,8192]{1,0:T(4,128)(2,1)S(1)}, bf16[3,8192]{1,0:T(4,128)(2,1)S(1)}, u32[]{:S(2)}, u32[]{:S(2)}) collective-permute-start(bf16[3,8192]{1,0:T(4,128)(2,1)S(1)} %bitcast_select_fusion), channel_id=1, source_target_pairs={{0,1},{1,2},{2,3},{3,4},{4,5},{5,6},{6,7},{7,8},{8,9},{9,10},{10,1... | collective-permute-start | bytes 147464 | tf_op jit(solution)/shard_map/ppermute | solution.py:472
  20.3 5.6 %collective-permute-start.4 = (bf16[4,32,640]{2,1,0:T(8,128)(2,1)S(1)}, bf16[4,32,640]{2,1,0:T(8,128)(2,1)S(1)}, u32[]{:S(2)}, u32[]{:S(2)}) collective-permute-start(bf16[4,32,640]{2,1,0:T(8,128)(2,1)S(1)} %pad_maximum_fusion.5), channel_id=1, source_target_pairs={{128,0},{129,1},{0,128},{1,129},{130,2},{131,3},{2,130},{3,131},{1... | collective-permute-start | bytes 491528 | tf_op jit(solution)/shard_map/ppermute | solution.py:402
  22.1 3.9 %collective-permute-start.5 = (bf16[4,32,640]{2,1,0:T(8,128)(2,1)S(1)}, bf16[4,32,640]{2,1,0:T(8,128)(2,1)S(1)}, u32[]{:S(2)}, u32[]{:S(2)}) collective-permute-start(bf16[4,32,640]{2,1,0:T(8,128)(2,1)S(1)} %pad_maximum_fusion.5), channel_id=1, source_target_pairs={{1,0},{0,1},{129,128},{128,129},{3,2},{2,3},{131,130},{130,131},{5... | collective-permute-start | bytes 491528 | tf_op jit(solution)/shard_map/ppermute | solution.py:402
  22.4 7.6 %collective-permute-start.6 = (bf16[4,32,640]{2,1,0:T(8,128)(2,1)S(1)}, bf16[4,32,640]{2,1,0:T(8,128)(2,1)S(1)}, u32[]{:S(2)}, u32[]{:S(2)}) collective-permute-start(bf16[4,32,640]{2,1,0:T(8,128)(2,1)S(1)} %pad_maximum_fusion.5), channel_id=1, source_target_pairs={{129,0},{128,1},{1,128},{0,129},{131,2},{130,3},{3,130},{2,131},{1... | collective-permute-start | bytes 491528 | tf_op jit(solution)/shard_map/ppermute | solution.py:402
  30.4 9.8 %collective-permute-start.12 = (bf16[1,2,2,4,16,640]{5,4,3,2,1,0:T(8,128)(2,1)S(1)}, bf16[1,2,2,4,16,640]{5,4,3,2,1,0:T(8,128)(2,1)S(1)}, u32[]{:S(2)}, u32[]{:S(2)}) collective-permute-start(bf16[1,2,2,4,16,640]{5,4,3,2,1,0:T(8,128)(2,1)S(1)} %get-tuple-element.29), channel_id=1, source_target_pairs={{8,0},{25,1},{136,128},{153,129},{10,2},{27,3},{138,130},{155,131}... | collective-permute-start | bytes 983048 | tf_op jit(solution)/shard_map/ppermute | solution.py:402
  34.5 9.9 %collective-permute-start.7 = (bf16[1,2,2,4,16,640]{5,4,3,2,1,0:T(8,128)(2,1)S(1)}, bf16[1,2,2,4,16,640]{5,4,3,2,1,0:T(8,128)(2,1)S(1)}, u32[]{:S(2)}, u32[]{:S(2)}) collective-permute-start(bf16[1,2,2,4,16,640]{5,4,3,2,1,0:T(8,128)(2,1)S(1)} %get-tuple-element.30), channel_id=1, source_target_pairs={{32,0},{97,1},{160,128},{225,129},{34,2},{99,3},{162,130},{227,131... | collective-permute-start | bytes 983048 | tf_op jit(solution)/shard_map/ppermute | solution.py:402
  40.2 5.6 %collective-permute-start.14 = (bf16[1,1,2,4,16,640]{5,4,3,2,1,0:T(8,128)(2,1)S(1)}, bf16[1,1,2,4,16,640]{5,4,3,2,1,0:T(8,128)(2,1)S(1)}, u32[]{:S(2)}, u32[]{:S(2)}) collective-permute-start(bf16[1,1,2,4,16,640]{5,4,3,2,1,0:T(8,128)(2,1)S(1)} %slice_select_fusion.2), channel_id=1, source_target_pairs={{8,0},{25,1},{136,128},{153,129},{10,2},{27,3},{138,130},{155,131}... | collective-permute-start | bytes 491528 | tf_op jit(solution)/shard_map/ppermute | solution.py:402
  40.8 10.1 %collective-permute-start.13 = (bf16[1,2,2,4,16,640]{5,4,3,2,1,0:T(8,128)(2,1)S(1)}, bf16[1,2,2,4,16,640]{5,4,3,2,1,0:T(8,128)(2,1)S(1)}, u32[]{:S(2)}, u32[]{:S(2)}) collective-permute-start(bf16[1,2,2,4,16,640]{5,4,3,2,1,0:T(8,128)(2,1)S(1)} %collective-permute-done.12), channel_id=1, source_target_pairs={{1,0},{0,1},{129,128},{128,129},{3,2},{2,3},{131,130},{130,131},{5... | collective-permute-start | bytes 983048 | tf_op jit(solution)/shard_map/ppermute | solution.py:402
  44.4 6.5 %collective-permute-start.8 = (bf16[1,2,2,4,16,640]{5,4,3,2,1,0:T(8,128)(2,1)S(1)}, bf16[1,2,2,4,16,640]{5,4,3,2,1,0:T(8,128)(2,1)S(1)}, u32[]{:S(2)}, u32[]{:S(2)}) collective-permute-start(bf16[1,2,2,4,16,640]{5,4,3,2,1,0:T(8,128)(2,1)S(1)} %collective-permute-done.7), channel_id=1, source_target_pairs={{1,0},{0,1},{129,128},{128,129},{3,2},{2,3},{131,130},{130,131},{5... | collective-permute-start | bytes 983048 | tf_op jit(solution)/shard_map/ppermute | solution.py:402
  44.4 5.5 %collective-permute-start.9 = (bf16[1,1,2,4,16,640]{5,4,3,2,1,0:T(8,128)(2,1)S(1)}, bf16[1,1,2,4,16,640]{5,4,3,2,1,0:T(8,128)(2,1)S(1)}, u32[]{:S(2)}, u32[]{:S(2)}) collective-permute-start(bf16[1,1,2,4,16,640]{5,4,3,2,1,0:T(8,128)(2,1)S(1)} %slice_select_fusion.3), channel_id=1, source_target_pairs={{32,0},{97,1},{160,128},{225,129},{34,2},{99,3},{162,130},{227,131... | collective-permute-start | bytes 491528 | tf_op jit(solution)/shard_map/ppermute | solution.py:402
  45.8 6.4 %collective-permute-start.15 = (bf16[1,1,2,4,16,640]{5,4,3,2,1,0:T(8,128)(2,1)S(1)}, bf16[1,1,2,4,16,640]{5,4,3,2,1,0:T(8,128)(2,1)S(1)}, u32[]{:S(2)}, u32[]{:S(2)}) collective-permute-start(bf16[1,1,2,4,16,640]{5,4,3,2,1,0:T(8,128)(2,1)S(1)} %collective-permute-done.14), channel_id=1, source_target_pairs={{1,0},{0,1},{129,128},{128,129},{3,2},{2,3},{131,130},{130,131},{5... | collective-permute-start | bytes 491528 | tf_op jit(solution)/shard_map/ppermute | solution.py:402
  49.9 1.9 collective-permute-start.10
  52.1 1.5 copy-start.1
  52.1 17.7 %collective-permute-start.11 = (bf16[4,2,2,4,16,640]{5,4,3,2,1,0:T(8,128)(2,1)S(1)}, bf16[4,2,2,4,16,640]{5,4,3,2,1,0:T(8,128)(2,1)S(1)}, u32[]{:S(2)}, u32[]{:S(2)}) collective-permute-start(bf16[4,2,2,4,16,640]{5,4,3,2,1,0:T(8,128)(2,1)S(1)} %pad_maximum_fusion.refs_0_), channel_id=1, source_target_pairs={{8,0},{25,1},{136,128},{153,129},{10,2},{27,3},{138,130},{155,131}... | collective-permute-start | bytes 3932168 | tf_op jit(solution)/shard_map/ppermute | solution.py:402
  53.6 18.7 %collective-permute-start.16 = (bf16[4,2,2,4,16,640]{5,4,3,2,1,0:T(8,128)(2,1)}, bf16[4,2,2,4,16,640]{5,4,3,2,1,0:T(8,128)(2,1)}, u32[]{:S(2)}, u32[]{:S(2)}) collective-permute-start(bf16[4,2,2,4,16,640]{5,4,3,2,1,0:T(8,128)(2,1)} %pad_maximum_fusion.1.refs_5_), channel_id=1, source_target_pairs={{32,0},{97,1},{160,128},{225,129},{34,2},{99,3},{162,130},{227,131... | collective-permute-start | bytes 3932168 | tf_op jit(solution)/shard_map/ppermute | solution.py:402
  69.9 4.3 %copy-start.2 = (bf16[4,2,2,4,16,640]{5,4,3,2,1,0:T(8,128)(2,1)}, bf16[4,2,2,4,16,640]{5,4,3,2,1,0:T(8,128)(2,1)S(1)}, u32[]{:S(2)}) copy-start(bf16[4,2,2,4,16,640]{5,4,3,2,1,0:T(8,128)(2,1)S(1)} %collective-permute-done.11.refs_1_) | copy-start | bytes 3932164
  73.7 10.9 %collective-permute-start.21 = (bf16[4,1,2,4,16,640]{5,4,3,2,1,0:T(8,128)(2,1)S(1)}, bf16[4,1,2,4,16,640]{5,4,3,2,1,0:T(8,128)(2,1)S(1)}, u32[]{:S(2)}, u32[]{:S(2)}) collective-permute-start(bf16[4,1,2,4,16,640]{5,4,3,2,1,0:T(8,128)(2,1)S(1)} %slice_select_fusion), channel_id=1, source_target_pairs={{32,0},{97,1},{160,128},{225,129},{34,2},{99,3},{162,130},{227,131... | collective-permute-start | bytes 1966088 | tf_op jit(solution)/shard_map/ppermute | solution.py:402
  74.1 12.7 %collective-permute-start.18 = (bf16[4,1,2,4,16,640]{5,4,3,2,1,0:T(8,128)(2,1)S(1)}, bf16[4,1,2,4,16,640]{5,4,3,2,1,0:T(8,128)(2,1)S(1)}, u32[]{:S(2)}, u32[]{:S(2)}) collective-permute-start(bf16[4,1,2,4,16,640]{5,4,3,2,1,0:T(8,128)(2,1)S(1)} %slice_select_fusion.1), channel_id=1, source_target_pairs={{8,0},{25,1},{136,128},{153,129},{10,2},{27,3},{138,130},{155,131}... | collective-permute-start | bytes 1966088 | tf_op jit(solution)/shard_map/ppermute | solution.py:402
  74.2 17.0 %collective-permute-start.17 = (bf16[4,2,2,4,16,640]{5,4,3,2,1,0:T(8,128)(2,1)S(1)}, bf16[4,2,2,4,16,640]{5,4,3,2,1,0:T(8,128)(2,1)S(1)}, u32[]{:S(2)}, u32[]{:S(2)}) collective-permute-start(bf16[4,2,2,4,16,640]{5,4,3,2,1,0:T(8,128)(2,1)S(1)} %collective-permute-done.11.refs_1_), channel_id=1, source_target_pairs={{1,0},{0,1},{129,128},{128,129},{3,2},{2,3},{131,130},{130,131},{5... | collective-permute-start | bytes 3932168 | tf_op jit(solution)/shard_map/ppermute | solution.py:402
  79.4 11.8 %collective-permute-start.20 = (bf16[4,2,2,4,16,640]{5,4,3,2,1,0:T(8,128)(2,1)}, bf16[4,2,2,4,16,640]{5,4,3,2,1,0:T(8,128)(2,1)S(1)}, u32[]{:S(2)}, u32[]{:S(2)}) collective-permute-start(bf16[4,2,2,4,16,640]{5,4,3,2,1,0:T(8,128)(2,1)} %collective-permute-done.16.refs_6_), channel_id=1, source_target_pairs={{1,0},{0,1},{129,128},{128,129},{3,2},{2,3},{131,130},{130,131},{5... | collective-permute-start | bytes 3932168 | tf_op jit(solution)/shard_map/ppermute | solution.py:402
  84.6 6.5 %copy-start.8 = (bf16[4,1,2,4,16,640]{5,4,3,2,1,0:T(8,128)(2,1)}, bf16[4,1,2,4,16,640]{5,4,3,2,1,0:T(8,128)(2,1)S(1)}, u32[]{:S(2)}) copy-start(bf16[4,1,2,4,16,640]{5,4,3,2,1,0:T(8,128)(2,1)S(1)} %collective-permute-done.21.refs_8_) | copy-start | bytes 1966084
  84.6 4.8 %collective-permute-start.22 = (bf16[4,1,2,4,16,640]{5,4,3,2,1,0:T(8,128)(2,1)S(1)}, bf16[4,1,2,4,16,640]{5,4,3,2,1,0:T(8,128)(2,1)S(1)}, u32[]{:S(2)}, u32[]{:S(2)}) collective-permute-start(bf16[4,1,2,4,16,640]{5,4,3,2,1,0:T(8,128)(2,1)S(1)} %collective-permute-done.21.refs_8_), channel_id=1, source_target_pairs={{1,0},{0,1},{129,128},{128,129},{3,2},{2,3},{131,130},{130,131},{5... | collective-permute-start | bytes 1966088 | tf_op jit(solution)/shard_map/ppermute | solution.py:402
  86.8 4.4 %copy-start.9 = (bf16[4,1,2,4,16,640]{5,4,3,2,1,0:T(8,128)(2,1)}, bf16[4,1,2,4,16,640]{5,4,3,2,1,0:T(8,128)(2,1)S(1)}, u32[]{:S(2)}) copy-start(bf16[4,1,2,4,16,640]{5,4,3,2,1,0:T(8,128)(2,1)S(1)} %collective-permute-done.18.refs_3_) | copy-start | bytes 1966084
  86.8 4.4 %collective-permute-start.19 = (bf16[4,1,2,4,16,640]{5,4,3,2,1,0:T(8,128)(2,1)S(1)}, bf16[4,1,2,4,16,640]{5,4,3,2,1,0:T(8,128)(2,1)S(1)}, u32[]{:S(2)}, u32[]{:S(2)}) collective-permute-start(bf16[4,1,2,4,16,640]{5,4,3,2,1,0:T(8,128)(2,1)S(1)} %collective-permute-done.18.refs_3_), channel_id=1, source_target_pairs={{1,0},{0,1},{129,128},{128,129},{3,2},{2,3},{131,130},{130,131},{5... | collective-permute-start | bytes 1966088 | tf_op jit(solution)/shard_map/ppermute | solution.py:402
  89.4 1.8 copy-start.10
  91.2 0.8 copy-start.11
  91.2 1.3 copy-start.4
  91.2 1.7 copy-start.5
  152.7 2.4 %collective-permute-start.23 = (f32[32,40,128]{2,1,0:T(8,128)}, f32[32,40,128]{2,1,0:T(8,128)S(1)}, u32[]{:S(2)}, u32[]{:S(2)}) collective-permute-start(f32[32,40,128]{2,1,0:T(8,128)} %get-tuple-element.22.ends_ref), channel_id=1, source_target_pairs={{1,0},{0,1},{129,128},{128,129},{3,2},{2,3},{131,130},{130,131},{5... | collective-permute-start | bytes 1966088 | tf_op jit(solution)/shard_map/ppermute | solution.py:402
  155.1 0.9 copy-start.3
  155.9 9.3 %copy-start = (f32[24,64,128]{2,1,0:T(8,128)S(1)}, f32[24,64,128]{2,1,0:T(8,128)}, u32[]{:S(2)}) copy-start(f32[24,64,128]{2,1,0:T(8,128)} %get-tuple-element.23.par_ref) | copy-start | bytes 2359300
  158.8 19.9 %all-to-all-start = ((f32[16,40,128]{2,1,0:T(8,128)}), f32[16,40,128]{2,1,0:T(8,128)S(1)}, u32[]{:S(2)}, u32[]{:S(2)}) async-start(f32[16,40,128]{2,1,0:T(8,128)} %combine.1), calls=%async_computation | async-start | bytes 655360 | tf_op jit(solution)/shard_map/all_to_all | solution.py:451
  178.7 0.7 copy-start.6
  197.9 2.5 %copy-start.7 = (f32[16,32,128]{2,1,0:T(8,128)}, f32[16,32,128]{2,1,0:T(8,128)S(1)}, u32[]{:S(2)}) copy-start(f32[16,32,128]{2,1,0:T(8,128)S(1)} %all_to_all.10.hin_ref) | copy-start | bytes 786436
  197.9 2.5 %collective-permute-start.24 = (f32[16,32,128]{2,1,0:T(8,128)S(1)}, f32[16,32,128]{2,1,0:T(8,128)S(1)}, u32[]{:S(2)}, u32[]{:S(2)}) collective-permute-start(f32[16,32,128]{2,1,0:T(8,128)S(1)} %all_to_all.10.hin_ref), channel_id=1, source_target_pairs={{1,0},{0,1},{129,128},{128,129},{3,2},{2,3},{131,130},{130,131},{5... | collective-permute-start | bytes 786440 | tf_op jit(solution)/shard_map/ppermute | solution.py:402
  200.5 0.7 copy-start.12

commit v7 on v6

--- a/solution.py
+++ b/solution.py
@@ -335,18 +335,18 @@
             h_scr[n] = jnp.exp2(a_scr[n] * e_scr[states]) * h_scr[n] + e_scr[n]
 
     def block(i, carry):
-        for o in range(8):
-            t = i * 8 + o
+        for o in range(16):
+            t = i * 16 + o
             cum = cum_ref[t]
             acc = [y_ref[t]] + [None] * 3
             for n in range(states):
                 c = c_ref[pl.ds(n * tok + t, ROWS, stride=0), :]
                 term = (c * h_scr[n]) * jnp.exp2(a_scr[n] * cum)
                 acc[n % 4] = term if acc[n % 4] is None else acc[n % 4] + term
-            y_scr[i, pl.ds(o, ROWS, stride=8), :] = (acc[0] + acc[1]) + (acc[2] + acc[3])
+            y_scr[i * 2 + o // 8, pl.ds(o % 8, ROWS, stride=8), :] = (acc[0] + acc[1]) + (acc[2] + acc[3])
         return carry
 
-    lax.fori_loop(0, tok // 8, block, 0)
+    lax.fori_loop(0, tok // 16, block, 0)
     for g in range(ROWS):
         cols = slice(g * LANES, (g + 1) * LANES)
         y = y_scr[:, g * 8 : (g + 1) * 8, :].reshape(tok, LANES)
@@ -470,7 +470,6 @@
     edge = jnp.arange(tok - (taps - 1), tok, dtype=jnp.int32)[:, None] < length
     edge = jnp.where(edge, x[tok - (taps - 1) :], jnp.bfloat16(0))
     rim = lax.ppermute(edge, "ctx", [(i, i + 1) for i in range(blocks - 1)])
-    rim = jnp.concatenate([jnp.zeros((8 - (taps - 1), chans), x.dtype), rim], axis=0)
 
     small = jnp.concatenate([conv_weight, conv_bias[None], dt_bias[None], skip_gain[None], a_log, a_log[:1]], axis=0).T
     width, count = small.shape
@@ -487,7 +486,8 @@
     upper = row_of_four(mats[..., : width // 2, :], "y", own_core)
     lower = row_of_four(mats[..., width // 2 :, :], "x", own_core)
     nears = fetch(upper, onward("x")), fetch(lower, onward("y"))
-    *nears, factor = lax.optimization_barrier((*nears, gate_factor(info, z)))
+    *nears, factor, rim = lax.optimization_barrier((*nears, gate_factor(info, z), rim))
+    rim = jnp.concatenate([jnp.zeros((8 - (taps - 1), chans), x.dtype), rim], axis=0)
     pieces = []
     for value, near, axis in ((upper, nears[0], "x"), (lower, nears[1], "y")):
         far = farther(near, axis, own_core)

time: 236 us -> 234 us (level)
  no operation moved by 1% of the time
where the time goes in v7:
time: 234 us; the launch traced here: 233 us
  Pallas kernels  106 us (45%)
  starting transfers between devices  49.5 us (21%)
  waiting for transfers between devices  46.1 us (20%)
  blocking collectives  16.8 us (7%)
  local copies, waits for them, and re-layouts  8.71 us (4%)
  other arithmetic  5.19 us (2%)
    pallas_call x1, Pallas kernels, scan_pass(): pl.pallas_call(scan_kernel, grid_spec=pltpu.PrefetchScalarGridSpec(num_sc...  59.8 us
    ppermute x24, starting transfers between devices, fetch(): return lax.ppermute(value, ('group', 'ctx'), route)  38.9 us
    pallas_call x1, Pallas kernels, gate_pass(): pl.pallas_call(gate_kernel, grid_spec=pltpu.PrefetchScalarGridSpec(num_sc...  32.7 us
    ppermute x24, waiting for transfers between devices, fetch(): return lax.ppermute(value, ('group', 'ctx'), route)  32.3 us
    all_to_all x1, blocking collectives, exchange(): lax.all_to_all(value, 'ctx', split_axis=0, concat_axis=0, tiled=True, axi...  16.8 us
    all_to_all x1, waiting for transfers between devices, exchange(): lax.all_to_all(value, 'ctx', split_axis=0, concat_axis=0, tiled=True, axi...  12.8 us
    pallas_call x1, Pallas kernels, gate_factor(): pl.pallas_call(factor_kernel, grid_spec=pltpu.PrefetchScalarGridSpec(num_...  8.81 us
    all_to_all x1, starting transfers between devices, exchange(): lax.all_to_all(value, 'ctx', split_axis=0, concat_axis=0, tiled=True, axi...  6.37 us
  transfers between devices with their start and end apart: 26, of which 14 were waited for; matrix products, arithmetic and copies ran while one was open for 2% of the time, Pallas kernels for 4%

profile of v7, /device:TPU:1, one launch (start us, length us, event | category | flops | bytes accessed | tf_op | source)
XLA Modules:
  0.0 233.2 jit_solution(4580206637901171013)
XLA Ops:
  0.0 0.7 slice.42
  0.7 1.5 concatenate.39
  2.5 0.8 concatenate.40
  3.3 6.9 %collective-permute-start.2 = (bf16[1,32,640]{2,1,0:T(8,128)(2,1)S(1)}, bf16[1,32,640]{2,1,0:T(8,128)(2,1)S(1)}, u32[]{:S(2)}, u32[]{:S(2)}) collective-permute-start(bf16[1,32,640]{2,1,0:T(8,128)(2,1)S(1)} %bitcast.31), channel_id=1, source_target_pairs={{6,0},{7,1},{134,128},{135,129},{4,2},{5,3},{132,130},{133,131},{2... | collective-permute-start | bytes 122888 | tf_op jit(solution)/shard_map/ppermute | solution.py:402
  10.3 1.2 collective-permute-start.1
  11.4 1.0 collective-permute-start
  13.1 1.0 bitcast_select_fusion
  14.1 4.2 %collective-permute-start.3 = (bf16[3,8192]{1,0:T(4,128)(2,1)S(1)}, bf16[3,8192]{1,0:T(4,128)(2,1)S(1)}, u32[]{:S(2)}, u32[]{:S(2)}) collective-permute-start(bf16[3,8192]{1,0:T(4,128)(2,1)S(1)} %bitcast_select_fusion), channel_id=1, source_target_pairs={{0,1},{1,2},{2,3},{3,4},{4,5},{5,6},{6,7},{7,8},{8,9},{9,10},{10,1... | collective-permute-start | bytes 147464 | tf_op jit(solution)/shard_map/ppermute | solution.py:472
  18.6 1.1 collective-permute-done.3
  19.6 1.8 collective-permute-start.4
  22.5 2.7 %collective-permute-done.4 = bf16[4,32,640]{2,1,0:T(8,128)(2,1)S(1)} collective-permute-done((bf16[4,32,640]{2,1,0:T(8,128)(2,1)S(1)}, bf16[4,32,640]{2,1,0:T(8,128)(2,1)S(1)}, u32[]{:S(2)}, u32[]{:S(2)}) %collective-permute-start.4) | collective-permute-done | bytes 163872 | tf_op jit(solution)/shard_map/ppermute | solution.py:402
  25.2 4.2 %collective-permute-done.6 = bf16[4,32,640]{2,1,0:T(8,128)(2,1)S(1)} collective-permute-done((bf16[4,32,640]{2,1,0:T(8,128)(2,1)S(1)}, bf16[4,32,640]{2,1,0:T(8,128)(2,1)S(1)}, u32[]{:S(2)}, u32[]{:S(2)}) %collective-permute-start.6) | collective-permute-done | bytes 163872 | tf_op jit(solution)/shard_map/ppermute | solution.py:402
  29.7 4.1 %collective-permute-start.12 = (bf16[1,2,2,4,16,640]{5,4,3,2,1,0:T(8,128)(2,1)S(1)}, bf16[1,2,2,4,16,640]{5,4,3,2,1,0:T(8,128)(2,1)S(1)}, u32[]{:S(2)}, u32[]{:S(2)}) collective-permute-start(bf16[1,2,2,4,16,640]{5,4,3,2,1,0:T(8,128)(2,1)S(1)} %get-tuple-element.31), channel_id=1, source_target_pairs={{8,0},{25,1},{136,128},{153,129},{10,2},{27,3},{138,130},{155,131}... | collective-permute-start | bytes 983048 | tf_op jit(solution)/shard_map/ppermute | solution.py:402
  33.8 1.3 collective-permute-start.7
  35.1 4.4 %collective-permute-done.12 = bf16[1,2,2,4,16,640]{5,4,3,2,1,0:T(8,128)(2,1)S(1)} collective-permute-done((bf16[1,2,2,4,16,640]{5,4,3,2,1,0:T(8,128)(2,1)S(1)}, bf16[1,2,2,4,16,640]{5,4,3,2,1,0:T(8,128)(2,1)S(1)}, u32[]{:S(2)}, u32[]{:S(2)}) %collective-permute-start.12) | collective-permute-done | bytes 327712 | tf_op jit(solution)/shard_map/ppermute | solution.py:402
  40.1 3.7 %collective-permute-start.13 = (bf16[1,2,2,4,16,640]{5,4,3,2,1,0:T(8,128)(2,1)S(1)}, bf16[1,2,2,4,16,640]{5,4,3,2,1,0:T(8,128)(2,1)S(1)}, u32[]{:S(2)}, u32[]{:S(2)}) collective-permute-start(bf16[1,2,2,4,16,640]{5,4,3,2,1,0:T(8,128)(2,1)S(1)} %collective-permute-done.12), channel_id=1, source_target_pairs={{1,0},{0,1},{129,128},{128,129},{3,2},{2,3},{131,130},{130,131},{5... | collective-permute-start | bytes 983048 | tf_op jit(solution)/shard_map/ppermute | solution.py:402
  43.8 1.4 collective-permute-start.9
  45.2 2.2 collective-permute-start.15
  47.5 1.9 collective-permute-done.9
  49.4 0.9 collective-permute-start.10
  50.4 0.9 collective-permute-done.10
  51.7 1.4 pad_maximum_fusion.1.refs_5_
  53.1 0.8 collective-permute-start.16
  53.8 0.6 pad_add_fusion.info_ref
  54.5 8.8 %gate_factor.1.factor_ref = f32[256,8192]{1,0:T(8,128)} custom-call(s32[4]{0:T(128)} %pad_add_fusion.info_ref, bf16[256,8192]{1,0:T(8,128)(2,1)} %bitcast.29), custom_call_target="tpu_custom_call" | custom-call | tf_op jit(solution)/shard_map/gate_factor/pallas_call | solution.py:297
  63.3 6.0 %collective-permute-done.11.refs_1_ = bf16[4,2,2,4,16,640]{5,4,3,2,1,0:T(8,128)(2,1)S(1)} collective-permute-done((bf16[4,2,2,4,16,640]{5,4,3,2,1,0:T(8,128)(2,1)S(1)}, bf16[4,2,2,4,16,640]{5,4,3,2,1,0:T(8,128)(2,1)S(1)}, u32[]{:S(2)}, u32[]{:S(2)}) %collective-permute-start.11) | collective-permute-done | bytes 1310752 | tf_op jit(solution)/shard_map/ppermute | solution.py:402
  69.3 2.5 %collective-permute-done.16.refs_6_ = bf16[4,2,2,4,16,640]{5,4,3,2,1,0:T(8,128)(2,1)} collective-permute-done((bf16[4,2,2,4,16,640]{5,4,3,2,1,0:T(8,128)(2,1)}, bf16[4,2,2,4,16,640]{5,4,3,2,1,0:T(8,128)(2,1)}, u32[]{:S(2)}, u32[]{:S(2)}) %collective-permute-start.16) | collective-permute-done | bytes 1310752 | tf_op jit(solution)/shard_map/ppermute | solution.py:402
  71.8 1.4 slice_select_fusion
  73.6 5.1 %collective-permute-start.17 = (bf16[4,2,2,4,16,640]{5,4,3,2,1,0:T(8,128)(2,1)S(1)}, bf16[4,2,2,4,16,640]{5,4,3,2,1,0:T(8,128)(2,1)S(1)}, u32[]{:S(2)}, u32[]{:S(2)}) collective-permute-start(bf16[4,2,2,4,16,640]{5,4,3,2,1,0:T(8,128)(2,1)S(1)} %collective-permute-done.11.refs_1_), channel_id=1, source_target_pairs={{1,0},{0,1},{129,128},{128,129},{3,2},{2,3},{131,130},{130,131},{5... | collective-permute-start | bytes 3932168 | tf_op jit(solution)/shard_map/ppermute | solution.py:402
  78.7 5.4 %collective-permute-done.21.refs_8_ = bf16[4,1,2,4,16,640]{5,4,3,2,1,0:T(8,128)(2,1)S(1)} collective-permute-done((bf16[4,1,2,4,16,640]{5,4,3,2,1,0:T(8,128)(2,1)S(1)}, bf16[4,1,2,4,16,640]{5,4,3,2,1,0:T(8,128)(2,1)S(1)}, u32[]{:S(2)}, u32[]{:S(2)}) %collective-permute-start.21) | collective-permute-done | bytes 655392 | tf_op jit(solution)/shard_map/ppermute | solution.py:402
  84.1 2.0 collective-permute-start.22
  86.1 2.6 %collective-permute-start.19 = (bf16[4,1,2,4,16,640]{5,4,3,2,1,0:T(8,128)(2,1)S(1)}, bf16[4,1,2,4,16,640]{5,4,3,2,1,0:T(8,128)(2,1)S(1)}, u32[]{:S(2)}, u32[]{:S(2)}) collective-permute-start(bf16[4,1,2,4,16,640]{5,4,3,2,1,0:T(8,128)(2,1)S(1)} %collective-permute-done.18.refs_3_), channel_id=1, source_target_pairs={{1,0},{0,1},{129,128},{128,129},{3,2},{2,3},{131,130},{130,131},{5... | collective-permute-start | bytes 1966088 | tf_op jit(solution)/shard_map/ppermute | solution.py:402
  88.7 0.7 concatenate.51.rim_ref
  89.4 1.0 collective-permute-done.19.refs_4_
  90.5 0.8 copy-done.11
  92.2 59.8 %scan_pass.1 = (bf16[256,8192]{1,0:T(8,128)(2,1)}, f32[24,64,128]{2,1,0:T(8,128)}, f32[256,64,128]{2,1,0:T(8,128)}, f32[256,64,128]{2,1,0:T(8,128)}, f32[32,40,128]{2,1,0:T(8,128)}, /*index=5*/f32[4096,128]{1,0:T(8,128)}) custom-call(s32[4]{0:T(128)} %pad_add_fusion.info_ref, bf16[256,8192]{1,0:T(8,128)(2,1)} %bitcast.28, ...), custom_call_target="tpu_custom_call" | custom-call | tf_op jit(solution)/shard_map/scan_pass/pallas_call | solution.py:189
  152.5 1.9 collective-permute-done.23.other_ref
  154.4 0.9 copy-done.3
  155.3 2.9 %combine.1 = f32[16,40,128]{2,1,0:T(8,128)} custom-call(s32[4]{0:T(128)} %pad_add_fusion.info_ref, f32[32,40,128]{2,1,0:T(8,128)} %get-tuple-element.24.ends_ref, f32[32,40,128]{2,1,0:T(8,128)} %copy-done.3, f32[24,64,128]{2,1,0:T(8,128)} %get-tuple-element.25.par_ref), custom_call_target="tpu_custom_call" | custom-call | tf_op jit(solution)/shard_map/combine/pallas_call | solution.py:253
  158.2 6.4 %all-to-all-start = ((f32[16,40,128]{2,1,0:T(8,128)}), f32[16,40,128]{2,1,0:T(8,128)S(1)}, u32[]{:S(2)}, u32[]{:S(2)}) async-start(f32[16,40,128]{2,1,0:T(8,128)} %combine.1), calls=%async_computation | async-start | bytes 655360 | tf_op jit(solution)/shard_map/all_to_all | solution.py:451
  165.2 12.8 %all-to-all-done.end_ref = f32[16,40,128]{2,1,0:T(8,128)S(1)} async-done(((f32[16,40,128]{2,1,0:T(8,128)}), f32[16,40,128]{2,1,0:T(8,128)S(1)}, u32[]{:S(2)}, u32[]{:S(2)}) %all-to-all-start) | async-done | bytes 327712 | tf_op jit(solution)/shard_map/all_to_all | solution.py:451
  178.0 0.7 copy-done.6
  178.7 1.7 prefix.1
  180.5 16.8 %all_to_all.10.hin_ref = f32[16,32,128]{2,1,0:T(8,128)S(1)} all-to-all(f32[16,32,128]{2,1,0:T(8,128)} %prefix.1), channel_id=1, replica_groups={{0,2,4,6,8,10,12,14,16,18,20,22,24,26,28,30},{1,3,5,7,9,11,13,15,17,19,..., dimensions={0} | all-to-all | bytes 524288 | tf_op jit(solution)/shard_map/all_to_all | solution.py:451
  197.2 1.4 collective-permute-start.24
  198.6 1.2 collective-permute-done.24.hin_too_ref
  199.8 0.7 copy-done.12
  200.5 32.7 %gate_pass.1 = bf16[256,8192]{1,0:T(8,128)(2,1)} custom-call(s32[4]{0:T(128)} %pad_add_fusion.info_ref, f32[256,64,128]{2,1,0:T(8,128)} %get-tuple-element.22.y_ref, f32[256,64,128]{2,1,0:T(8,128)} %get-tuple-element.23.cum_ref, f32[16,32,128]{2,1,0:T(8,128)} %copy-done.7, f32[16,32,128]{2,1,0:T(8,128)} %copy-done.12, f32[32,40,128]{2,1,0:T(8,128)} %copy-done.3, ...), custom_call_target="tpu_custom_call" | custom-call | tf_op jit(solution)/shard_map/gate_pass/pallas_call | solution.py:361
  (68 shorter events, 5.4 us)
Async XLA Ops:
  3.3 15.1 %collective-permute-start.2 = (bf16[1,32,640]{2,1,0:T(8,128)(2,1)S(1)}, bf16[1,32,640]{2,1,0:T(8,128)(2,1)S(1)}, u32[]{:S(2)}, u32[]{:S(2)}) collective-permute-start(bf16[1,32,640]{2,1,0:T(8,128)(2,1)S(1)} %bitcast.31), channel_id=1, source_target_pairs={{6,0},{7,1},{134,128},{135,129},{4,2},{5,3},{132,130},{133,131},{2... | collective-permute-start | bytes 122888 | tf_op jit(solution)/shard_map/ppermute | solution.py:402
  10.3 8.2 %collective-permute-start.1 = (bf16[1,32,640]{2,1,0:T(8,128)(2,1)S(1)}, bf16[1,32,640]{2,1,0:T(8,128)(2,1)S(1)}, u32[]{:S(2)}, u32[]{:S(2)}) collective-permute-start(bf16[1,32,640]{2,1,0:T(8,128)(2,1)S(1)} %bitcast.32), channel_id=1, source_target_pairs={{2,0},{3,1},{130,128},{131,129},{0,2},{1,3},{128,130},{129,131},{6... | collective-permute-start | bytes 122888 | tf_op jit(solution)/shard_map/ppermute | solution.py:402
  11.4 7.0 %collective-permute-start = (bf16[1,32,640]{2,1,0:T(8,128)(2,1)S(1)}, bf16[1,32,640]{2,1,0:T(8,128)(2,1)S(1)}, u32[]{:S(2)}, u32[]{:S(2)}) collective-permute-start(bf16[1,32,640]{2,1,0:T(8,128)(2,1)S(1)} %bitcast.33), channel_id=1, source_target_pairs={{4,0},{5,1},{132,128},{133,129},{6,2},{7,3},{134,130},{135,131},{0... | collective-permute-start | bytes 122888 | tf_op jit(solution)/shard_map/ppermute | solution.py:402
  14.1 5.5 %collective-permute-start.3 = (bf16[3,8192]{1,0:T(4,128)(2,1)S(1)}, bf16[3,8192]{1,0:T(4,128)(2,1)S(1)}, u32[]{:S(2)}, u32[]{:S(2)}) collective-permute-start(bf16[3,8192]{1,0:T(4,128)(2,1)S(1)} %bitcast_select_fusion), channel_id=1, source_target_pairs={{0,1},{1,2},{2,3},{3,4},{4,5},{5,6},{6,7},{7,8},{8,9},{9,10},{10,1... | collective-permute-start | bytes 147464 | tf_op jit(solution)/shard_map/ppermute | solution.py:472
  19.6 5.5 %collective-permute-start.4 = (bf16[4,32,640]{2,1,0:T(8,128)(2,1)S(1)}, bf16[4,32,640]{2,1,0:T(8,128)(2,1)S(1)}, u32[]{:S(2)}, u32[]{:S(2)}) collective-permute-start(bf16[4,32,640]{2,1,0:T(8,128)(2,1)S(1)} %pad_maximum_fusion.5), channel_id=1, source_target_pairs={{128,0},{129,1},{0,128},{1,129},{130,2},{131,3},{2,130},{3,131},{1... | collective-permute-start | bytes 491528 | tf_op jit(solution)/shard_map/ppermute | solution.py:402
  21.4 3.8 %collective-permute-start.5 = (bf16[4,32,640]{2,1,0:T(8,128)(2,1)S(1)}, bf16[4,32,640]{2,1,0:T(8,128)(2,1)S(1)}, u32[]{:S(2)}, u32[]{:S(2)}) collective-permute-start(bf16[4,32,640]{2,1,0:T(8,128)(2,1)S(1)} %pad_maximum_fusion.5), channel_id=1, source_target_pairs={{1,0},{0,1},{129,128},{128,129},{3,2},{2,3},{131,130},{130,131},{5... | collective-permute-start | bytes 491528 | tf_op jit(solution)/shard_map/ppermute | solution.py:402
  21.8 7.5 %collective-permute-start.6 = (bf16[4,32,640]{2,1,0:T(8,128)(2,1)S(1)}, bf16[4,32,640]{2,1,0:T(8,128)(2,1)S(1)}, u32[]{:S(2)}, u32[]{:S(2)}) collective-permute-start(bf16[4,32,640]{2,1,0:T(8,128)(2,1)S(1)} %pad_maximum_fusion.5), channel_id=1, source_target_pairs={{129,0},{128,1},{1,128},{0,129},{131,2},{130,3},{3,130},{2,131},{1... | collective-permute-start | bytes 491528 | tf_op jit(solution)/shard_map/ppermute | solution.py:402
  29.7 9.8 %collective-permute-start.12 = (bf16[1,2,2,4,16,640]{5,4,3,2,1,0:T(8,128)(2,1)S(1)}, bf16[1,2,2,4,16,640]{5,4,3,2,1,0:T(8,128)(2,1)S(1)}, u32[]{:S(2)}, u32[]{:S(2)}) collective-permute-start(bf16[1,2,2,4,16,640]{5,4,3,2,1,0:T(8,128)(2,1)S(1)} %get-tuple-element.31), channel_id=1, source_target_pairs={{8,0},{25,1},{136,128},{153,129},{10,2},{27,3},{138,130},{155,131}... | collective-permute-start | bytes 983048 | tf_op jit(solution)/shard_map/ppermute | solution.py:402
  33.8 10.0 %collective-permute-start.7 = (bf16[1,2,2,4,16,640]{5,4,3,2,1,0:T(8,128)(2,1)S(1)}, bf16[1,2,2,4,16,640]{5,4,3,2,1,0:T(8,128)(2,1)S(1)}, u32[]{:S(2)}, u32[]{:S(2)}) collective-permute-start(bf16[1,2,2,4,16,640]{5,4,3,2,1,0:T(8,128)(2,1)S(1)} %get-tuple-element.32), channel_id=1, source_target_pairs={{32,0},{97,1},{160,128},{225,129},{34,2},{99,3},{162,130},{227,131... | collective-permute-start | bytes 983048 | tf_op jit(solution)/shard_map/ppermute | solution.py:402
  39.5 5.7 %collective-permute-start.14 = (bf16[1,1,2,4,16,640]{5,4,3,2,1,0:T(8,128)(2,1)S(1)}, bf16[1,1,2,4,16,640]{5,4,3,2,1,0:T(8,128)(2,1)S(1)}, u32[]{:S(2)}, u32[]{:S(2)}) collective-permute-start(bf16[1,1,2,4,16,640]{5,4,3,2,1,0:T(8,128)(2,1)S(1)} %slice_select_fusion.2), channel_id=1, source_target_pairs={{8,0},{25,1},{136,128},{153,129},{10,2},{27,3},{138,130},{155,131}... | collective-permute-start | bytes 491528 | tf_op jit(solution)/shard_map/ppermute | solution.py:402
  40.1 10.2 %collective-permute-start.13 = (bf16[1,2,2,4,16,640]{5,4,3,2,1,0:T(8,128)(2,1)S(1)}, bf16[1,2,2,4,16,640]{5,4,3,2,1,0:T(8,128)(2,1)S(1)}, u32[]{:S(2)}, u32[]{:S(2)}) collective-permute-start(bf16[1,2,2,4,16,640]{5,4,3,2,1,0:T(8,128)(2,1)S(1)} %collective-permute-done.12), channel_id=1, source_target_pairs={{1,0},{0,1},{129,128},{128,129},{3,2},{2,3},{131,130},{130,131},{5... | collective-permute-start | bytes 983048 | tf_op jit(solution)/shard_map/ppermute | solution.py:402
  43.8 6.5 %collective-permute-start.8 = (bf16[1,2,2,4,16,640]{5,4,3,2,1,0:T(8,128)(2,1)S(1)}, bf16[1,2,2,4,16,640]{5,4,3,2,1,0:T(8,128)(2,1)S(1)}, u32[]{:S(2)}, u32[]{:S(2)}) collective-permute-start(bf16[1,2,2,4,16,640]{5,4,3,2,1,0:T(8,128)(2,1)S(1)} %collective-permute-done.7), channel_id=1, source_target_pairs={{1,0},{0,1},{129,128},{128,129},{3,2},{2,3},{131,130},{130,131},{5... | collective-permute-start | bytes 983048 | tf_op jit(solution)/shard_map/ppermute | solution.py:402
  43.8 5.5 %collective-permute-start.9 = (bf16[1,1,2,4,16,640]{5,4,3,2,1,0:T(8,128)(2,1)S(1)}, bf16[1,1,2,4,16,640]{5,4,3,2,1,0:T(8,128)(2,1)S(1)}, u32[]{:S(2)}, u32[]{:S(2)}) collective-permute-start(bf16[1,1,2,4,16,640]{5,4,3,2,1,0:T(8,128)(2,1)S(1)} %slice_select_fusion.3), channel_id=1, source_target_pairs={{32,0},{97,1},{160,128},{225,129},{34,2},{99,3},{162,130},{227,131... | collective-permute-start | bytes 491528 | tf_op jit(solution)/shard_map/ppermute | solution.py:402
  45.2 6.4 %collective-permute-start.15 = (bf16[1,1,2,4,16,640]{5,4,3,2,1,0:T(8,128)(2,1)S(1)}, bf16[1,1,2,4,16,640]{5,4,3,2,1,0:T(8,128)(2,1)S(1)}, u32[]{:S(2)}, u32[]{:S(2)}) collective-permute-start(bf16[1,1,2,4,16,640]{5,4,3,2,1,0:T(8,128)(2,1)S(1)} %collective-permute-done.14), channel_id=1, source_target_pairs={{1,0},{0,1},{129,128},{128,129},{3,2},{2,3},{131,130},{130,131},{5... | collective-permute-start | bytes 491528 | tf_op jit(solution)/shard_map/ppermute | solution.py:402
  49.4 1.9 collective-permute-start.10
  51.6 1.5 copy-start.1
  51.6 17.7 %collective-permute-start.11 = (bf16[4,2,2,4,16,640]{5,4,3,2,1,0:T(8,128)(2,1)S(1)}, bf16[4,2,2,4,16,640]{5,4,3,2,1,0:T(8,128)(2,1)S(1)}, u32[]{:S(2)}, u32[]{:S(2)}) collective-permute-start(bf16[4,2,2,4,16,640]{5,4,3,2,1,0:T(8,128)(2,1)S(1)} %pad_maximum_fusion.refs_0_), channel_id=1, source_target_pairs={{8,0},{25,1},{136,128},{153,129},{10,2},{27,3},{138,130},{155,131}... | collective-permute-start | bytes 3932168 | tf_op jit(solution)/shard_map/ppermute | solution.py:402
  53.1 18.7 %collective-permute-start.16 = (bf16[4,2,2,4,16,640]{5,4,3,2,1,0:T(8,128)(2,1)}, bf16[4,2,2,4,16,640]{5,4,3,2,1,0:T(8,128)(2,1)}, u32[]{:S(2)}, u32[]{:S(2)}) collective-permute-start(bf16[4,2,2,4,16,640]{5,4,3,2,1,0:T(8,128)(2,1)} %pad_maximum_fusion.1.refs_5_), channel_id=1, source_target_pairs={{32,0},{97,1},{160,128},{225,129},{34,2},{99,3},{162,130},{227,131... | collective-permute-start | bytes 3932168 | tf_op jit(solution)/shard_map/ppermute | solution.py:402
  69.3 4.3 %copy-start.2 = (bf16[4,2,2,4,16,640]{5,4,3,2,1,0:T(8,128)(2,1)}, bf16[4,2,2,4,16,640]{5,4,3,2,1,0:T(8,128)(2,1)S(1)}, u32[]{:S(2)}) copy-start(bf16[4,2,2,4,16,640]{5,4,3,2,1,0:T(8,128)(2,1)S(1)} %collective-permute-done.11.refs_1_) | copy-start | bytes 3932164
  73.2 10.9 %collective-permute-start.21 = (bf16[4,1,2,4,16,640]{5,4,3,2,1,0:T(8,128)(2,1)S(1)}, bf16[4,1,2,4,16,640]{5,4,3,2,1,0:T(8,128)(2,1)S(1)}, u32[]{:S(2)}, u32[]{:S(2)}) collective-permute-start(bf16[4,1,2,4,16,640]{5,4,3,2,1,0:T(8,128)(2,1)S(1)} %slice_select_fusion), channel_id=1, source_target_pairs={{32,0},{97,1},{160,128},{225,129},{34,2},{99,3},{162,130},{227,131... | collective-permute-start | bytes 1966088 | tf_op jit(solution)/shard_map/ppermute | solution.py:402
  73.5 12.6 %collective-permute-start.18 = (bf16[4,1,2,4,16,640]{5,4,3,2,1,0:T(8,128)(2,1)S(1)}, bf16[4,1,2,4,16,640]{5,4,3,2,1,0:T(8,128)(2,1)S(1)}, u32[]{:S(2)}, u32[]{:S(2)}) collective-permute-start(bf16[4,1,2,4,16,640]{5,4,3,2,1,0:T(8,128)(2,1)S(1)} %slice_select_fusion.1), channel_id=1, source_target_pairs={{8,0},{25,1},{136,128},{153,129},{10,2},{27,3},{138,130},{155,131}... | collective-permute-start | bytes 1966088 | tf_op jit(solution)/shard_map/ppermute | solution.py:402
  73.6 16.8 %collective-permute-start.17 = (bf16[4,2,2,4,16,640]{5,4,3,2,1,0:T(8,128)(2,1)S(1)}, bf16[4,2,2,4,16,640]{5,4,3,2,1,0:T(8,128)(2,1)S(1)}, u32[]{:S(2)}, u32[]{:S(2)}) collective-permute-start(bf16[4,2,2,4,16,640]{5,4,3,2,1,0:T(8,128)(2,1)S(1)} %collective-permute-done.11.refs_1_), channel_id=1, source_target_pairs={{1,0},{0,1},{129,128},{128,129},{3,2},{2,3},{131,130},{130,131},{5... | collective-permute-start | bytes 3932168 | tf_op jit(solution)/shard_map/ppermute | solution.py:402
  78.7 11.8 %collective-permute-start.20 = (bf16[4,2,2,4,16,640]{5,4,3,2,1,0:T(8,128)(2,1)}, bf16[4,2,2,4,16,640]{5,4,3,2,1,0:T(8,128)(2,1)S(1)}, u32[]{:S(2)}, u32[]{:S(2)}) collective-permute-start(bf16[4,2,2,4,16,640]{5,4,3,2,1,0:T(8,128)(2,1)} %collective-permute-done.16.refs_6_), channel_id=1, source_target_pairs={{1,0},{0,1},{129,128},{128,129},{3,2},{2,3},{131,130},{130,131},{5... | collective-permute-start | bytes 3932168 | tf_op jit(solution)/shard_map/ppermute | solution.py:402
  84.1 6.4 %copy-start.8 = (bf16[4,1,2,4,16,640]{5,4,3,2,1,0:T(8,128)(2,1)}, bf16[4,1,2,4,16,640]{5,4,3,2,1,0:T(8,128)(2,1)S(1)}, u32[]{:S(2)}) copy-start(bf16[4,1,2,4,16,640]{5,4,3,2,1,0:T(8,128)(2,1)S(1)} %collective-permute-done.21.refs_8_) | copy-start | bytes 1966084
  84.1 5.4 %collective-permute-start.22 = (bf16[4,1,2,4,16,640]{5,4,3,2,1,0:T(8,128)(2,1)S(1)}, bf16[4,1,2,4,16,640]{5,4,3,2,1,0:T(8,128)(2,1)S(1)}, u32[]{:S(2)}, u32[]{:S(2)}) collective-permute-start(bf16[4,1,2,4,16,640]{5,4,3,2,1,0:T(8,128)(2,1)S(1)} %collective-permute-done.21.refs_8_), channel_id=1, source_target_pairs={{1,0},{0,1},{129,128},{128,129},{3,2},{2,3},{131,130},{130,131},{5... | collective-permute-start | bytes 1966088 | tf_op jit(solution)/shard_map/ppermute | solution.py:402
  86.1 4.4 %copy-start.9 = (bf16[4,1,2,4,16,640]{5,4,3,2,1,0:T(8,128)(2,1)}, bf16[4,1,2,4,16,640]{5,4,3,2,1,0:T(8,128)(2,1)S(1)}, u32[]{:S(2)}) copy-start(bf16[4,1,2,4,16,640]{5,4,3,2,1,0:T(8,128)(2,1)S(1)} %collective-permute-done.18.refs_3_) | copy-start | bytes 1966084
  86.1 4.4 %collective-permute-start.19 = (bf16[4,1,2,4,16,640]{5,4,3,2,1,0:T(8,128)(2,1)S(1)}, bf16[4,1,2,4,16,640]{5,4,3,2,1,0:T(8,128)(2,1)S(1)}, u32[]{:S(2)}, u32[]{:S(2)}) collective-permute-start(bf16[4,1,2,4,16,640]{5,4,3,2,1,0:T(8,128)(2,1)S(1)} %collective-permute-done.18.refs_3_), channel_id=1, source_target_pairs={{1,0},{0,1},{129,128},{128,129},{3,2},{2,3},{131,130},{130,131},{5... | collective-permute-start | bytes 1966088 | tf_op jit(solution)/shard_map/ppermute | solution.py:402
  89.4 1.1 copy-start.10
  90.5 0.8 copy-start.11
  90.5 1.3 copy-start.4
  90.5 1.7 copy-start.5
  152.0 2.4 %collective-permute-start.23 = (f32[32,40,128]{2,1,0:T(8,128)}, f32[32,40,128]{2,1,0:T(8,128)S(1)}, u32[]{:S(2)}, u32[]{:S(2)}) collective-permute-start(f32[32,40,128]{2,1,0:T(8,128)} %get-tuple-element.24.ends_ref), channel_id=1, source_target_pairs={{1,0},{0,1},{129,128},{128,129},{3,2},{2,3},{131,130},{130,131},{5... | collective-permute-start | bytes 1966088 | tf_op jit(solution)/shard_map/ppermute | solution.py:402
  154.4 0.9 copy-start.3
  155.2 9.3 %copy-start = (f32[24,64,128]{2,1,0:T(8,128)S(1)}, f32[24,64,128]{2,1,0:T(8,128)}, u32[]{:S(2)}) copy-start(f32[24,64,128]{2,1,0:T(8,128)} %get-tuple-element.25.par_ref) | copy-start | bytes 2359300
  158.2 19.9 %all-to-all-start = ((f32[16,40,128]{2,1,0:T(8,128)}), f32[16,40,128]{2,1,0:T(8,128)S(1)}, u32[]{:S(2)}, u32[]{:S(2)}) async-start(f32[16,40,128]{2,1,0:T(8,128)} %combine.1), calls=%async_computation | async-start | bytes 655360 | tf_op jit(solution)/shard_map/all_to_all | solution.py:451
  178.0 0.7 copy-start.6
  197.2 2.5 %copy-start.7 = (f32[16,32,128]{2,1,0:T(8,128)}, f32[16,32,128]{2,1,0:T(8,128)S(1)}, u32[]{:S(2)}) copy-start(f32[16,32,128]{2,1,0:T(8,128)S(1)} %all_to_all.10.hin_ref) | copy-start | bytes 786436
  197.2 2.5 %collective-permute-start.24 = (f32[16,32,128]{2,1,0:T(8,128)S(1)}, f32[16,32,128]{2,1,0:T(8,128)S(1)}, u32[]{:S(2)}, u32[]{:S(2)}) collective-permute-start(f32[16,32,128]{2,1,0:T(8,128)S(1)} %all_to_all.10.hin_ref), channel_id=1, source_target_pairs={{1,0},{0,1},{129,128},{128,129},{3,2},{2,3},{131,130},{130,131},{5... | collective-permute-start | bytes 786440 | tf_op jit(solution)/shard_map/ppermute | solution.py:402
  199.8 0.7 copy-start.12

commit v8 on v7

--- a/solution.py
+++ b/solution.py
@@ -144,9 +144,9 @@
         def block(i, carry):
             hs, cum = carry
             hs = list(hs)
-            for o in range(16):
-                t = i * 16 + o
-                tile = i * 2 + o // 8
+            for o in range(32):
+                t = i * 32 + o
+                tile = i * 4 + o // 8
                 d = d_scr[tile, pl.ds(o % 8, ROWS, stride=8), :]
                 dx = x_scr[tile, pl.ds(o % 8, ROWS, stride=8), :]
                 cum = cum + d
@@ -162,7 +162,7 @@
             return tuple(hs), cum
 
         zero = jnp.zeros((ROWS, LANES), jnp.float32)
-        hs, cum = lax.fori_loop(0, tok // 16, block, ((zero,) * states, zero))
+        hs, cum = lax.fori_loop(0, tok // 32, block, ((zero,) * states, zero))
         for q in range(ROWS // 2):
             pair = slice(2 * q, 2 * q + 2)
             for n in range(states):
@@ -335,18 +335,18 @@
             h_scr[n] = jnp.exp2(a_scr[n] * e_scr[states]) * h_scr[n] + e_scr[n]
 
     def block(i, carry):
-        for o in range(16):
-            t = i * 16 + o
+        for o in range(32):
+            t = i * 32 + o
             cum = cum_ref[t]
             acc = [y_ref[t]] + [None] * 3
             for n in range(states):
                 c = c_ref[pl.ds(n * tok + t, ROWS, stride=0), :]
                 term = (c * h_scr[n]) * jnp.exp2(a_scr[n] * cum)
                 acc[n % 4] = term if acc[n % 4] is None else acc[n % 4] + term
-            y_scr[i * 2 + o // 8, pl.ds(o % 8, ROWS, stride=8), :] = (acc[0] + acc[1]) + (acc[2] + acc[3])
+            y_scr[i * 4 + o // 8, pl.ds(o % 8, ROWS, stride=8), :] = (acc[0] + acc[1]) + (acc[2] + acc[3])
         return carry
 
-    lax.fori_loop(0, tok // 16, block, 0)
+    lax.fori_loop(0, tok // 32, block, 0)
     for g in range(ROWS):
         cols = slice(g * LANES, (g + 1) * LANES)
         y = y_scr[:, g * 8 : (g + 1) * 8, :].reshape(tok, LANES)

time: 234 us -> 232 us (level)
  no operation moved by 1% of the time
where the time goes in v8:
time: 232 us
  Pallas kernels  104 us (45%)
  starting transfers between devices  49.4 us (21%)
  waiting for transfers between devices  46.1 us (20%)
  blocking collectives  16.8 us (7%)
  local copies, waits for them, and re-layouts  8.71 us (4%)
  other arithmetic  5.19 us (2%)
    pallas_call x1, Pallas kernels, scan_pass(): pl.pallas_call(scan_kernel, grid_spec=pltpu.PrefetchScalarGridSpec(num_sc...  59.3 us
    ppermute x24, starting transfers between devices, fetch(): return lax.ppermute(value, ('group', 'ctx'), route)  38.9 us
    ppermute x24, waiting for transfers between devices, fetch(): return lax.ppermute(value, ('group', 'ctx'), route)  32.3 us
    pallas_call x1, Pallas kernels, gate_pass(): pl.pallas_call(gate_kernel, grid_spec=pltpu.PrefetchScalarGridSpec(num_sc...  31.6 us
    all_to_all x1, blocking collectives, exchange(): lax.all_to_all(value, 'ctx', split_axis=0, concat_axis=0, tiled=True, axi...  16.8 us
    all_to_all x1, waiting for transfers between devices, exchange(): lax.all_to_all(value, 'ctx', split_axis=0, concat_axis=0, tiled=True, axi...  12.8 us
    pallas_call x1, Pallas kernels, gate_factor(): pl.pallas_call(factor_kernel, grid_spec=pltpu.PrefetchScalarGridSpec(num_...  8.81 us
    all_to_all x1, starting transfers between devices, exchange(): lax.all_to_all(value, 'ctx', split_axis=0, concat_axis=0, tiled=True, axi...  6.37 us
  transfers between devices with their start and end apart: 26, of which 14 were waited for; matrix products, arithmetic and copies ran while one was open for 2% of the time, Pallas kernels for 4%

profile of v8, /device:TPU:1, one launch (start us, length us, event | category | flops | bytes accessed | tf_op | source)
XLA Modules:
  0.0 231.6 jit_solution(4038035150307537509)
XLA Ops:
  0.0 0.7 slice.42
  0.7 1.5 concatenate.39
  2.5 0.8 concatenate.40
  3.3 6.9 %collective-permute-start.2 = (bf16[1,32,640]{2,1,0:T(8,128)(2,1)S(1)}, bf16[1,32,640]{2,1,0:T(8,128)(2,1)S(1)}, u32[]{:S(2)}, u32[]{:S(2)}) collective-permute-start(bf16[1,32,640]{2,1,0:T(8,128)(2,1)S(1)} %bitcast.31), channel_id=1, source_target_pairs={{6,0},{7,1},{134,128},{135,129},{4,2},{5,3},{132,130},{133,131},{2... | collective-permute-start | bytes 122888 | tf_op jit(solution)/shard_map/ppermute | solution.py:402
  10.3 1.2 collective-permute-start.1
  11.4 1.0 collective-permute-start
  13.1 1.0 bitcast_select_fusion
  14.1 4.2 %collective-permute-start.3 = (bf16[3,8192]{1,0:T(4,128)(2,1)S(1)}, bf16[3,8192]{1,0:T(4,128)(2,1)S(1)}, u32[]{:S(2)}, u32[]{:S(2)}) collective-permute-start(bf16[3,8192]{1,0:T(4,128)(2,1)S(1)} %bitcast_select_fusion), channel_id=1, source_target_pairs={{0,1},{1,2},{2,3},{3,4},{4,5},{5,6},{6,7},{7,8},{8,9},{9,10},{10,1... | collective-permute-start | bytes 147464 | tf_op jit(solution)/shard_map/ppermute | solution.py:472
  18.6 1.1 collective-permute-done.3
  19.6 1.8 collective-permute-start.4
  22.5 2.7 %collective-permute-done.4 = bf16[4,32,640]{2,1,0:T(8,128)(2,1)S(1)} collective-permute-done((bf16[4,32,640]{2,1,0:T(8,128)(2,1)S(1)}, bf16[4,32,640]{2,1,0:T(8,128)(2,1)S(1)}, u32[]{:S(2)}, u32[]{:S(2)}) %collective-permute-start.4) | collective-permute-done | bytes 163872 | tf_op jit(solution)/shard_map/ppermute | solution.py:402
  25.2 4.2 %collective-permute-done.6 = bf16[4,32,640]{2,1,0:T(8,128)(2,1)S(1)} collective-permute-done((bf16[4,32,640]{2,1,0:T(8,128)(2,1)S(1)}, bf16[4,32,640]{2,1,0:T(8,128)(2,1)S(1)}, u32[]{:S(2)}, u32[]{:S(2)}) %collective-permute-start.6) | collective-permute-done | bytes 163872 | tf_op jit(solution)/shard_map/ppermute | solution.py:402
  29.7 4.1 %collective-permute-start.12 = (bf16[1,2,2,4,16,640]{5,4,3,2,1,0:T(8,128)(2,1)S(1)}, bf16[1,2,2,4,16,640]{5,4,3,2,1,0:T(8,128)(2,1)S(1)}, u32[]{:S(2)}, u32[]{:S(2)}) collective-permute-start(bf16[1,2,2,4,16,640]{5,4,3,2,1,0:T(8,128)(2,1)S(1)} %get-tuple-element.31), channel_id=1, source_target_pairs={{8,0},{25,1},{136,128},{153,129},{10,2},{27,3},{138,130},{155,131}... | collective-permute-start | bytes 983048 | tf_op jit(solution)/shard_map/ppermute | solution.py:402
  33.8 1.3 collective-permute-start.7
  35.1 4.4 %collective-permute-done.12 = bf16[1,2,2,4,16,640]{5,4,3,2,1,0:T(8,128)(2,1)S(1)} collective-permute-done((bf16[1,2,2,4,16,640]{5,4,3,2,1,0:T(8,128)(2,1)S(1)}, bf16[1,2,2,4,16,640]{5,4,3,2,1,0:T(8,128)(2,1)S(1)}, u32[]{:S(2)}, u32[]{:S(2)}) %collective-permute-start.12) | collective-permute-done | bytes 327712 | tf_op jit(solution)/shard_map/ppermute | solution.py:402
  40.1 3.7 %collective-permute-start.13 = (bf16[1,2,2,4,16,640]{5,4,3,2,1,0:T(8,128)(2,1)S(1)}, bf16[1,2,2,4,16,640]{5,4,3,2,1,0:T(8,128)(2,1)S(1)}, u32[]{:S(2)}, u32[]{:S(2)}) collective-permute-start(bf16[1,2,2,4,16,640]{5,4,3,2,1,0:T(8,128)(2,1)S(1)} %collective-permute-done.12), channel_id=1, source_target_pairs={{1,0},{0,1},{129,128},{128,129},{3,2},{2,3},{131,130},{130,131},{5... | collective-permute-start | bytes 983048 | tf_op jit(solution)/shard_map/ppermute | solution.py:402
  43.8 1.4 collective-permute-start.9
  45.2 2.2 collective-permute-start.15
  47.5 1.9 collective-permute-done.9
  49.4 0.9 collective-permute-start.10
  50.4 0.9 collective-permute-done.10
  51.7 1.4 pad_maximum_fusion.1.refs_5_
  53.1 0.8 collective-permute-start.16
  53.8 0.6 pad_add_fusion.info_ref
  54.5 8.8 %gate_factor.1.factor_ref = f32[256,8192]{1,0:T(8,128)} custom-call(s32[4]{0:T(128)} %pad_add_fusion.info_ref, bf16[256,8192]{1,0:T(8,128)(2,1)} %bitcast.29), custom_call_target="tpu_custom_call" | custom-call | tf_op jit(solution)/shard_map/gate_factor/pallas_call | solution.py:297
  63.3 6.0 %collective-permute-done.11.refs_1_ = bf16[4,2,2,4,16,640]{5,4,3,2,1,0:T(8,128)(2,1)S(1)} collective-permute-done((bf16[4,2,2,4,16,640]{5,4,3,2,1,0:T(8,128)(2,1)S(1)}, bf16[4,2,2,4,16,640]{5,4,3,2,1,0:T(8,128)(2,1)S(1)}, u32[]{:S(2)}, u32[]{:S(2)}) %collective-permute-start.11) | collective-permute-done | bytes 1310752 | tf_op jit(solution)/shard_map/ppermute | solution.py:402
  69.3 2.5 %collective-permute-done.16.refs_6_ = bf16[4,2,2,4,16,640]{5,4,3,2,1,0:T(8,128)(2,1)} collective-permute-done((bf16[4,2,2,4,16,640]{5,4,3,2,1,0:T(8,128)(2,1)}, bf16[4,2,2,4,16,640]{5,4,3,2,1,0:T(8,128)(2,1)}, u32[]{:S(2)}, u32[]{:S(2)}) %collective-permute-start.16) | collective-permute-done | bytes 1310752 | tf_op jit(solution)/shard_map/ppermute | solution.py:402
  71.8 1.4 slice_select_fusion
  73.6 5.1 %collective-permute-start.17 = (bf16[4,2,2,4,16,640]{5,4,3,2,1,0:T(8,128)(2,1)S(1)}, bf16[4,2,2,4,16,640]{5,4,3,2,1,0:T(8,128)(2,1)S(1)}, u32[]{:S(2)}, u32[]{:S(2)}) collective-permute-start(bf16[4,2,2,4,16,640]{5,4,3,2,1,0:T(8,128)(2,1)S(1)} %collective-permute-done.11.refs_1_), channel_id=1, source_target_pairs={{1,0},{0,1},{129,128},{128,129},{3,2},{2,3},{131,130},{130,131},{5... | collective-permute-start | bytes 3932168 | tf_op jit(solution)/shard_map/ppermute | solution.py:402
  78.7 5.4 %collective-permute-done.21.refs_8_ = bf16[4,1,2,4,16,640]{5,4,3,2,1,0:T(8,128)(2,1)S(1)} collective-permute-done((bf16[4,1,2,4,16,640]{5,4,3,2,1,0:T(8,128)(2,1)S(1)}, bf16[4,1,2,4,16,640]{5,4,3,2,1,0:T(8,128)(2,1)S(1)}, u32[]{:S(2)}, u32[]{:S(2)}) %collective-permute-start.21) | collective-permute-done | bytes 655392 | tf_op jit(solution)/shard_map/ppermute | solution.py:402
  84.1 2.0 collective-permute-start.22
  86.1 2.6 %collective-permute-start.19 = (bf16[4,1,2,4,16,640]{5,4,3,2,1,0:T(8,128)(2,1)S(1)}, bf16[4,1,2,4,16,640]{5,4,3,2,1,0:T(8,128)(2,1)S(1)}, u32[]{:S(2)}, u32[]{:S(2)}) collective-permute-start(bf16[4,1,2,4,16,640]{5,4,3,2,1,0:T(8,128)(2,1)S(1)} %collective-permute-done.18.refs_3_), channel_id=1, source_target_pairs={{1,0},{0,1},{129,128},{128,129},{3,2},{2,3},{131,130},{130,131},{5... | collective-permute-start | bytes 1966088 | tf_op jit(solution)/shard_map/ppermute | solution.py:402
  88.7 0.7 concatenate.51.rim_ref
  89.4 1.0 collective-permute-done.19.refs_4_
  90.5 0.8 copy-done.11
  92.2 59.3 %scan_pass.1 = (bf16[256,8192]{1,0:T(8,128)(2,1)}, f32[24,64,128]{2,1,0:T(8,128)}, f32[256,64,128]{2,1,0:T(8,128)}, f32[256,64,128]{2,1,0:T(8,128)}, f32[32,40,128]{2,1,0:T(8,128)}, /*index=5*/f32[4096,128]{1,0:T(8,128)}) custom-call(s32[4]{0:T(128)} %pad_add_fusion.info_ref, bf16[256,8192]{1,0:T(8,128)(2,1)} %bitcast.28, ...), custom_call_target="tpu_custom_call" | custom-call | tf_op jit(solution)/shard_map/scan_pass/pallas_call | solution.py:189
  151.9 1.9 collective-permute-done.23.other_ref
  153.9 0.9 copy-done.3
  154.7 2.9 %combine.1 = f32[16,40,128]{2,1,0:T(8,128)} custom-call(s32[4]{0:T(128)} %pad_add_fusion.info_ref, f32[32,40,128]{2,1,0:T(8,128)} %get-tuple-element.24.ends_ref, f32[32,40,128]{2,1,0:T(8,128)} %copy-done.3, f32[24,64,128]{2,1,0:T(8,128)} %get-tuple-element.25.par_ref), custom_call_target="tpu_custom_call" | custom-call | tf_op jit(solution)/shard_map/combine/pallas_call | solution.py:253
  157.6 6.4 %all-to-all-start = ((f32[16,40,128]{2,1,0:T(8,128)}), f32[16,40,128]{2,1,0:T(8,128)S(1)}, u32[]{:S(2)}, u32[]{:S(2)}) async-start(f32[16,40,128]{2,1,0:T(8,128)} %combine.1), calls=%async_computation | async-start | bytes 655360 | tf_op jit(solution)/shard_map/all_to_all | solution.py:451
  164.7 12.8 %all-to-all-done.end_ref = f32[16,40,128]{2,1,0:T(8,128)S(1)} async-done(((f32[16,40,128]{2,1,0:T(8,128)}), f32[16,40,128]{2,1,0:T(8,128)S(1)}, u32[]{:S(2)}, u32[]{:S(2)}) %all-to-all-start) | async-done | bytes 327712 | tf_op jit(solution)/shard_map/all_to_all | solution.py:451
  177.5 0.7 copy-done.6
  178.2 1.7 prefix.1
  180.0 16.8 %all_to_all.10.hin_ref = f32[16,32,128]{2,1,0:T(8,128)S(1)} all-to-all(f32[16,32,128]{2,1,0:T(8,128)} %prefix.1), channel_id=1, replica_groups={{0,2,4,6,8,10,12,14,16,18,20,22,24,26,28,30},{1,3,5,7,9,11,13,15,17,19,..., dimensions={0} | all-to-all | bytes 524288 | tf_op jit(solution)/shard_map/all_to_all | solution.py:451
  196.7 1.4 collective-permute-start.24
  198.1 1.2 collective-permute-done.24.hin_too_ref
  199.3 0.7 copy-done.12
  199.9 31.6 %gate_pass.1 = bf16[256,8192]{1,0:T(8,128)(2,1)} custom-call(s32[4]{0:T(128)} %pad_add_fusion.info_ref, f32[256,64,128]{2,1,0:T(8,128)} %get-tuple-element.22.y_ref, f32[256,64,128]{2,1,0:T(8,128)} %get-tuple-element.23.cum_ref, f32[16,32,128]{2,1,0:T(8,128)} %copy-done.7, f32[16,32,128]{2,1,0:T(8,128)} %copy-done.12, f32[32,40,128]{2,1,0:T(8,128)} %copy-done.3, ...), custom_call_target="tpu_custom_call" | custom-call | tf_op jit(solution)/shard_map/gate_pass/pallas_call | solution.py:361
  (68 shorter events, 5.4 us)
Async XLA Ops:
  3.3 15.1 %collective-permute-start.2 = (bf16[1,32,640]{2,1,0:T(8,128)(2,1)S(1)}, bf16[1,32,640]{2,1,0:T(8,128)(2,1)S(1)}, u32[]{:S(2)}, u32[]{:S(2)}) collective-permute-start(bf16[1,32,640]{2,1,0:T(8,128)(2,1)S(1)} %bitcast.31), channel_id=1, source_target_pairs={{6,0},{7,1},{134,128},{135,129},{4,2},{5,3},{132,130},{133,131},{2... | collective-permute-start | bytes 122888 | tf_op jit(solution)/shard_map/ppermute | solution.py:402
  10.3 8.2 %collective-permute-start.1 = (bf16[1,32,640]{2,1,0:T(8,128)(2,1)S(1)}, bf16[1,32,640]{2,1,0:T(8,128)(2,1)S(1)}, u32[]{:S(2)}, u32[]{:S(2)}) collective-permute-start(bf16[1,32,640]{2,1,0:T(8,128)(2,1)S(1)} %bitcast.32), channel_id=1, source_target_pairs={{2,0},{3,1},{130,128},{131,129},{0,2},{1,3},{128,130},{129,131},{6... | collective-permute-start | bytes 122888 | tf_op jit(solution)/shard_map/ppermute | solution.py:402
  11.4 7.0 %collective-permute-start = (bf16[1,32,640]{2,1,0:T(8,128)(2,1)S(1)}, bf16[1,32,640]{2,1,0:T(8,128)(2,1)S(1)}, u32[]{:S(2)}, u32[]{:S(2)}) collective-permute-start(bf16[1,32,640]{2,1,0:T(8,128)(2,1)S(1)} %bitcast.33), channel_id=1, source_target_pairs={{4,0},{5,1},{132,128},{133,129},{6,2},{7,3},{134,130},{135,131},{0... | collective-permute-start | bytes 122888 | tf_op jit(solution)/shard_map/ppermute | solution.py:402
  14.1 5.5 %collective-permute-start.3 = (bf16[3,8192]{1,0:T(4,128)(2,1)S(1)}, bf16[3,8192]{1,0:T(4,128)(2,1)S(1)}, u32[]{:S(2)}, u32[]{:S(2)}) collective-permute-start(bf16[3,8192]{1,0:T(4,128)(2,1)S(1)} %bitcast_select_fusion), channel_id=1, source_target_pairs={{0,1},{1,2},{2,3},{3,4},{4,5},{5,6},{6,7},{7,8},{8,9},{9,10},{10,1... | collective-permute-start | bytes 147464 | tf_op jit(solution)/shard_map/ppermute | solution.py:472
  19.6 5.5 %collective-permute-start.4 = (bf16[4,32,640]{2,1,0:T(8,128)(2,1)S(1)}, bf16[4,32,640]{2,1,0:T(8,128)(2,1)S(1)}, u32[]{:S(2)}, u32[]{:S(2)}) collective-permute-start(bf16[4,32,640]{2,1,0:T(8,128)(2,1)S(1)} %pad_maximum_fusion.5), channel_id=1, source_target_pairs={{128,0},{129,1},{0,128},{1,129},{130,2},{131,3},{2,130},{3,131},{1... | collective-permute-start | bytes 491528 | tf_op jit(solution)/shard_map/ppermute | solution.py:402
  21.4 3.8 %collective-permute-start.5 = (bf16[4,32,640]{2,1,0:T(8,128)(2,1)S(1)}, bf16[4,32,640]{2,1,0:T(8,128)(2,1)S(1)}, u32[]{:S(2)}, u32[]{:S(2)}) collective-permute-start(bf16[4,32,640]{2,1,0:T(8,128)(2,1)S(1)} %pad_maximum_fusion.5), channel_id=1, source_target_pairs={{1,0},{0,1},{129,128},{128,129},{3,2},{2,3},{131,130},{130,131},{5... | collective-permute-start | bytes 491528 | tf_op jit(solution)/shard_map/ppermute | solution.py:402
  21.8 7.5 %collective-permute-start.6 = (bf16[4,32,640]{2,1,0:T(8,128)(2,1)S(1)}, bf16[4,32,640]{2,1,0:T(8,128)(2,1)S(1)}, u32[]{:S(2)}, u32[]{:S(2)}) collective-permute-start(bf16[4,32,640]{2,1,0:T(8,128)(2,1)S(1)} %pad_maximum_fusion.5), channel_id=1, source_target_pairs={{129,0},{128,1},{1,128},{0,129},{131,2},{130,3},{3,130},{2,131},{1... | collective-permute-start | bytes 491528 | tf_op jit(solution)/shard_map/ppermute | solution.py:402
  29.7 9.8 %collective-permute-start.12 = (bf16[1,2,2,4,16,640]{5,4,3,2,1,0:T(8,128)(2,1)S(1)}, bf16[1,2,2,4,16,640]{5,4,3,2,1,0:T(8,128)(2,1)S(1)}, u32[]{:S(2)}, u32[]{:S(2)}) collective-permute-start(bf16[1,2,2,4,16,640]{5,4,3,2,1,0:T(8,128)(2,1)S(1)} %get-tuple-element.31), channel_id=1, source_target_pairs={{8,0},{25,1},{136,128},{153,129},{10,2},{27,3},{138,130},{155,131}... | collective-permute-start | bytes 983048 | tf_op jit(solution)/shard_map/ppermute | solution.py:402
  33.8 10.0 %collective-permute-start.7 = (bf16[1,2,2,4,16,640]{5,4,3,2,1,0:T(8,128)(2,1)S(1)}, bf16[1,2,2,4,16,640]{5,4,3,2,1,0:T(8,128)(2,1)S(1)}, u32[]{:S(2)}, u32[]{:S(2)}) collective-permute-start(bf16[1,2,2,4,16,640]{5,4,3,2,1,0:T(8,128)(2,1)S(1)} %get-tuple-element.32), channel_id=1, source_target_pairs={{32,0},{97,1},{160,128},{225,129},{34,2},{99,3},{162,130},{227,131... | collective-permute-start | bytes 983048 | tf_op jit(solution)/shard_map/ppermute | solution.py:402
  39.5 5.7 %collective-permute-start.14 = (bf16[1,1,2,4,16,640]{5,4,3,2,1,0:T(8,128)(2,1)S(1)}, bf16[1,1,2,4,16,640]{5,4,3,2,1,0:T(8,128)(2,1)S(1)}, u32[]{:S(2)}, u32[]{:S(2)}) collective-permute-start(bf16[1,1,2,4,16,640]{5,4,3,2,1,0:T(8,128)(2,1)S(1)} %slice_select_fusion.2), channel_id=1, source_target_pairs={{8,0},{25,1},{136,128},{153,129},{10,2},{27,3},{138,130},{155,131}... | collective-permute-start | bytes 491528 | tf_op jit(solution)/shard_map/ppermute | solution.py:402
  40.1 10.2 %collective-permute-start.13 = (bf16[1,2,2,4,16,640]{5,4,3,2,1,0:T(8,128)(2,1)S(1)}, bf16[1,2,2,4,16,640]{5,4,3,2,1,0:T(8,128)(2,1)S(1)}, u32[]{:S(2)}, u32[]{:S(2)}) collective-permute-start(bf16[1,2,2,4,16,640]{5,4,3,2,1,0:T(8,128)(2,1)S(1)} %collective-permute-done.12), channel_id=1, source_target_pairs={{1,0},{0,1},{129,128},{128,129},{3,2},{2,3},{131,130},{130,131},{5... | collective-permute-start | bytes 983048 | tf_op jit(solution)/shard_map/ppermute | solution.py:402
  43.8 6.5 %collective-permute-start.8 = (bf16[1,2,2,4,16,640]{5,4,3,2,1,0:T(8,128)(2,1)S(1)}, bf16[1,2,2,4,16,640]{5,4,3,2,1,0:T(8,128)(2,1)S(1)}, u32[]{:S(2)}, u32[]{:S(2)}) collective-permute-start(bf16[1,2,2,4,16,640]{5,4,3,2,1,0:T(8,128)(2,1)S(1)} %collective-permute-done.7), channel_id=1, source_target_pairs={{1,0},{0,1},{129,128},{128,129},{3,2},{2,3},{131,130},{130,131},{5... | collective-permute-start | bytes 983048 | tf_op jit(solution)/shard_map/ppermute | solution.py:402
  43.8 5.5 %collective-permute-start.9 = (bf16[1,1,2,4,16,640]{5,4,3,2,1,0:T(8,128)(2,1)S(1)}, bf16[1,1,2,4,16,640]{5,4,3,2,1,0:T(8,128)(2,1)S(1)}, u32[]{:S(2)}, u32[]{:S(2)}) collective-permute-start(bf16[1,1,2,4,16,640]{5,4,3,2,1,0:T(8,128)(2,1)S(1)} %slice_select_fusion.3), channel_id=1, source_target_pairs={{32,0},{97,1},{160,128},{225,129},{34,2},{99,3},{162,130},{227,131... | collective-permute-start | bytes 491528 | tf_op jit(solution)/shard_map/ppermute | solution.py:402
  45.2 6.4 %collective-permute-start.15 = (bf16[1,1,2,4,16,640]{5,4,3,2,1,0:T(8,128)(2,1)S(1)}, bf16[1,1,2,4,16,640]{5,4,3,2,1,0:T(8,128)(2,1)S(1)}, u32[]{:S(2)}, u32[]{:S(2)}) collective-permute-start(bf16[1,1,2,4,16,640]{5,4,3,2,1,0:T(8,128)(2,1)S(1)} %collective-permute-done.14), channel_id=1, source_target_pairs={{1,0},{0,1},{129,128},{128,129},{3,2},{2,3},{131,130},{130,131},{5... | collective-permute-start | bytes 491528 | tf_op jit(solution)/shard_map/ppermute | solution.py:402
  49.4 1.9 collective-permute-start.10
  51.6 1.5 copy-start.1
  51.6 17.7 %collective-permute-start.11 = (bf16[4,2,2,4,16,640]{5,4,3,2,1,0:T(8,128)(2,1)S(1)}, bf16[4,2,2,4,16,640]{5,4,3,2,1,0:T(8,128)(2,1)S(1)}, u32[]{:S(2)}, u32[]{:S(2)}) collective-permute-start(bf16[4,2,2,4,16,640]{5,4,3,2,1,0:T(8,128)(2,1)S(1)} %pad_maximum_fusion.refs_0_), channel_id=1, source_target_pairs={{8,0},{25,1},{136,128},{153,129},{10,2},{27,3},{138,130},{155,131}... | collective-permute-start | bytes 3932168 | tf_op jit(solution)/shard_map/ppermute | solution.py:402
  53.1 18.7 %collective-permute-start.16 = (bf16[4,2,2,4,16,640]{5,4,3,2,1,0:T(8,128)(2,1)}, bf16[4,2,2,4,16,640]{5,4,3,2,1,0:T(8,128)(2,1)}, u32[]{:S(2)}, u32[]{:S(2)}) collective-permute-start(bf16[4,2,2,4,16,640]{5,4,3,2,1,0:T(8,128)(2,1)} %pad_maximum_fusion.1.refs_5_), channel_id=1, source_target_pairs={{32,0},{97,1},{160,128},{225,129},{34,2},{99,3},{162,130},{227,131... | collective-permute-start | bytes 3932168 | tf_op jit(solution)/shard_map/ppermute | solution.py:402
  69.3 4.3 %copy-start.2 = (bf16[4,2,2,4,16,640]{5,4,3,2,1,0:T(8,128)(2,1)}, bf16[4,2,2,4,16,640]{5,4,3,2,1,0:T(8,128)(2,1)S(1)}, u32[]{:S(2)}) copy-start(bf16[4,2,2,4,16,640]{5,4,3,2,1,0:T(8,128)(2,1)S(1)} %collective-permute-done.11.refs_1_) | copy-start | bytes 3932164
  73.2 10.9 %collective-permute-start.21 = (bf16[4,1,2,4,16,640]{5,4,3,2,1,0:T(8,128)(2,1)S(1)}, bf16[4,1,2,4,16,640]{5,4,3,2,1,0:T(8,128)(2,1)S(1)}, u32[]{:S(2)}, u32[]{:S(2)}) collective-permute-start(bf16[4,1,2,4,16,640]{5,4,3,2,1,0:T(8,128)(2,1)S(1)} %slice_select_fusion), channel_id=1, source_target_pairs={{32,0},{97,1},{160,128},{225,129},{34,2},{99,3},{162,130},{227,131... | collective-permute-start | bytes 1966088 | tf_op jit(solution)/shard_map/ppermute | solution.py:402
  73.5 12.6 %collective-permute-start.18 = (bf16[4,1,2,4,16,640]{5,4,3,2,1,0:T(8,128)(2,1)S(1)}, bf16[4,1,2,4,16,640]{5,4,3,2,1,0:T(8,128)(2,1)S(1)}, u32[]{:S(2)}, u32[]{:S(2)}) collective-permute-start(bf16[4,1,2,4,16,640]{5,4,3,2,1,0:T(8,128)(2,1)S(1)} %slice_select_fusion.1), channel_id=1, source_target_pairs={{8,0},{25,1},{136,128},{153,129},{10,2},{27,3},{138,130},{155,131}... | collective-permute-start | bytes 1966088 | tf_op jit(solution)/shard_map/ppermute | solution.py:402
  73.6 16.8 %collective-permute-start.17 = (bf16[4,2,2,4,16,640]{5,4,3,2,1,0:T(8,128)(2,1)S(1)}, bf16[4,2,2,4,16,640]{5,4,3,2,1,0:T(8,128)(2,1)S(1)}, u32[]{:S(2)}, u32[]{:S(2)}) collective-permute-start(bf16[4,2,2,4,16,640]{5,4,3,2,1,0:T(8,128)(2,1)S(1)} %collective-permute-done.11.refs_1_), channel_id=1, source_target_pairs={{1,0},{0,1},{129,128},{128,129},{3,2},{2,3},{131,130},{130,131},{5... | collective-permute-start | bytes 3932168 | tf_op jit(solution)/shard_map/ppermute | solution.py:402
  78.7 11.8 %collective-permute-start.20 = (bf16[4,2,2,4,16,640]{5,4,3,2,1,0:T(8,128)(2,1)}, bf16[4,2,2,4,16,640]{5,4,3,2,1,0:T(8,128)(2,1)S(1)}, u32[]{:S(2)}, u32[]{:S(2)}) collective-permute-start(bf16[4,2,2,4,16,640]{5,4,3,2,1,0:T(8,128)(2,1)} %collective-permute-done.16.refs_6_), channel_id=1, source_target_pairs={{1,0},{0,1},{129,128},{128,129},{3,2},{2,3},{131,130},{130,131},{5... | collective-permute-start | bytes 3932168 | tf_op jit(solution)/shard_map/ppermute | solution.py:402
  84.1 6.4 %copy-start.8 = (bf16[4,1,2,4,16,640]{5,4,3,2,1,0:T(8,128)(2,1)}, bf16[4,1,2,4,16,640]{5,4,3,2,1,0:T(8,128)(2,1)S(1)}, u32[]{:S(2)}) copy-start(bf16[4,1,2,4,16,640]{5,4,3,2,1,0:T(8,128)(2,1)S(1)} %collective-permute-done.21.refs_8_) | copy-start | bytes 1966084
  84.1 5.4 %collective-permute-start.22 = (bf16[4,1,2,4,16,640]{5,4,3,2,1,0:T(8,128)(2,1)S(1)}, bf16[4,1,2,4,16,640]{5,4,3,2,1,0:T(8,128)(2,1)S(1)}, u32[]{:S(2)}, u32[]{:S(2)}) collective-permute-start(bf16[4,1,2,4,16,640]{5,4,3,2,1,0:T(8,128)(2,1)S(1)} %collective-permute-done.21.refs_8_), channel_id=1, source_target_pairs={{1,0},{0,1},{129,128},{128,129},{3,2},{2,3},{131,130},{130,131},{5... | collective-permute-start | bytes 1966088 | tf_op jit(solution)/shard_map/ppermute | solution.py:402
  86.1 4.4 %copy-start.9 = (bf16[4,1,2,4,16,640]{5,4,3,2,1,0:T(8,128)(2,1)}, bf16[4,1,2,4,16,640]{5,4,3,2,1,0:T(8,128)(2,1)S(1)}, u32[]{:S(2)}) copy-start(bf16[4,1,2,4,16,640]{5,4,3,2,1,0:T(8,128)(2,1)S(1)} %collective-permute-done.18.refs_3_) | copy-start | bytes 1966084
  86.1 4.4 %collective-permute-start.19 = (bf16[4,1,2,4,16,640]{5,4,3,2,1,0:T(8,128)(2,1)S(1)}, bf16[4,1,2,4,16,640]{5,4,3,2,1,0:T(8,128)(2,1)S(1)}, u32[]{:S(2)}, u32[]{:S(2)}) collective-permute-start(bf16[4,1,2,4,16,640]{5,4,3,2,1,0:T(8,128)(2,1)S(1)} %collective-permute-done.18.refs_3_), channel_id=1, source_target_pairs={{1,0},{0,1},{129,128},{128,129},{3,2},{2,3},{131,130},{130,131},{5... | collective-permute-start | bytes 1966088 | tf_op jit(solution)/shard_map/ppermute | solution.py:402
  89.4 1.1 copy-start.10
  90.5 0.8 copy-start.11
  90.5 1.3 copy-start.4
  90.5 1.7 copy-start.5
  151.5 2.4 %collective-permute-start.23 = (f32[32,40,128]{2,1,0:T(8,128)}, f32[32,40,128]{2,1,0:T(8,128)S(1)}, u32[]{:S(2)}, u32[]{:S(2)}) collective-permute-start(f32[32,40,128]{2,1,0:T(8,128)} %get-tuple-element.24.ends_ref), channel_id=1, source_target_pairs={{1,0},{0,1},{129,128},{128,129},{3,2},{2,3},{131,130},{130,131},{5... | collective-permute-start | bytes 1966088 | tf_op jit(solution)/shard_map/ppermute | solution.py:402
  153.9 0.9 copy-start.3
  154.7 9.3 %copy-start = (f32[24,64,128]{2,1,0:T(8,128)S(1)}, f32[24,64,128]{2,1,0:T(8,128)}, u32[]{:S(2)}) copy-start(f32[24,64,128]{2,1,0:T(8,128)} %get-tuple-element.25.par_ref) | copy-start | bytes 2359300
  157.6 19.9 %all-to-all-start = ((f32[16,40,128]{2,1,0:T(8,128)}), f32[16,40,128]{2,1,0:T(8,128)S(1)}, u32[]{:S(2)}, u32[]{:S(2)}) async-start(f32[16,40,128]{2,1,0:T(8,128)} %combine.1), calls=%async_computation | async-start | bytes 655360 | tf_op jit(solution)/shard_map/all_to_all | solution.py:451
  177.5 0.7 copy-start.6
  196.7 2.5 %copy-start.7 = (f32[16,32,128]{2,1,0:T(8,128)}, f32[16,32,128]{2,1,0:T(8,128)S(1)}, u32[]{:S(2)}) copy-start(f32[16,32,128]{2,1,0:T(8,128)S(1)} %all_to_all.10.hin_ref) | copy-start | bytes 786436
  196.7 2.5 %collective-permute-start.24 = (f32[16,32,128]{2,1,0:T(8,128)S(1)}, f32[16,32,128]{2,1,0:T(8,128)S(1)}, u32[]{:S(2)}, u32[]{:S(2)}) collective-permute-start(f32[16,32,128]{2,1,0:T(8,128)S(1)} %all_to_all.10.hin_ref), channel_id=1, source_target_pairs={{1,0},{0,1},{129,128},{128,129},{3,2},{2,3},{131,130},{130,131},{5... | collective-permute-start | bytes 786440 | tf_op jit(solution)/shard_map/ppermute | solution.py:402
  199.3 0.7 copy-start.12
